TPU v7x, 128 devices: a whole 4x4x4 slice. The times are simulated.
128 devices in a mesh: row: 16 (over z_hi, y, core), col: 8 (over x, z_lo).
Axes of the slice: x: 4, y: 4, z: 4 (z_hi: 2, z_lo: 2; z = z_hi * 2 + z_lo), core: 2. Of those that a mesh axis runs over, the one named last changes fastest.
Arguments:
- context: bfloat16 [256, 512, 384], P('row', 'col'), may hold values from -6 to 6
- first_dilated_weight: bfloat16 [3, 3, 384, 384], replicated, may hold values from -0.109375 to 0.109375
- first_plain_weight: bfloat16 [3, 3, 384, 384], replicated, may hold values from -0.109375 to 0.109375
- second_dilated_weight: bfloat16 [3, 3, 384, 384], replicated, may hold values from -0.109375 to 0.109375
- second_plain_weight: bfloat16 [3, 3, 384, 384], replicated, may hold values from -0.109375 to 0.109375
- lift_weight: bfloat16 [384, 1536], replicated, may hold values from -0.3125 to 0.3125
- fine_weight: bfloat16 [3, 3, 96, 96], replicated, may hold values from -0.21875 to 0.21875
Outputs:
- context_out: bfloat16 [256, 512, 384], P('row', 'col')
- target: bfloat16 [256, 512, 96], P('row', 'col')
All inputs are finite; a program needn't handle non-finite values.
Results may differ from a plain program's by a relative error of at most 0.015.
Values may be sent and summed in bfloat16 or wider, within the bound.
No kernel may reach another device: no remote copies, remote signals or barrier semaphores. Data moves between devices by JAX's collectives and lax.ppermute only.
A program may use at most 64 MiB of HBM per device.

v0:
```python
import jax
import jax.numpy as jnp
from jax import lax
from jax.sharding import PartitionSpec as P

FIRST_DILATION = 32
SECOND_DILATION = 64


def with_halo(block, sides, width):
    for axis, dim in sides:
        count = lax.axis_size(axis)
        forward = [(i, i + 1) for i in range(count - 1)]
        backward = [(target, source) for source, target in forward]
        low = lax.ppermute(
            lax.slice_in_dim(block, block.shape[dim] - width, None, axis=dim), axis, forward
        )
        high = lax.ppermute(lax.slice_in_dim(block, 0, width, axis=dim), axis, backward)
        block = jnp.concatenate([low, block, high], axis=dim)
    return block


def shifted(block, axis, distance):
    devices = range(lax.axis_size(axis))
    route = [(i - distance, i) for i in devices if i - distance in devices]
    return lax.ppermute(block, axis, route)


def tap_line(source, kernel, tap_row, tap_spacing, breadth):
    summed = None
    for tap_col in range(3):
        window = source[:, tap_col * tap_spacing : tap_col * tap_spacing + breadth, :]
        product = jnp.einsum(
            "rcf,fg->rcg", window, kernel[tap_row, tap_col], preferred_element_type=jnp.float32
        )
        summed = product if summed is None else summed + product
    return summed


def dilated_output(running_state, kernel, tap_spacing):
    height, breadth = (running_state.shape[0], running_state.shape[1])
    device_hops = tap_spacing // height
    widened = with_halo(running_state, (("col", 1),), tap_spacing)
    shifted_down = shifted(widened, "row", device_hops)
    shifted_up = shifted(widened, "row", -device_hops)
    result = (
        tap_line(shifted_down, kernel, 0, tap_spacing, breadth)
        + tap_line(widened, kernel, 1, tap_spacing, breadth)
        + tap_line(shifted_up, kernel, 2, tap_spacing, breadth)
    )
    return result


def plain_sum(padded, kernel, height, breadth):
    summed = None
    for tap_row in range(3):
        for tap_col in range(3):
            window = padded[tap_row : tap_row + height, tap_col : tap_col + breadth, :]
            product = jnp.einsum(
                "rcf,fg->rcg", window, kernel[tap_row, tap_col], preferred_element_type=jnp.float32
            )
            summed = product if summed is None else summed + product
    return summed


def crop_pick(count, piece_rows, offset, position, length):
    target_slot = lax.broadcasted_iota(jnp.int32, (count * piece_rows, length), 0)
    source_slot = lax.broadcasted_iota(jnp.int32, (count * piece_rows, length), 1)
    return (offset + target_slot == position * length + source_slot).astype(jnp.bfloat16)


def shards(
    context,
    first_dilated_weight,
    first_plain_weight,
    second_dilated_weight,
    second_plain_weight,
    lift_weight,
    fine_weight,
):
    height, breadth, channels = (context.shape[0], context.shape[1], context.shape[2])
    running_state = context
    for dilated_kernel, kernel_border, tap_spacing in (
        (first_dilated_weight, first_plain_weight, FIRST_DILATION),
        (second_dilated_weight, second_plain_weight, SECOND_DILATION),
    ):
        hidden_state = jax.nn.silu(
            dilated_output(running_state, dilated_kernel, tap_spacing)
        ).astype(jnp.bfloat16)
        padded = with_halo(hidden_state, (("row", 0), ("col", 1)), 1)
        running_state = (
            running_state.astype(jnp.float32) + plain_sum(padded, kernel_border, height, breadth)
        ).astype(jnp.bfloat16)
    row_count, col_count = (lax.axis_size("row"), lax.axis_size("col"))
    row_piece, col_piece = (height // 4, breadth // 4)
    row_pick = crop_pick(
        row_count, row_piece, height * row_count // 2, lax.axis_index("row"), height
    )
    col_pick = crop_pick(
        col_count, col_piece, breadth * col_count // 2, lax.axis_index("col"), breadth
    )
    outgoing = jnp.einsum(
        "ml,lcf->mcf", row_pick, running_state, preferred_element_type=jnp.float32
    ).astype(jnp.bfloat16)
    landed = lax.all_to_all(outgoing, "row", split_axis=0, concat_axis=0, tiled=True)
    row_strip = (
        landed.astype(jnp.float32)
        .reshape(row_count, row_piece, breadth, channels)
        .sum(0)
        .astype(jnp.bfloat16)
    )
    outgoing = jnp.einsum(
        "nm,rmf->rnf", col_pick, row_strip, preferred_element_type=jnp.float32
    ).astype(jnp.bfloat16)
    landed = lax.all_to_all(outgoing, "col", split_axis=1, concat_axis=1, tiled=True)
    crop_cells = (
        landed.astype(jnp.float32)
        .reshape(row_piece, col_count, col_piece, channels)
        .sum(1)
        .astype(jnp.bfloat16)
    )
    lifted = jnp.einsum(
        "rcf,fg->rcg", crop_cells, lift_weight, preferred_element_type=jnp.float32
    ).astype(jnp.bfloat16)
    fine_width = lifted.shape[2] // 16
    lifted = (
        lifted.reshape(row_piece, col_piece, 4, 4, fine_width)
        .transpose(0, 2, 1, 3, 4)
        .reshape(height, breadth, fine_width)
    )
    padded = with_halo(lifted, (("row", 0), ("col", 1)), 1)
    target = plain_sum(padded, fine_weight, height, breadth).astype(jnp.bfloat16)
    return (running_state, target)


def solution(mesh):
    return jax.shard_map(
        shards,
        mesh=mesh,
        in_specs=(P("row", "col", None), P(), P(), P(), P(), P(), P()),
        out_specs=(P("row", "col", None), P("row", "col", None)),
        check_vma=False,
    )
```

profile of v0, /device:TPU:0, one launch (start us, length us, event | category | flops | bytes accessed | tf_op | source)
XLA Modules:
  0.0 362.5 jit_solution(2243694041366908419)
XLA Ops:
  0.7 1.3 fusion.220
  2.0 4.0 %collective-permute-start = (bf16[16,32,384]{2,1,0:T(8,128)(2,1)S(1)}, bf16[16,32,384]{2,1,0:T(8,128)(2,1)S(1)}, u32[]{:S(2)}, u32[]{:S(2)}) collective-permute-start(bf16[16,32,384]{2,1,0:T(8,128)(2,1)S(1)} %get-tuple-element.15), channel_id=1, source_target_pairs={{0,1},{1,2},{2,3},{3,4},{4,5},{5,6},{6,7},{8,9},{9,10},{10,11},{11... | collective-permute-start | bytes 1179656 | tf_op jit(solution)/shard_map/ppermute | solution.py:15
  6.0 1.6 collective-permute-start.1
  7.5 15.2 %collective-permute-done = bf16[16,32,384]{2,1,0:T(8,128)(2,1)S(1)} collective-permute-done((bf16[16,32,384]{2,1,0:T(8,128)(2,1)S(1)}, bf16[16,32,384]{2,1,0:T(8,128)(2,1)S(1)}, u32[]{:S(2)}, u32[]{:S(2)}) %collective-permute-start) | collective-permute-done | bytes 393248 | tf_op jit(solution)/shard_map/ppermute | solution.py:15
  23.1 1.3 collective-permute-start.3
  24.4 4.6 %collective-permute-start.2 = (bf16[16,128,384]{2,1,0:T(8,128)(2,1)S(1)}, bf16[16,128,384]{2,1,0:T(8,128)(2,1)S(1)}, u32[]{:S(2)}, u32[]{:S(2)}) collective-permute-start(bf16[16,128,384]{2,1,0:T(8,128)(2,1)S(1)} %constant_dynamic-update-slice_fusion), channel_id=1, source_target_pairs={{0,16},{8,24},{16,32},{24,40},{32,48},{40,56},{48,64},{56,72},{64,... | collective-permute-start | bytes 4718600 | tf_op jit(solution)/shard_map/ppermute | solution.py:26
  29.0 0.6 fusion.122
  30.9 29.3 %collective-permute-done.3 = bf16[16,128,384]{2,1,0:T(8,128)(2,1)S(1)} collective-permute-done((bf16[16,128,384]{2,1,0:T(8,128)(2,1)S(1)}, bf16[16,128,384]{2,1,0:T(8,128)(2,1)S(1)}, u32[]{:S(2)}, u32[]{:S(2)}) %collective-permute-start.3) | collective-permute-done | bytes 1572896 | tf_op jit(solution)/shard_map/ppermute | solution.py:26
  63.4 1.1 multiply_convert_fusion.1
  64.6 1.3 collective-permute-start.4
  65.9 1.3 collective-permute-start.5
  67.2 0.6 fusion.112
  67.8 3.8 %collective-permute-done.5 = bf16[1,64,384]{2,1,0:T(8,128)(2,1)S(1)} collective-permute-done((bf16[1,64,384]{2,1,0:T(8,128)(2,1)S(1)}, bf16[1,64,384]{2,1,0:T(8,128)(2,1)S(1)}, u32[]{:S(2)}, u32[]{:S(2)}) %collective-permute-start.5) | collective-permute-done | bytes 49184 | tf_op jit(solution)/shard_map/ppermute | solution.py:18
  71.7 4.4 %collective-permute-start.6 = (bf16[18,1,384]{2,1,0:T(2,128)(2,1)S(1)}, bf16[18,1,384]{2,1,0:T(2,128)(2,1)S(1)}, u32[]{:S(2)}, u32[]{:S(2)}) collective-permute-start(bf16[18,1,384]{2,1,0:T(2,128)(2,1)S(1)} %get-tuple-element.9), channel_id=1, source_target_pairs={{0,1},{1,2},{2,3},{3,4},{4,5},{5,6},{6,7},{8,9},{9,10},{10,11},{11... | collective-permute-start | bytes 41480 | tf_op jit(solution)/shard_map/ppermute | solution.py:15
  76.1 1.5 collective-permute-start.7
  77.5 0.6 fusion.9
  78.8 4.0 %collective-permute-done.7 = bf16[18,1,384]{2,1,0:T(2,128)(2,1)S(1)} collective-permute-done((bf16[18,1,384]{2,1,0:T(2,128)(2,1)S(1)}, bf16[18,1,384]{2,1,0:T(2,128)(2,1)S(1)}, u32[]{:S(2)}, u32[]{:S(2)}) %collective-permute-start.7) | collective-permute-done | bytes 13856 | tf_op jit(solution)/shard_map/ppermute | solution.py:18
  83.4 0.6 fusion.57
  84.0 0.6 fusion.61
  84.6 0.6 fusion.59
  85.3 0.6 fusion.63
  85.9 0.6 fusion.65
  86.6 1.3 add_convert_fusion.1
  87.9 4.6 %collective-permute-start.8 = (bf16[16,64,384]{2,1,0:T(8,128)(2,1)S(1)}, bf16[16,64,384]{2,1,0:T(8,128)(2,1)S(1)}, u32[]{:S(2)}, u32[]{:S(2)}) collective-permute-start(bf16[16,64,384]{2,1,0:T(8,128)(2,1)S(1)} %add_convert_fusion.1), channel_id=1, source_target_pairs={{0,1},{1,2},{2,3},{3,4},{4,5},{5,6},{6,7},{8,9},{9,10},{10,11},{11... | collective-permute-start | bytes 2359304 | tf_op jit(solution)/shard_map/ppermute | solution.py:15
  92.5 1.3 collective-permute-start.9
  93.8 33.0 %collective-permute-done.8 = bf16[16,64,384]{2,1,0:T(8,128)(2,1)S(1)} collective-permute-done((bf16[16,64,384]{2,1,0:T(8,128)(2,1)S(1)}, bf16[16,64,384]{2,1,0:T(8,128)(2,1)S(1)}, u32[]{:S(2)}, u32[]{:S(2)}) %collective-permute-start.8) | collective-permute-done | bytes 786464 | tf_op jit(solution)/shard_map/ppermute | solution.py:15
  126.8 1.7 pad_maximum_fusion
  128.5 1.3 collective-permute-start.11
  129.8 9.7 %collective-permute-start.10 = (bf16[16,192,384]{2,1,0:T(8,128)(2,1)}, bf16[16,192,384]{2,1,0:T(8,128)(2,1)}, u32[]{:S(2)}, u32[]{:S(2)}) collective-permute-start(bf16[16,192,384]{2,1,0:T(8,128)(2,1)} %pad_maximum_fusion), channel_id=1, source_target_pairs={{0,32},{8,40},{16,48},{24,56},{32,64},{40,72},{48,80},{56,88},{64,... | collective-permute-start | bytes 7077896 | tf_op jit(solution)/shard_map/ppermute | solution.py:26
  139.5 1.7 fusion.101
  142.6 45.9 %collective-permute-done.11 = bf16[16,192,384]{2,1,0:T(8,128)(2,1)} collective-permute-done((bf16[16,192,384]{2,1,0:T(8,128)(2,1)}, bf16[16,192,384]{2,1,0:T(8,128)(2,1)}, u32[]{:S(2)}, u32[]{:S(2)}) %collective-permute-start.11) | collective-permute-done | bytes 2359328 | tf_op jit(solution)/shard_map/ppermute | solution.py:26
  188.5 1.8 fusion.43
  190.3 1.8 fusion.45
  192.1 1.8 fusion.47
  193.9 1.8 fusion.49
  195.6 1.8 fusion.51
  197.4 2.4 multiply_convert_fusion
  199.9 1.6 collective-permute-start.12
  201.5 1.3 collective-permute-start.13
  202.8 0.6 fusion.90
  203.5 1.6 collective-permute-done.13
  205.1 4.7 %collective-permute-start.14 = (bf16[18,1,384]{2,1,0:T(2,128)(2,1)S(1)}, bf16[18,1,384]{2,1,0:T(2,128)(2,1)S(1)}, u32[]{:S(2)}, u32[]{:S(2)}) collective-permute-start(bf16[18,1,384]{2,1,0:T(2,128)(2,1)S(1)} %get-tuple-element.5), channel_id=1, source_target_pairs={{0,1},{1,2},{2,3},{3,4},{4,5},{5,6},{6,7},{8,9},{9,10},{10,11},{11... | collective-permute-start | bytes 41480 | tf_op jit(solution)/shard_map/ppermute | solution.py:15
  209.8 1.6 collective-permute-start.15
  212.6 26.1 %collective-permute-done.14 = bf16[18,1,384]{2,1,0:T(2,128)(2,1)S(1)} collective-permute-done((bf16[18,1,384]{2,1,0:T(2,128)(2,1)S(1)}, bf16[18,1,384]{2,1,0:T(2,128)(2,1)S(1)}, u32[]{:S(2)}, u32[]{:S(2)}) %collective-permute-start.14) | collective-permute-done | bytes 13856 | tf_op jit(solution)/shard_map/ppermute | solution.py:15
  238.7 2.2 collective-permute-done.15
  241.5 0.6 fusion.29
  242.1 0.6 fusion.33
  242.8 0.6 fusion.31
  243.4 0.6 fusion.35
  244.0 0.6 fusion.37
  244.7 1.3 add_convert_fusion
  246.0 1.1 convolution_convert_fusion.1
  247.1 3.5 copy.15
  250.7 33.8 %all-to-all-start = ((bf16[64,64,384]{2,1,0:T(8,128)(2,1)}), bf16[64,64,384]{2,1,0:T(8,128)(2,1)}, u32[]{:S(2)}, u32[]{:S(2)}) async-start(bf16[64,64,384]{2,1,0:T(8,128)(2,1)} %copy.15), calls=%async_computation | async-start | bytes 6291456 | tf_op jit(solution)/shard_map/all_to_all | solution.py:105
  284.5 42.3 %all-to-all-done = bf16[64,64,384]{2,1,0:T(8,128)(2,1)} async-done(((bf16[64,64,384]{2,1,0:T(8,128)(2,1)}), bf16[64,64,384]{2,1,0:T(8,128)(2,1)}, u32[]{:S(2)}, u32[]{:S(2)}) %all-to-all-start) | async-done | bytes 3145760 | tf_op jit(solution)/shard_map/all_to_all | solution.py:105
  326.8 2.5 reduce
  329.9 14.0 %all_to_all.10 = bf16[4,128,384]{2,0,1:T(4,128)(2,1)S(1)} all-to-all(bf16[4,128,384]{2,0,1:T(4,128)(2,1)S(1)} %copy.18), channel_id=1, replica_groups=mesh['row'=16,'col'=8] {'col'}, dimensions={1} | all-to-all | bytes 786432 | tf_op jit(solution)/shard_map/all_to_all | solution.py:115
  344.8 1.3 collective-permute-start.16
  346.1 1.3 collective-permute-start.17
  347.6 4.3 %collective-permute-done.17 = bf16[1,64,96]{2,1,0:T(8,128)(2,1)S(1)} collective-permute-done((bf16[1,64,96]{2,1,0:T(8,128)(2,1)S(1)}, bf16[1,64,96]{2,1,0:T(8,128)(2,1)S(1)}, u32[]{:S(2)}, u32[]{:S(2)}) %collective-permute-start.17) | collective-permute-done | bytes 12320 | tf_op jit(solution)/shard_map/ppermute | solution.py:18
  351.9 2.9 collective-permute-start.18
  354.8 1.3 collective-permute-start.19
  356.6 3.8 %collective-permute-done.19 = bf16[18,1,96]{2,1,0:T(2,128)(2,1)S(1)} collective-permute-done((bf16[18,1,96]{2,1,0:T(2,128)(2,1)S(1)}, bf16[18,1,96]{2,1,0:T(2,128)(2,1)S(1)}, u32[]{:S(2)}, u32[]{:S(2)}) %collective-permute-start.19) | collective-permute-done | bytes 3488 | tf_op jit(solution)/shard_map/ppermute | solution.py:18
  361.6 0.9 fusion.6
  (67 shorter events, 12.4 us)
Async XLA Ops:
  0.6 343.4 %copy-start = (bf16[384,1536]{1,0:T(8,128)(2,1)S(1)}, bf16[384,1536]{1,0:T(8,128)(2,1)}, u32[]{:S(2)}) copy-start(bf16[384,1536]{1,0:T(8,128)(2,1)} %param.12) | copy-start | bytes 3538948
  0.6 22.1 %copy-start.1 = (bf16[16,64,384]{2,1,0:T(8,128)(2,1)S(1)}, bf16[16,64,384]{2,1,0:T(8,128)(2,1)}, u32[]{:S(2)}) copy-start(bf16[16,64,384]{2,1,0:T(8,128)(2,1)} %param.7) | copy-start | bytes 2359300
  2.0 20.7 %collective-permute-start = (bf16[16,32,384]{2,1,0:T(8,128)(2,1)S(1)}, bf16[16,32,384]{2,1,0:T(8,128)(2,1)S(1)}, u32[]{:S(2)}, u32[]{:S(2)}) collective-permute-start(bf16[16,32,384]{2,1,0:T(8,128)(2,1)S(1)} %get-tuple-element.15), channel_id=1, source_target_pairs={{0,1},{1,2},{2,3},{3,4},{4,5},{5,6},{6,7},{8,9},{9,10},{10,11},{11... | collective-permute-start | bytes 1179656 | tf_op jit(solution)/shard_map/ppermute | solution.py:15
  6.0 23.0 %copy-start.3 = (bf16[3,3,384,384]{3,2,1,0:T(8,128)(2,1)S(1)}, bf16[3,3,384,384]{3,2,1,0:T(8,128)(2,1)}, u32[]{:S(2)}) copy-start(bf16[3,3,384,384]{3,2,1,0:T(8,128)(2,1)} %param.8) | copy-start | bytes 7962628
  6.0 17.0 %collective-permute-start.1 = (bf16[16,32,384]{2,1,0:T(8,128)(2,1)S(1)}, bf16[16,32,384]{2,1,0:T(8,128)(2,1)S(1)}, u32[]{:S(2)}, u32[]{:S(2)}) collective-permute-start(bf16[16,32,384]{2,1,0:T(8,128)(2,1)S(1)} %get-tuple-element.14), channel_id=1, source_target_pairs={{1,0},{2,1},{3,2},{4,3},{5,4},{6,5},{7,6},{9,8},{10,9},{11,10},{12... | collective-permute-start | bytes 1179656 | tf_op jit(solution)/shard_map/ppermute | solution.py:18
  23.1 37.2 %collective-permute-start.3 = (bf16[16,128,384]{2,1,0:T(8,128)(2,1)S(1)}, bf16[16,128,384]{2,1,0:T(8,128)(2,1)S(1)}, u32[]{:S(2)}, u32[]{:S(2)}) collective-permute-start(bf16[16,128,384]{2,1,0:T(8,128)(2,1)S(1)} %constant_dynamic-update-slice_fusion), channel_id=1, source_target_pairs={{16,0},{24,8},{32,16},{40,24},{48,32},{56,40},{64,48},{72,56},{80,... | collective-permute-start | bytes 4718600 | tf_op jit(solution)/shard_map/ppermute | solution.py:26
  24.4 37.1 %collective-permute-start.2 = (bf16[16,128,384]{2,1,0:T(8,128)(2,1)S(1)}, bf16[16,128,384]{2,1,0:T(8,128)(2,1)S(1)}, u32[]{:S(2)}, u32[]{:S(2)}) collective-permute-start(bf16[16,128,384]{2,1,0:T(8,128)(2,1)S(1)} %constant_dynamic-update-slice_fusion), channel_id=1, source_target_pairs={{0,16},{8,24},{16,32},{24,40},{32,48},{40,56},{48,64},{56,72},{64,... | collective-permute-start | bytes 4718600 | tf_op jit(solution)/shard_map/ppermute | solution.py:26
  63.4 3.8 %copy-start.5 = (bf16[3,3,384,384]{3,2,1,0:T(8,128)(2,1)S(1)}, bf16[3,3,384,384]{3,2,1,0:T(8,128)(2,1)}, u32[]{:S(2)}) copy-start(bf16[3,3,384,384]{3,2,1,0:T(8,128)(2,1)} %param.9) | copy-start | bytes 7962628
  64.6 3.2 collective-permute-start.4
  65.9 5.8 %collective-permute-start.5 = (bf16[1,64,384]{2,1,0:T(8,128)(2,1)S(1)}, bf16[1,64,384]{2,1,0:T(8,128)(2,1)S(1)}, u32[]{:S(2)}, u32[]{:S(2)}) collective-permute-start(bf16[1,64,384]{2,1,0:T(8,128)(2,1)S(1)} %get-tuple-element.13), channel_id=1, source_target_pairs={{8,0},{16,8},{24,16},{32,24},{40,32},{48,40},{56,48},{64,56},{72,6... | collective-permute-start | bytes 147464 | tf_op jit(solution)/shard_map/ppermute | solution.py:18
  71.7 7.1 %collective-permute-start.6 = (bf16[18,1,384]{2,1,0:T(2,128)(2,1)S(1)}, bf16[18,1,384]{2,1,0:T(2,128)(2,1)S(1)}, u32[]{:S(2)}, u32[]{:S(2)}) collective-permute-start(bf16[18,1,384]{2,1,0:T(2,128)(2,1)S(1)} %get-tuple-element.9), channel_id=1, source_target_pairs={{0,1},{1,2},{2,3},{3,4},{4,5},{5,6},{6,7},{8,9},{9,10},{10,11},{11... | collective-permute-start | bytes 41480 | tf_op jit(solution)/shard_map/ppermute | solution.py:15
  76.1 6.7 %collective-permute-start.7 = (bf16[18,1,384]{2,1,0:T(2,128)(2,1)S(1)}, bf16[18,1,384]{2,1,0:T(2,128)(2,1)S(1)}, u32[]{:S(2)}, u32[]{:S(2)}) collective-permute-start(bf16[18,1,384]{2,1,0:T(2,128)(2,1)S(1)} %get-tuple-element.8), channel_id=1, source_target_pairs={{1,0},{2,1},{3,2},{4,3},{5,4},{6,5},{7,6},{9,8},{10,9},{11,10},{12... | collective-permute-start | bytes 41480 | tf_op jit(solution)/shard_map/ppermute | solution.py:18
  87.9 38.9 %collective-permute-start.8 = (bf16[16,64,384]{2,1,0:T(8,128)(2,1)S(1)}, bf16[16,64,384]{2,1,0:T(8,128)(2,1)S(1)}, u32[]{:S(2)}, u32[]{:S(2)}) collective-permute-start(bf16[16,64,384]{2,1,0:T(8,128)(2,1)S(1)} %add_convert_fusion.1), channel_id=1, source_target_pairs={{0,1},{1,2},{2,3},{3,4},{4,5},{5,6},{6,7},{8,9},{9,10},{10,11},{11... | collective-permute-start | bytes 2359304 | tf_op jit(solution)/shard_map/ppermute | solution.py:15
  92.5 34.3 %collective-permute-start.9 = (bf16[16,64,384]{2,1,0:T(8,128)(2,1)S(1)}, bf16[16,64,384]{2,1,0:T(8,128)(2,1)S(1)}, u32[]{:S(2)}, u32[]{:S(2)}) collective-permute-start(bf16[16,64,384]{2,1,0:T(8,128)(2,1)S(1)} %add_convert_fusion.1), channel_id=1, source_target_pairs={{1,0},{2,1},{3,2},{4,3},{5,4},{6,5},{7,6},{9,8},{10,9},{11,10},{12... | collective-permute-start | bytes 2359304 | tf_op jit(solution)/shard_map/ppermute | solution.py:18
  128.5 60.0 %collective-permute-start.11 = (bf16[16,192,384]{2,1,0:T(8,128)(2,1)}, bf16[16,192,384]{2,1,0:T(8,128)(2,1)}, u32[]{:S(2)}, u32[]{:S(2)}) collective-permute-start(bf16[16,192,384]{2,1,0:T(8,128)(2,1)} %pad_maximum_fusion), channel_id=1, source_target_pairs={{32,0},{40,8},{48,16},{56,24},{64,32},{72,40},{80,48},{88,56},{96,... | collective-permute-start | bytes 7077896 | tf_op jit(solution)/shard_map/ppermute | solution.py:26
  129.8 62.3 %collective-permute-start.10 = (bf16[16,192,384]{2,1,0:T(8,128)(2,1)}, bf16[16,192,384]{2,1,0:T(8,128)(2,1)}, u32[]{:S(2)}, u32[]{:S(2)}) collective-permute-start(bf16[16,192,384]{2,1,0:T(8,128)(2,1)} %pad_maximum_fusion), channel_id=1, source_target_pairs={{0,32},{8,40},{16,48},{24,56},{32,64},{40,72},{48,80},{56,88},{64,... | collective-permute-start | bytes 7077896 | tf_op jit(solution)/shard_map/ppermute | solution.py:26
  139.5 1.8 copy-start.4
  197.4 5.4 %copy-start.6 = (bf16[3,3,384,384]{3,2,1,0:T(8,128)(2,1)S(1)}, bf16[3,3,384,384]{3,2,1,0:T(8,128)(2,1)}, u32[]{:S(2)}) copy-start(bf16[3,3,384,384]{3,2,1,0:T(8,128)(2,1)} %param.11) | copy-start | bytes 7962628
  199.9 3.6 collective-permute-start.12
  201.5 3.5 collective-permute-start.13
  205.1 33.6 %collective-permute-start.14 = (bf16[18,1,384]{2,1,0:T(2,128)(2,1)S(1)}, bf16[18,1,384]{2,1,0:T(2,128)(2,1)S(1)}, u32[]{:S(2)}, u32[]{:S(2)}) collective-permute-start(bf16[18,1,384]{2,1,0:T(2,128)(2,1)S(1)} %get-tuple-element.5), channel_id=1, source_target_pairs={{0,1},{1,2},{2,3},{3,4},{4,5},{5,6},{6,7},{8,9},{9,10},{10,11},{11... | collective-permute-start | bytes 41480 | tf_op jit(solution)/shard_map/ppermute | solution.py:15
  209.8 31.1 %collective-permute-start.15 = (bf16[18,1,384]{2,1,0:T(2,128)(2,1)S(1)}, bf16[18,1,384]{2,1,0:T(2,128)(2,1)S(1)}, u32[]{:S(2)}, u32[]{:S(2)}) collective-permute-start(bf16[18,1,384]{2,1,0:T(2,128)(2,1)S(1)} %get-tuple-element.4), channel_id=1, source_target_pairs={{1,0},{2,1},{3,2},{4,3},{5,4},{6,5},{7,6},{9,8},{10,9},{11,10},{12... | collective-permute-start | bytes 41480 | tf_op jit(solution)/shard_map/ppermute | solution.py:18
  246.0 1.1 copy-start.2
  250.7 76.1 %all-to-all-start = ((bf16[64,64,384]{2,1,0:T(8,128)(2,1)}), bf16[64,64,384]{2,1,0:T(8,128)(2,1)}, u32[]{:S(2)}, u32[]{:S(2)}) async-start(bf16[64,64,384]{2,1,0:T(8,128)(2,1)} %copy.15), calls=%async_computation | async-start | bytes 6291456 | tf_op jit(solution)/shard_map/all_to_all | solution.py:105
  343.9 3.5 copy-start.7
  344.8 2.8 collective-permute-start.16
  346.1 5.8 %collective-permute-start.17 = (bf16[1,64,96]{2,1,0:T(8,128)(2,1)S(1)}, bf16[1,64,96]{2,1,0:T(8,128)(2,1)S(1)}, u32[]{:S(2)}, u32[]{:S(2)}) collective-permute-start(bf16[1,64,96]{2,1,0:T(8,128)(2,1)S(1)} %get-tuple-element.21), channel_id=1, source_target_pairs={{8,0},{16,8},{24,16},{32,24},{40,32},{48,40},{56,48},{64,56},{72,6... | collective-permute-start | bytes 36872 | tf_op jit(solution)/shard_map/ppermute | solution.py:18
  351.9 4.7 %collective-permute-start.18 = (bf16[18,1,96]{2,1,0:T(2,128)(2,1)S(1)}, bf16[18,1,96]{2,1,0:T(2,128)(2,1)S(1)}, u32[]{:S(2)}, u32[]{:S(2)}) collective-permute-start(bf16[18,1,96]{2,1,0:T(2,128)(2,1)S(1)} %get-tuple-element.18), channel_id=1, source_target_pairs={{0,1},{1,2},{2,3},{3,4},{4,5},{5,6},{6,7},{8,9},{9,10},{10,11},{11... | collective-permute-start | bytes 10376 | tf_op jit(solution)/shard_map/ppermute | solution.py:15
  354.8 5.6 %collective-permute-start.19 = (bf16[18,1,96]{2,1,0:T(2,128)(2,1)S(1)}, bf16[18,1,96]{2,1,0:T(2,128)(2,1)S(1)}, u32[]{:S(2)}, u32[]{:S(2)}) collective-permute-start(bf16[18,1,96]{2,1,0:T(2,128)(2,1)S(1)} %get-tuple-element.19), channel_id=1, source_target_pairs={{1,0},{2,1},{3,2},{4,3},{5,4},{6,5},{7,6},{9,8},{10,9},{11,10},{12... | collective-permute-start | bytes 10376 | tf_op jit(solution)/shard_map/ppermute | solution.py:18
where the time goes:
time: 368 us; the launch traced here: 363 us
  waiting for transfers between devices  211 us (57%)
  starting transfers between devices  86.5 us (24%)
  matrix products  37.4 us (10%)
  blocking collectives  14 us (4%)
  local copies, waits for them, and re-layouts  5.93 us (2%)
  other arithmetic  5.77 us (2%)
    ppermute x4, waiting for transfers between devices, shifted(): return lax.ppermute(block, axis, route)  75.2 us
    ppermute x8, waiting for transfers between devices, with_halo(): lax.ppermute(lax.slice_in_dim(block, block.shape[dim] - width, None, axis...  74.4 us
    all_to_all x1, waiting for transfers between devices, shards(): lax.all_to_all(outgoing, 'row', split_axis=0, concat_axis=0, tiled=True)  42.3 us
    all_to_all x1, starting transfers between devices, shards(): lax.all_to_all(outgoing, 'row', split_axis=0, concat_axis=0, tiled=True)  33.8 us
    ppermute x8, starting transfers between devices, with_halo(): lax.ppermute(lax.slice_in_dim(block, block.shape[dim] - width, None, axis...  24.8 us
    dot_general x18, matrix products, tap_line(): jnp.einsum('rcf,fg->rcg', window, kernel[tap_row, tap_col], preferred_ele...  20.3 us
    ppermute x8, waiting for transfers between devices, with_halo(): lax.ppermute(lax.slice_in_dim(block, 0, width, axis=dim), axis, backward)  19.6 us
    ppermute x4, starting transfers between devices, shifted(): return lax.ppermute(block, axis, route)  16.9 us
  transfers between devices with their start and end apart: 21, of which 12 were waited for; matrix products, arithmetic and copies ran while one was open for 4% of the time, Pallas kernels for 0%

commit v1 on v0

v1 whole, which is shorter than its diff:
```python
import jax
import jax.numpy as jnp
from jax import lax
from jax.sharding import Mesh, PartitionSpec as P

AXES = ("zh", "y1", "y0", "core", "x1", "x0", "zl")
ROW = ("zh", "y1", "y0", "core")
COL = ("x1", "x0", "zl")
SPREAD = ("zh", "y1", "y0", "x1", "x0", "zl")
BF16 = jnp.bfloat16
F32 = jnp.float32


def device_of_band(band):
    core, rest = divmod(band, 8)
    return rest * 2 + core


def band_route(step):
    return [(device_of_band(b), device_of_band((b + step) % 16)) for b in range(16)]


def ring_route(step):
    return [(i, (i + step) % 8) for i in range(8)]


def line_route(count, step):
    return [(i, i + step) for i in range(count) if 0 <= i + step < count]


def dilated(cells, kernel, spacing):
    return lax.conv_general_dilated(
        cells, kernel, (1, 1), ((spacing, spacing), (spacing, spacing)),
        rhs_dilation=(spacing, spacing), dimension_numbers=("HWNC", "HWIO", "HWNC"),
        preferred_element_type=F32,
    )


def plain(hidden, state, kernel, first_band, last_band, first_ring, last_ring):
    channels = hidden.shape[-1]
    tiles = hidden.reshape(8, 16, 2, 4, channels)
    up = lax.ppermute(tiles[:, :, 1], ROW, band_route(1))
    down = lax.ppermute(tiles[:, :, 0], ROW, band_route(-1))
    nothing = jnp.zeros((1, 16, 4, channels), BF16)
    up = jnp.where(first_band, jnp.concatenate([nothing, up[:-1]], 0), up)
    down = jnp.where(last_band, jnp.concatenate([down[1:], nothing], 0), down)
    above = jnp.concatenate([up[:, :, None], tiles[:, :, :1]], 2)
    below = jnp.concatenate([tiles[:, :, 1:], down[:, :, None]], 2)
    stack = jnp.concatenate([t.reshape(1024, channels) for t in (above, tiles, below)], 1)
    weights = [kernel[:, b].reshape(3 * channels, channels) for b in range(3)]
    to_right, centre, to_left = (
        jnp.dot(stack, w, preferred_element_type=F32).reshape(8, 16, 2, 4, channels)
        for w in weights
    )
    from_left = lax.ppermute(to_right[:, :, :, 3].astype(BF16), COL, ring_route(1))
    from_right = lax.ppermute(to_left[:, :, :, 0].astype(BF16), COL, ring_route(-1))
    nothing = jnp.zeros((8, 1, 2, channels), BF16)
    from_left = jnp.where(first_ring, jnp.concatenate([nothing, from_left[:, :-1]], 1), from_left)
    from_right = jnp.where(last_ring, jnp.concatenate([from_right[:, 1:], nothing], 1), from_right)
    total = (
        centre
        + jnp.concatenate([from_left[:, :, :, None].astype(F32), to_right[:, :, :, :3]], 3)
        + jnp.concatenate([to_left[:, :, :, 1:], from_right[:, :, :, None].astype(F32)], 3)
    )
    return (state.astype(F32) + total.reshape(8, 16, 8, channels)).astype(BF16)


def crop_route():
    route = []
    for bits in range(128):
        i3, i2, i5, i4, j4, j6, j5 = ((bits >> k) & 1 for k in range(6, -1, -1))
        target = 0
        for bit in (i5, i4, i3, i2, j6, j5, j4):
            target = target * 2 + bit
        route.append((bits, target))
    return route


def fine_target(state, lift_weight, fine_weight):
    channels = state.shape[-1]
    width = fine_weight.shape[-1]
    crop = state[4:6, 8:12].reshape(8, 8, channels)
    crop = lax.all_to_all(crop, ("y0", "x0", "zl"), 0, 0, tiled=True)
    crop = crop.reshape(2, 4, 2, 4, channels).transpose(0, 2, 1, 3, 4).reshape(4, 16, channels)
    crop = lax.ppermute(crop, AXES, crop_route())
    for axis, dim, count in ((ROW, 0, 16), (COL, 1, 8)):
        size = crop.shape[dim]
        low = lax.ppermute(lax.slice_in_dim(crop, size - 1, size, axis=dim), axis, line_route(count, 1))
        high = lax.ppermute(lax.slice_in_dim(crop, 0, 1, axis=dim), axis, line_route(count, -1))
        crop = jnp.concatenate([low, crop, high], dim)
    lifted = jnp.einsum("rcf,fg->rcg", crop, lift_weight, preferred_element_type=F32).astype(BF16)
    lifted = lifted.reshape(6, 18, 4, 4, width).transpose(0, 2, 1, 3, 4).reshape(24, 72, width)
    lifted = lifted[3:21, 3:69]
    target = lax.conv_general_dilated(
        lifted[None], fine_weight, (1, 1), ((0, 0), (0, 0)),
        dimension_numbers=("NHWC", "HWIO", "NHWC"), preferred_element_type=F32,
    )
    return target[0].astype(BF16)


def shards(context, first_dilated_weight, first_plain_weight, second_dilated_weight,
           second_plain_weight, lift_weight, fine_weight):
    channels = context.shape[-1]
    band = 8 * lax.axis_index("core") + lax.axis_index(("zh", "y1", "y0"))
    ring = lax.axis_index(COL)
    ends = (band == 0, band == 15, ring == 0, ring == 7)
    sent = context.reshape(8, 2, 2, 8, 4, channels).transpose(0, 3, 2, 1, 4, 5)
    state = lax.all_to_all(sent.reshape(64, 16, channels), SPREAD, 0, 0, tiled=True)
    state = state.reshape(8, 16, 8, channels)
    for dilated_kernel, plain_kernel, spacing in (
        (first_dilated_weight, first_plain_weight, 1),
        (second_dilated_weight, second_plain_weight, 2),
    ):
        hidden = jax.nn.silu(dilated(state, dilated_kernel, spacing)).astype(BF16)
        state = plain(hidden, state, plain_kernel, *ends)
    target = fine_target(state, lift_weight, fine_weight)
    back = lax.all_to_all(state.reshape(64, 16, channels), SPREAD, 0, 0, tiled=True)
    back = back.reshape(8, 8, 2, 2, 4, channels).transpose(0, 3, 2, 1, 4, 5)
    return back.reshape(16, 64, channels), target


def solution(mesh):
    fine_mesh = Mesh(mesh.devices.reshape((2,) * 7), AXES)
    return jax.shard_map(
        shards,
        mesh=fine_mesh,
        in_specs=(P(ROW, COL, None), P(), P(), P(), P(), P(), P()),
        out_specs=(P(ROW, COL, None), P(ROW, COL, None)),
        check_vma=False,
    )
```

time: 368 us -> 191 us (0.52); the launches traced: 363 us -> 190 us
  waiting for transfers between devices: 211 us -> 53.2 us
  starting transfers between devices: 86.5 us -> 40.4 us
  local copies, waits for them, and re-layouts: 5.93 us -> 31.6 us
  blocking collectives: 14 us -> 35.3 us
  matrix products: 37.4 us -> 23.4 us
    ppermute x20 -> x13, waiting for transfers between devices: 169 us -> 40.2 us  [the longest x2 12.8 us: plain(): up = lax.ppermute(tiles[:, :, 1], ROW, band_route(1))]
    all_to_all x1, waiting for transfers between devices: 42.3 us -> 13.1 us  [shards(): lax.all_to_all(state.reshape(64, 16, channels), SPREAD, 0, 0, tiled=True)]
    ppermute x20 -> x13, starting transfers between devices: 52.7 us -> 25 us  [the longest x2 9.68 us: fine_target(): lax.ppermute(lax.slice_in_dim(crop, size - 1, size, axis=dim), axis, line...]
    dot_general x48 -> x7, matrix products: 37.4 us -> 12.8 us  [the longest x6 12.4 us: plain(): jnp.dot(stack, w, preferred_element_type=F32).reshape(8, 16, 2, 4, channels)]
    all_to_all x1 -> x2, blocking collectives: 14 us -> 35.3 us  [the longest x1 27.1 us: shards(): lax.all_to_all(sent.reshape(64, 16, channels), SPREAD, 0, 0, tiled=True)]
    all_to_all x1, starting transfers between devices: 33.8 us -> 15.4 us  [shards(): lax.all_to_all(state.reshape(64, 16, channels), SPREAD, 0, 0, tiled=True)]
    reshape x1 -> x16, local copies, waits for them, and re-layouts: 0.23 us -> 17.8 us  [the longest x4 5.6 us: plain(): tiles = hidden.reshape(8, 16, 2, 4, channels)]
    conv_general_dilated x0 -> x3, matrix products: none -> 10.6 us  [the longest x2 9.8 us: dilated(): lax.conv_general_dilated(cells, kernel, (1, 1), ((spacing, spacing), (spa...]
  transfers between devices with their start and end apart: 21 -> 14, of which waited for: 12 -> 10; matrix products, arithmetic and copies ran while one was open for 4% -> 11% of each run, Pallas kernels for 0% -> 0%
where the time goes in v1:
time: 191 us; the launch traced here: 190 us
  waiting for transfers between devices  53.2 us (28%)
  starting transfers between devices  40.4 us (21%)
  blocking collectives  35.3 us (18%)
  local copies, waits for them, and re-layouts  31.6 us (17%)
  matrix products  23.4 us (12%)
  other arithmetic  5.19 us (3%)
    all_to_all x1, blocking collectives, shards(): lax.all_to_all(sent.reshape(64, 16, channels), SPREAD, 0, 0, tiled=True)  27.1 us
    all_to_all x1, starting transfers between devices, shards(): lax.all_to_all(state.reshape(64, 16, channels), SPREAD, 0, 0, tiled=True)  15.4 us
    all_to_all x1, waiting for transfers between devices, shards(): lax.all_to_all(state.reshape(64, 16, channels), SPREAD, 0, 0, tiled=True)  13.1 us
    ppermute x2, waiting for transfers between devices, plain(): up = lax.ppermute(tiles[:, :, 1], ROW, band_route(1))  12.8 us
    dot_general x6, matrix products, plain(): jnp.dot(stack, w, preferred_element_type=F32).reshape(8, 16, 2, 4, channels)  12.4 us
    ppermute x2, waiting for transfers between devices, plain(): lax.ppermute(to_right[:, :, :, 3].astype(BF16), COL, ring_route(1))  11.8 us
    conv_general_dilated x2, matrix products, dilated(): lax.conv_general_dilated(cells, kernel, (1, 1), ((spacing, spacing), (spa...  9.8 us
    ppermute x2, starting transfers between devices, fine_target(): lax.ppermute(lax.slice_in_dim(crop, size - 1, size, axis=dim), axis, line...  9.68 us
  transfers between devices with their start and end apart: 14, of which 10 were waited for; matrix products, arithmetic and copies ran while one was open for 11% of the time, Pallas kernels for 0%

profile of v1, /device:TPU:0, one launch (start us, length us, event | category | flops | bytes accessed | tf_op | source)
XLA Modules:
  0.0 190.4 jit_solution(16847305540246276469)
XLA Ops:
  0.6 2.5 %reshape.118 = bf16[8,2,2,8,4,384]{5,4,3,2,1,0:T(4,128)(2,1)} reshape(bf16[16,64,384]{2,1,0:T(8,128)(2,1)} %param.7) | data formatting | bytes 1572864 | tf_op jit(solution)/shard_map/reshape | solution.py:107
  3.2 1.4 copy.118
  4.6 1.1 reshape.119
  5.6 27.1 %all_to_all.15 = bf16[64,16,384]{2,1,0:T(8,128)(2,1)S(1)} all-to-all(bf16[64,16,384]{2,1,0:T(8,128)(2,1)} %reshape.119), channel_id=1, replica_groups=mesh['zh'=2,'y1'=2,'y0'=2,'core'=2,'x1'=2,'x0'=2,'zl'=2] {'zh','y1','y0'..., dimensions={0} | all-to-all | bytes 1572864 | tf_op jit(solution)/shard_map/all_to_all | solution.py:108
  32.7 4.9 %multiply_convert_fusion.1 = bf16[8,16,8,384]{3,2,1,0:T(8,128)(2,1)} fusion(bf16[8,16,8,384]{3,2,1,0:T(8,128)(2,1)S(1)} %bitcast.118, bf16[3,3,384,384]{3,2,1,0:T(8,128)(2,1)S(1)} %copy-done), kind=kOutput, calls=%fused_computation.18 | convolution fusion | flops 2389573632 | bytes 4227072 | tf_op jit(solution)/shard_map/conv_general_dilated | solution.py:32
  37.6 1.7 reshape.121
  39.3 0.4 fusion.40
  39.7 0.8 copy.119
  40.5 0.8 copy.121
  41.3 2.0 %collective-permute-start = (bf16[8,16,4,384]{3,1,2,0:T(8,128)(2,1)}, bf16[8,16,4,384]{3,1,2,0:T(8,128)(2,1)S(1)}, u32[]{:S(2)}, u32[]{:S(2)}) collective-permute-start(bf16[8,16,4,384]{3,1,2,0:T(8,128)(2,1)} %bitcast.114), channel_id=1, source_target_pairs={{0,16},{16,32},{32,48},{48,64},{64,80},{80,96},{96,112},{112,8},{8... | collective-permute-start | bytes 1179656 | tf_op jit(solution)/shard_map/ppermute | solution.py:42
  43.3 2.0 %fusion.39 = (bf16[3,1,384,384]{3,2,1,0:T(8,128)(2,1)S(1)}, bf16[3,1,384,384]{3,2,1,0:T(8,128)(2,1)S(1)}, bf16[3,1,384,384]{3,2,1,0:T(8,128)(2,1)S(1)}) fusion(bf16[3,3,384,384]{3,2,1,0:T(8,128)(2,1)} %param.9), kind=kLoop, calls=%fused_computation.74 | loop fusion | bytes 5308416 | tf_op jit(solution)/shard_map/slice | solution.py:50
  45.3 0.1 copy.36
  45.4 4.9 %collective-permute-done.1 = bf16[8,16,4,384]{3,1,2,0:T(8,128)(2,1)S(1)} collective-permute-done((bf16[8,16,4,384]{3,1,2,0:T(8,128)(2,1)}, bf16[8,16,4,384]{3,1,2,0:T(8,128)(2,1)S(1)}, u32[]{:S(2)}, u32[]{:S(2)}) %collective-permute-start.1) | collective-permute-done | bytes 393248 | tf_op jit(solution)/shard_map/ppermute | solution.py:43
  50.3 4.1 %collective-permute-done = bf16[8,16,4,384]{3,1,2,0:T(8,128)(2,1)S(1)} collective-permute-done((bf16[8,16,4,384]{3,1,2,0:T(8,128)(2,1)}, bf16[8,16,4,384]{3,1,2,0:T(8,128)(2,1)S(1)}, u32[]{:S(2)}, u32[]{:S(2)}) %collective-permute-start) | collective-permute-done | bytes 393248 | tf_op jit(solution)/shard_map/ppermute | solution.py:42
  54.6 2.7 %fusion.35 = f32[8,16,2,4,384]{4,1,3,2,0:T(8,128)S(1)} fusion(bf16[1152,384,1,1,1]{1,0,4,3,2:T(8,128)(2,1)S(1)} %bitcast.132, bf16[8,16,1,4,384]{4,1,3,2,0:T(8,128)(2,1)S(1)} %select_bitcast_fusion.2, bf16[8,16,1,4,384]{4,1,3,2,0:T(8,128)(2,1)} %bitcast.84.clone.2, bf16[8,16,2,4,384]{4,1,3,2,0:T(8,128)(2,1)S(1)} %copy.36, ...), kind=kOutput, calls=%fused_computation.70 | convolution fusion | flops 915800064 | bytes 4816896 | tf_op jit(solution)/shard_map/dot_general | solution.py:52
  57.4 1.4 collective-permute-start.3
  58.7 2.7 %fusion.36 = f32[8,16,2,4,384]{4,1,3,2,0:T(8,128)S(1)} fusion(bf16[1152,384,1,1,1]{1,0,4,3,2:T(8,128)(2,1)S(1)} %bitcast.131, bf16[8,16,1,4,384]{4,1,3,2,0:T(8,128)(2,1)S(1)} %select_bitcast_fusion.2, bf16[8,16,1,4,384]{4,1,3,2,0:T(8,128)(2,1)} %bitcast.84.clone.2, bf16[8,16,2,4,384]{4,1,3,2,0:T(8,128)(2,1)S(1)} %copy.36, ...), kind=kOutput, calls=%fused_computation.71 | convolution fusion | flops 915800064 | bytes 4816896 | tf_op jit(solution)/shard_map/dot_general | solution.py:52
  61.5 1.0 collective-permute-start.2
  62.5 1.8 collective-permute-done.3
  64.4 6.5 %collective-permute-done.2 = bf16[8,16,2,384]{3,1,2,0:T(8,128)(2,1)S(1)} collective-permute-done((bf16[8,16,2,384]{3,1,2,0:T(8,128)(2,1)S(1)}, bf16[8,16,2,384]{3,1,2,0:T(8,128)(2,1)S(1)}, u32[]{:S(2)}, u32[]{:S(2)}) %collective-permute-start.2) | collective-permute-done | bytes 196640 | tf_op jit(solution)/shard_map/ppermute | solution.py:55
  71.1 2.8 %fusion.6 = f32[8,16,2,4,384]{4,1,3,2,0:T(8,128)S(1)} fusion(f32[8,16,2,3,384]{4,1,3,2,0:T(8,128)S(1)} %slice.144, f32[8,16,2,1,384]{4,1,3,2,0:T(8,128)S(1)} %bitcast_convert_fusion.3, f32[8,16,2,1,384]{4,1,3,2,0:T(8,128)S(1)} %bitcast_convert_fusion.2, f32[8,16,2,3,384]{4,1,3,2,0:T(8,128)S(1)} %slice-done, bf16[1152,384,1,1,1]{1,0,4,3,2:T(8,128)(2,1)S(1)} %bitcast.128, ...), kind=kOutput, calls=%fused_computation.10 | convolution fusion | flops 917372928 | bytes 7962624 | tf_op jit(solution)/shard_map/dot_general | solution.py:52
  73.9 0.6 fusion.8
  74.5 1.1 copy-done.8
  75.6 4.9 %multiply_convert_fusion = bf16[8,16,8,384]{3,2,1,0:T(8,128)(2,1)} fusion(bf16[8,16,8,384]{3,2,1,0:T(8,128)(2,1)S(1)} %fusion.8, bf16[3,3,384,384]{3,2,1,0:T(8,128)(2,1)S(1)} %copy-done.8), kind=kOutput, calls=%fused_computation.16 | convolution fusion | flops 2078146560 | bytes 4227072 | tf_op jit(solution)/shard_map/conv_general_dilated | solution.py:32
  80.5 2.4 %reshape.124 = bf16[8,16,2,4,384]{4,3,2,1,0:T(4,128)(2,1)} reshape(bf16[8,16,8,384]{3,2,1,0:T(8,128)(2,1)} %multiply_convert_fusion) | data formatting | bytes 1572864 | tf_op jit(solution)/shard_map/reshape | solution.py:41
  82.9 1.4 copy.41
  84.3 0.2 slice_bitcast_fusion.3
  84.7 5.3 %collective-permute-start.5 = (bf16[8,16,4,384]{3,1,2,0:T(8,128)(2,1)S(1)}, bf16[8,16,4,384]{3,1,2,0:T(8,128)(2,1)S(1)}, u32[]{:S(2)}, u32[]{:S(2)}) collective-permute-start(bf16[8,16,4,384]{3,1,2,0:T(8,128)(2,1)S(1)} %get-tuple-element.11), channel_id=1, source_target_pairs={{0,120},{16,0},{32,16},{48,32},{64,48},{80,64},{96,80},{112,96},{8... | collective-permute-start | bytes 1179656 | tf_op jit(solution)/shard_map/ppermute | solution.py:43
  90.0 0.3 fusion.38
  90.3 8.7 %collective-permute-done.4 = bf16[8,16,4,384]{3,1,2,0:T(8,128)(2,1)S(1)} collective-permute-done((bf16[8,16,4,384]{3,1,2,0:T(8,128)(2,1)S(1)}, bf16[8,16,4,384]{3,1,2,0:T(8,128)(2,1)S(1)}, u32[]{:S(2)}, u32[]{:S(2)}) %collective-permute-start.4) | collective-permute-done | bytes 393248 | tf_op jit(solution)/shard_map/ppermute | solution.py:42
  99.1 0.3 collective-permute-done.5
  99.4 0.3 maximum_maximum_fusion.1
  99.7 1.4 fusion
  101.2 2.0 %collective-permute-start.7 = (bf16[8,16,2,384]{3,1,2,0:T(8,128)(2,1)S(1)}, bf16[8,16,2,384]{3,1,2,0:T(8,128)(2,1)S(1)}, u32[]{:S(2)}, u32[]{:S(2)}) collective-permute-start(bf16[8,16,2,384]{3,1,2,0:T(8,128)(2,1)S(1)} %fusion.24), channel_id=1, source_target_pairs={{0,7},{1,0},{2,1},{3,2},{4,3},{5,4},{6,5},{7,6},{8,15},{9,8},{10,9... | collective-permute-start | bytes 589832 | tf_op jit(solution)/shard_map/ppermute | solution.py:56
  103.2 1.4 fusion.2
  104.7 0.1 slice.154
  104.8 0.2 collective-permute-start.6
  105.0 3.4 %collective-permute-done.7 = bf16[8,16,2,384]{3,1,2,0:T(8,128)(2,1)S(1)} collective-permute-done((bf16[8,16,2,384]{3,1,2,0:T(8,128)(2,1)S(1)}, bf16[8,16,2,384]{3,1,2,0:T(8,128)(2,1)S(1)}, u32[]{:S(2)}, u32[]{:S(2)}) %collective-permute-start.7) | collective-permute-done | bytes 196640 | tf_op jit(solution)/shard_map/ppermute | solution.py:56
  108.5 5.2 %collective-permute-done.6 = bf16[8,16,2,384]{3,1,2,0:T(8,128)(2,1)S(1)} collective-permute-done((bf16[8,16,2,384]{3,1,2,0:T(8,128)(2,1)S(1)}, bf16[8,16,2,384]{3,1,2,0:T(8,128)(2,1)S(1)}, u32[]{:S(2)}, u32[]{:S(2)}) %collective-permute-start.6) | collective-permute-done | bytes 196640 | tf_op jit(solution)/shard_map/ppermute | solution.py:55
  113.8 1.5 fusion.7
  115.3 1.2 copy-done.3
  116.4 0.8 fusion.30
  117.3 8.2 %all_to_all.16 = bf16[8,8,384]{2,1,0:T(8,128)(2,1)S(1)} all-to-all(bf16[8,8,384]{2,1,0:T(8,128)(2,1)S(1)} %bitcast.136), channel_id=1, replica_groups=mesh['zh'=2,'y1'=2,'y0'=2,'core'=2,'x1'=2,'x0'=2,'zl'=2] {'y0','x0','zl'}, dimensions={0} | all-to-all | bytes 98304 | tf_op jit(solution)/shard_map/all_to_all | solution.py:83
  125.5 0.7 collective-permute-start.8
  126.2 6.4 %collective-permute-start.9 = (bf16[1,16,384]{2,1,0:T(8,128)(2,1)S(1)}, bf16[1,16,384]{2,1,0:T(8,128)(2,1)S(1)}, u32[]{:S(2)}, u32[]{:S(2)}) collective-permute-start(bf16[1,16,384]{2,1,0:T(8,128)(2,1)S(1)} %get-tuple-element.23), channel_id=1, source_target_pairs={{0,8},{8,16},{16,24},{24,32},{32,40},{40,48},{48,56},{56,64},{64,7... | collective-permute-start | bytes 36872 | tf_op jit(solution)/shard_map/ppermute | solution.py:88
  132.7 1.8 copy.39
  134.5 2.8 %reshape.122 = f32[64,16,384]{2,1,0:T(8,128)} reshape(f32[8,16,2,4,384]{4,3,2,1,0:T(4,128)} %copy.39) | data formatting | bytes 3145728 | tf_op jit(solution)/shard_map/reshape | solution.py:65
  137.2 2.0 %copy.51 = f32[8,16,2,4,384]{4,3,2,1,0:T(4,128)S(1)} copy(f32[8,16,2,4,384]{4,1,3,2,0:T(8,128)} %copy-done.3) | data formatting | bytes 3145728 | tf_op jit(solution)/shard_map/add | solution.py:61
  139.2 1.7 reshape.125
  140.9 1.3 collective-permute-start.10
  142.3 5.3 %collective-permute-done.10 = bf16[1,16,384]{2,1,0:T(8,128)(2,1)S(1)} collective-permute-done((bf16[1,16,384]{2,1,0:T(8,128)(2,1)S(1)}, bf16[1,16,384]{2,1,0:T(8,128)(2,1)S(1)}, u32[]{:S(2)}, u32[]{:S(2)}) %collective-permute-start.10) | collective-permute-done | bytes 12320 | tf_op jit(solution)/shard_map/ppermute | solution.py:89
  147.6 3.2 %collective-permute-start.11 = (bf16[6,1,384]{2,1,0:T(2,128)(2,1)S(1)}, bf16[6,1,384]{2,1,0:T(2,128)(2,1)S(1)}, u32[]{:S(2)}, u32[]{:S(2)}) collective-permute-start(bf16[6,1,384]{2,1,0:T(2,128)(2,1)S(1)} %get-tuple-element.20), channel_id=1, source_target_pairs={{0,1},{1,2},{2,3},{3,4},{4,5},{5,6},{6,7},{8,9},{9,10},{10,11},{11... | collective-permute-start | bytes 13832 | tf_op jit(solution)/shard_map/ppermute | solution.py:88
  150.8 1.4 collective-permute-start.12
  152.3 3.0 %add_convert_fusion = bf16[64,16,384]{2,1,0:T(8,128)(2,1)} fusion(f32[64,16,384]{2,1,0:T(8,128)} %reshape.125, f32[64,16,384]{2,1,0:T(8,128)} %reshape.122, bf16[64,16,384]{2,1,0:T(8,128)(2,1)S(1)} %all_to_all.15), kind=kLoop, calls=%fused_computation.15 | loop fusion | flops 2359296 | bytes 4718592 | tf_op jit(solution)/shard_map/convert_element_type | solution.py:65
  155.3 15.4 %all-to-all-start.1 = ((bf16[64,16,384]{2,1,0:T(8,128)(2,1)}), bf16[64,16,384]{2,1,0:T(8,128)(2,1)S(1)}, u32[]{:S(2)}, u32[]{:S(2)}) async-start(bf16[64,16,384]{2,1,0:T(8,128)(2,1)} %add_convert_fusion), calls=%async_computation.1 | async-start | bytes 1572864 | tf_op jit(solution)/shard_map/all_to_all | solution.py:117
  170.7 0.4 convolution_convert_fusion
  171.2 0.4 reshape.132
  171.6 0.2 copy.55
  172.1 0.8 fusion.11
  173.0 0.8 copy.60
  173.7 13.1 %all-to-all-done.1 = bf16[64,16,384]{2,1,0:T(8,128)(2,1)S(1)} async-done(((bf16[64,16,384]{2,1,0:T(8,128)(2,1)}), bf16[64,16,384]{2,1,0:T(8,128)(2,1)S(1)}, u32[]{:S(2)}, u32[]{:S(2)}) %all-to-all-start.1) | async-done | bytes 786464 | tf_op jit(solution)/shard_map/all_to_all | solution.py:117
  186.8 1.1 reshape.126
  187.9 1.5 copy.52
  189.4 1.1 reshape.127
  (65 shorter events, 1.5 us)
Async XLA Ops:
  0.6 32.1 %copy-start = (bf16[3,3,384,384]{3,2,1,0:T(8,128)(2,1)S(1)}, bf16[3,3,384,384]{3,2,1,0:T(8,128)(2,1)}, u32[]{:S(2)}) copy-start(bf16[3,3,384,384]{3,2,1,0:T(8,128)(2,1)} %param.8) | copy-start | bytes 7962628
  41.3 9.0 %collective-permute-start.1 = (bf16[8,16,4,384]{3,1,2,0:T(8,128)(2,1)}, bf16[8,16,4,384]{3,1,2,0:T(8,128)(2,1)S(1)}, u32[]{:S(2)}, u32[]{:S(2)}) collective-permute-start(bf16[8,16,4,384]{3,1,2,0:T(8,128)(2,1)} %bitcast.99.clone.2), channel_id=1, source_target_pairs={{0,120},{16,0},{32,16},{48,32},{64,48},{80,64},{96,80},{112,96},{8... | collective-permute-start | bytes 1179656 | tf_op jit(solution)/shard_map/ppermute | solution.py:43
  41.3 13.2 %collective-permute-start = (bf16[8,16,4,384]{3,1,2,0:T(8,128)(2,1)}, bf16[8,16,4,384]{3,1,2,0:T(8,128)(2,1)S(1)}, u32[]{:S(2)}, u32[]{:S(2)}) collective-permute-start(bf16[8,16,4,384]{3,1,2,0:T(8,128)(2,1)} %bitcast.114), channel_id=1, source_target_pairs={{0,16},{16,32},{32,48},{48,64},{64,80},{80,96},{96,112},{112,8},{8... | collective-permute-start | bytes 1179656 | tf_op jit(solution)/shard_map/ppermute | solution.py:42
  57.3 4.1 %copy-start.4 = (f32[8,16,2,4,384]{4,1,3,2,0:T(8,128)}, f32[8,16,2,4,384]{4,1,3,2,0:T(8,128)S(1)}, u32[]{:S(2)}) copy-start(f32[8,16,2,4,384]{4,1,3,2,0:T(8,128)S(1)} %fusion.35) | copy-start | bytes 4718596
  57.4 7.0 %collective-permute-start.3 = (bf16[8,16,2,384]{3,1,2,0:T(8,128)(2,1)S(1)}, bf16[8,16,2,384]{3,1,2,0:T(8,128)(2,1)S(1)}, u32[]{:S(2)}, u32[]{:S(2)}) collective-permute-start(bf16[8,16,2,384]{3,1,2,0:T(8,128)(2,1)S(1)} %fusion.22), channel_id=1, source_target_pairs={{0,7},{1,0},{2,1},{3,2},{4,3},{5,4},{6,5},{7,6},{8,15},{9,8},{10,9... | collective-permute-start | bytes 589832 | tf_op jit(solution)/shard_map/ppermute | solution.py:56
  61.5 9.6 %slice-start = ((f32[8,16,2,4,384]{4,1,3,2,0:T(8,128)}), f32[8,16,2,3,384]{4,1,3,2,0:T(8,128)S(1)}, s32[]{:S(2)}) async-start(f32[8,16,2,4,384]{4,1,3,2,0:T(8,128)} %copy-done.4), calls=%async_computation.3 | async-start | bytes 2359296 | tf_op jit(solution)/shard_map/slice | solution.py:63
  61.5 9.4 %collective-permute-start.2 = (bf16[8,16,2,384]{3,1,2,0:T(8,128)(2,1)S(1)}, bf16[8,16,2,384]{3,1,2,0:T(8,128)(2,1)S(1)}, u32[]{:S(2)}, u32[]{:S(2)}) collective-permute-start(bf16[8,16,2,384]{3,1,2,0:T(8,128)(2,1)S(1)} %fusion.21), channel_id=1, source_target_pairs={{0,1},{1,2},{2,3},{3,4},{4,5},{5,6},{6,7},{7,0},{8,9},{9,10},{10,1... | collective-permute-start | bytes 589832 | tf_op jit(solution)/shard_map/ppermute | solution.py:55
  73.9 1.8 copy-start.8
  75.6 4.9 %copy-start.7 = (bf16[8,16,8,384]{3,2,1,0:T(8,128)(2,1)}, bf16[8,16,8,384]{3,2,1,0:T(8,128)(2,1)S(1)}, u32[]{:S(2)}) copy-start(bf16[8,16,8,384]{3,2,1,0:T(8,128)(2,1)S(1)} %fusion.8) | copy-start | bytes 2359300
  82.9 7.1 %copy-start.2 = (bf16[3,3,384,384]{3,2,1,0:T(8,128)(2,1)S(1)}, bf16[3,3,384,384]{3,2,1,0:T(8,128)(2,1)}, u32[]{:S(2)}) copy-start(bf16[3,3,384,384]{3,2,1,0:T(8,128)(2,1)} %param.11) | copy-start | bytes 7962628
  84.6 14.4 %collective-permute-start.4 = (bf16[8,16,4,384]{3,1,2,0:T(8,128)(2,1)S(1)}, bf16[8,16,4,384]{3,1,2,0:T(8,128)(2,1)S(1)}, u32[]{:S(2)}, u32[]{:S(2)}) collective-permute-start(bf16[8,16,4,384]{3,1,2,0:T(8,128)(2,1)S(1)} %get-tuple-element.10), channel_id=1, source_target_pairs={{0,16},{16,32},{32,48},{48,64},{64,80},{80,96},{96,112},{112,8},{8... | collective-permute-start | bytes 1179656 | tf_op jit(solution)/shard_map/ppermute | solution.py:42
  84.7 14.7 %collective-permute-start.5 = (bf16[8,16,4,384]{3,1,2,0:T(8,128)(2,1)S(1)}, bf16[8,16,4,384]{3,1,2,0:T(8,128)(2,1)S(1)}, u32[]{:S(2)}, u32[]{:S(2)}) collective-permute-start(bf16[8,16,4,384]{3,1,2,0:T(8,128)(2,1)S(1)} %get-tuple-element.11), channel_id=1, source_target_pairs={{0,120},{16,0},{32,16},{48,32},{64,48},{80,64},{96,80},{112,96},{8... | collective-permute-start | bytes 1179656 | tf_op jit(solution)/shard_map/ppermute | solution.py:43
  101.2 3.5 %copy-start.5 = (f32[8,16,2,4,384]{4,1,3,2,0:T(8,128)}, f32[8,16,2,4,384]{4,1,3,2,0:T(8,128)S(1)}, u32[]{:S(2)}) copy-start(f32[8,16,2,4,384]{4,1,3,2,0:T(8,128)S(1)} %fusion) | copy-start | bytes 4718596
  101.2 7.2 %collective-permute-start.7 = (bf16[8,16,2,384]{3,1,2,0:T(8,128)(2,1)S(1)}, bf16[8,16,2,384]{3,1,2,0:T(8,128)(2,1)S(1)}, u32[]{:S(2)}, u32[]{:S(2)}) collective-permute-start(bf16[8,16,2,384]{3,1,2,0:T(8,128)(2,1)S(1)} %fusion.24), channel_id=1, source_target_pairs={{0,7},{1,0},{2,1},{3,2},{4,3},{5,4},{6,5},{7,6},{8,15},{9,8},{10,9... | collective-permute-start | bytes 589832 | tf_op jit(solution)/shard_map/ppermute | solution.py:56
  104.8 9.0 %slice-start.1 = ((f32[8,16,2,4,384]{4,1,3,2,0:T(8,128)}), f32[8,16,2,3,384]{4,1,3,2,0:T(8,128)S(1)}, s32[]{:S(2)}) async-start(f32[8,16,2,4,384]{4,1,3,2,0:T(8,128)} %copy-done.5), calls=%async_computation.4 | async-start | bytes 2359296 | tf_op jit(solution)/shard_map/slice | solution.py:63
  104.8 8.9 %collective-permute-start.6 = (bf16[8,16,2,384]{3,1,2,0:T(8,128)(2,1)S(1)}, bf16[8,16,2,384]{3,1,2,0:T(8,128)(2,1)S(1)}, u32[]{:S(2)}, u32[]{:S(2)}) collective-permute-start(bf16[8,16,2,384]{3,1,2,0:T(8,128)(2,1)S(1)} %fusion.23), channel_id=1, source_target_pairs={{0,1},{1,2},{2,3},{3,4},{4,5},{5,6},{6,7},{7,0},{8,9},{9,10},{10,1... | collective-permute-start | bytes 589832 | tf_op jit(solution)/shard_map/ppermute | solution.py:55
  115.3 1.2 copy-start.3
  125.5 0.7 collective-permute-start.8
  126.2 16.0 %collective-permute-start.9 = (bf16[1,16,384]{2,1,0:T(8,128)(2,1)S(1)}, bf16[1,16,384]{2,1,0:T(8,128)(2,1)S(1)}, u32[]{:S(2)}, u32[]{:S(2)}) collective-permute-start(bf16[1,16,384]{2,1,0:T(8,128)(2,1)S(1)} %get-tuple-element.23), channel_id=1, source_target_pairs={{0,8},{8,16},{16,24},{24,32},{32,40},{40,48},{48,56},{56,64},{64,7... | collective-permute-start | bytes 36872 | tf_op jit(solution)/shard_map/ppermute | solution.py:88
  140.9 6.6 %collective-permute-start.10 = (bf16[1,16,384]{2,1,0:T(8,128)(2,1)S(1)}, bf16[1,16,384]{2,1,0:T(8,128)(2,1)S(1)}, u32[]{:S(2)}, u32[]{:S(2)}) collective-permute-start(bf16[1,16,384]{2,1,0:T(8,128)(2,1)S(1)} %get-tuple-element.22), channel_id=1, source_target_pairs={{8,0},{16,8},{24,16},{32,24},{40,32},{48,40},{56,48},{64,56},{72,6... | collective-permute-start | bytes 36872 | tf_op jit(solution)/shard_map/ppermute | solution.py:89
  147.6 23.1 %collective-permute-start.11 = (bf16[6,1,384]{2,1,0:T(2,128)(2,1)S(1)}, bf16[6,1,384]{2,1,0:T(2,128)(2,1)S(1)}, u32[]{:S(2)}, u32[]{:S(2)}) collective-permute-start(bf16[6,1,384]{2,1,0:T(2,128)(2,1)S(1)} %get-tuple-element.20), channel_id=1, source_target_pairs={{0,1},{1,2},{2,3},{3,4},{4,5},{5,6},{6,7},{8,9},{9,10},{10,11},{11... | collective-permute-start | bytes 13832 | tf_op jit(solution)/shard_map/ppermute | solution.py:88
  150.8 19.9 %copy-start.6 = (bf16[384,1536]{1,0:T(8,128)(2,1)S(1)}, bf16[384,1536]{1,0:T(8,128)(2,1)}, u32[]{:S(2)}) copy-start(bf16[384,1536]{1,0:T(8,128)(2,1)} %param.12) | copy-start | bytes 3538948
  150.8 19.9 %collective-permute-start.12 = (bf16[6,1,384]{2,1,0:T(2,128)(2,1)S(1)}, bf16[6,1,384]{2,1,0:T(2,128)(2,1)S(1)}, u32[]{:S(2)}, u32[]{:S(2)}) collective-permute-start(bf16[6,1,384]{2,1,0:T(2,128)(2,1)S(1)} %get-tuple-element.21), channel_id=1, source_target_pairs={{1,0},{2,1},{3,2},{4,3},{5,4},{6,5},{7,6},{9,8},{10,9},{11,10},{12... | collective-permute-start | bytes 13832 | tf_op jit(solution)/shard_map/ppermute | solution.py:89
  155.3 31.5 %all-to-all-start.1 = ((bf16[64,16,384]{2,1,0:T(8,128)(2,1)}), bf16[64,16,384]{2,1,0:T(8,128)(2,1)S(1)}, u32[]{:S(2)}, u32[]{:S(2)}) async-start(bf16[64,16,384]{2,1,0:T(8,128)(2,1)} %add_convert_fusion), calls=%async_computation.1 | async-start | bytes 1572864 | tf_op jit(solution)/shard_map/all_to_all | solution.py:117
  171.1 0.9 copy-start.9
  171.2 0.9 copy-start.10
  172.9 17.5 %copy-start.1 = (bf16[3,3,384,384]{3,2,1,0:T(8,128)(2,1)S(1)}, bf16[3,3,384,384]{3,2,1,0:T(8,128)(2,1)}, u32[]{:S(2)}) copy-start(bf16[3,3,384,384]{3,2,1,0:T(8,128)(2,1)} %param.8) | copy-start | bytes 7962628

commit v2 on v1

v2 whole, which is shorter than its diff:
```python
import jax
import jax.numpy as jnp
from jax import lax
from jax.experimental import pallas as pl
from jax.experimental.pallas import tpu as pltpu
from jax.sharding import Mesh, PartitionSpec as P


AXES = ("zh", "y1", "y0", "core", "x1", "x0", "zl")
ROW = ("zh", "y1", "y0", "core")
COL = ("x1", "x0", "zl")
SPREAD = ("zh", "y1", "y0", "x1", "x0", "zl")
BF16 = jnp.bfloat16
F32 = jnp.float32
VMEM = pl.BlockSpec(memory_space=pltpu.VMEM)
SMEM = pl.BlockSpec(memory_space=pltpu.SMEM)


def kernel_call(body, outs, scratch=(), inputs=0, scalars=0, limit=24):
    call = pl.pallas_call(
        body,
        out_shape=[pltpu.VMEM(s, t) for s, t in outs],
        in_specs=[SMEM] * scalars + [VMEM] * inputs,
        out_specs=[VMEM] * len(outs),
        scratch_shapes=[pltpu.VMEM(s, t) for s, t in scratch],
        compiler_params=pltpu.CompilerParams(vmem_limit_bytes=limit << 20),
    )

    def run(*operands):
        near = [pltpu.with_memory_space_constraint(x, pltpu.VMEM) for x in operands[scalars:]]
        return call(*operands[:scalars], *near)

    return run


def device_of_band(band):
    core, rest = divmod(band, 8)
    return rest * 2 + core


def band_route(step):
    return [(device_of_band(b), device_of_band((b + step) % 16)) for b in range(16)]


def ring_route(step):
    return [(i, (i + step) % 8) for i in range(8)]


def line_route(count, step):
    return [(i, i + step) for i in range(count) if 0 <= i + step < count]


def gather_body(context, sent):
    channels = context.shape[-1]
    first = lax.broadcasted_iota(jnp.int32, (4, 8, channels), 1) < 4

    def step(row, carry):
        line = context[row].astype(F32)
        low = line[:32].reshape(4, 8, channels)
        high = line[32:].reshape(4, 8, channels)
        even = jnp.where(first, low, pltpu.roll(high, 4, 1))
        odd = jnp.where(first, pltpu.roll(low, 4, 1), high)
        for pair in range(4):
            place = 8 * (row // 2) + 2 * pair
            sent[place, row % 2] = even[pair].astype(BF16)
            sent[place + 1, row % 2] = odd[pair].astype(BF16)
        return carry

    lax.fori_loop(0, 16, step, 0)


def scatter_body(landed, result):
    channels = result.shape[-1]
    first = lax.broadcasted_iota(jnp.int32, (8, channels), 0) < 4

    def step(row, carry):
        for pair in range(4):
            place = 8 * (row // 2) + 2 * pair
            even = landed[place, row % 2].astype(F32)
            odd = landed[place + 1, row % 2].astype(F32)
            low = jnp.where(first, even, pltpu.roll(odd, 4, 0))
            high = jnp.where(first, pltpu.roll(even, 4, 0), odd)
            result[row, 8 * pair : 8 * pair + 8] = low.astype(BF16)
            result[row, 32 + 8 * pair : 40 + 8 * pair] = high.astype(BF16)
        return carry

    lax.fori_loop(0, 16, step, 0)


def dilated_band(cells, kernel, hidden, shelves, spacing):
    channels = cells.shape[-1]
    reach = 4 * spacing
    place = lax.broadcasted_iota(jnp.int32, cells.shape, 1)
    left = jnp.where(place < reach, 0.0, pltpu.roll(cells, reach, 1))
    right = jnp.where(place >= 64 - reach, 0.0, pltpu.roll(cells, 64 - reach, 1))
    edge = jnp.zeros((spacing, 64, channels), BF16)
    for index, shelf in enumerate((left, cells, right)):
        shelves[index, :spacing] = edge
        shelves[index, spacing : spacing + 8] = shelf.astype(BF16)
        shelves[index, spacing + 8 : spacing + 8 + spacing] = edge
    stack = jnp.concatenate(
        [
            shelves[b, a * spacing : a * spacing + 8].reshape(512, channels)
            for a in range(3)
            for b in range(3)
        ],
        axis=1,
    )
    total = jnp.dot(stack, kernel[...], preferred_element_type=F32)
    hidden[...] = (total / (1.0 + jnp.exp(-total))).astype(BF16)


def first_dilated_body(landed, kernel, hidden0, hidden1, shelves):
    channels = landed.shape[-1]
    for i0, hidden in enumerate((hidden0, hidden1)):
        cells = landed[:, i0].astype(F32).reshape(8, 64, channels)
        dilated_band(cells, kernel, hidden, shelves, 1)


def settle(partial, sums, from_left, from_right, ends, i0, channels):
    place = lax.broadcasted_iota(jnp.int32, (128, channels), 0) % 16
    left = from_left[i0].astype(F32)
    right = from_right[i0].astype(F32)
    left = jnp.where(
        ends[2] == 1, jnp.where(place == 0, 0.0, pltpu.roll(left, 1, 0)), left
    )
    right = jnp.where(
        ends[3] == 1, jnp.where(place == 15, 0.0, pltpu.roll(right, 127, 0)), right
    )
    pieces = []
    for lane in range(0, channels, 128):
        inner = sums.at[i0, lane // 128]
        inner[...] = partial[i0, :, lane : lane + 128]
        inner[pl.ds(0, 128, stride=4)] = inner[pl.ds(0, 128, stride=4)] + left[:, lane : lane + 128]
        inner[pl.ds(3, 128, stride=4)] = inner[pl.ds(3, 128, stride=4)] + right[:, lane : lane + 128]
        pieces.append(inner[...].astype(BF16))
    return jnp.concatenate(pieces, 1)


def second_dilated_body(ends, partial, from_left, from_right, kernel, state, hidden0, hidden1, sums, shelves):
    channels = state.shape[-1]
    for i0, hidden in enumerate((hidden0, hidden1)):
        cells = settle(partial, sums, from_left, from_right, ends, i0, channels)
        state[:, i0] = cells.reshape(64, 8, channels)
        dilated_band(cells.astype(F32).reshape(8, 64, channels), kernel, hidden, shelves, 2)


def final_body(ends, partial, from_left, from_right, state, sums):
    channels = state.shape[-1]
    for i0 in range(2):
        cells = settle(partial, sums, from_left, from_right, ends, i0, channels)
        state[:, i0] = cells.reshape(64, 8, channels)


def edge_body(ends, up, down, hidden0, hidden1, kernel, to_left, to_right, above, below, wide):
    channels = up.shape[-1]
    blank = jnp.zeros((64, channels), BF16)
    above[:64] = blank
    above[64:] = up[...]
    below[:512] = down[...]
    below[512:] = blank
    start = pl.multiple_of(64 - 64 * ends[0], 64)
    lines = [above[pl.ds(start, 512)], hidden0[...], hidden1[...]]
    start = pl.multiple_of(64 * ends[1], 64)
    lines.append(below[pl.ds(start, 512)])
    for index, line in enumerate(lines):
        for lane in range(0, channels, 128):
            wide[index, lane // 128] = line[:, lane : lane + 128].astype(F32)
    for column, tap, sums in ((3, 0, to_right), (0, 2, to_left)):
        weights = kernel[:, tap].reshape(3 * channels, channels)
        lines = [
            jnp.concatenate(
                [
                    wide.at[line, lane][pl.ds(column, 128, stride=4)].astype(BF16)
                    for lane in range(channels // 128)
                ],
                1,
            )
            for line in range(4)
        ]
        stack = jnp.concatenate(
            [jnp.concatenate(lines[:3], 1), jnp.concatenate(lines[1:], 1)], 0
        )
        product = jnp.dot(stack, weights, preferred_element_type=F32).astype(BF16)
        sums[0] = product[:128]
        sums[1] = product[128:]


def plain_body(ends, up, down, hidden0, hidden1, state, kernel, partial, above, below):
    channels = up.shape[-1]
    blank = jnp.zeros((64, channels), BF16)
    above[:64] = blank
    above[64:] = up[...]
    below[:512] = down[...]
    below[512:] = blank
    over = above[pl.ds(pl.multiple_of(64 - 64 * ends[0], 64), 512)]
    under = below[pl.ds(pl.multiple_of(64 * ends[1], 64), 512)]
    lines = (over, hidden0[...], hidden1[...], under)
    place = lax.broadcasted_iota(jnp.int32, (512, channels), 0) % 4
    for i0 in range(2):
        stack = jnp.concatenate(lines[i0 : i0 + 3], 1)
        products = [
            jnp.dot(stack, kernel[:, tap].reshape(3 * channels, channels), preferred_element_type=F32)
            for tap in range(3)
        ]
        total = state[:, i0].reshape(512, channels).astype(F32) + products[1]
        total = total + jnp.where(place == 0, 0.0, pltpu.roll(products[0], 1, 0))
        total = total + jnp.where(place == 3, 0.0, pltpu.roll(products[2], 511, 0))
        partial[i0] = total


def crop_route(shift):
    route = []
    for bits in range(128):
        i3, i2, i5, i4, j4, j6, j5 = ((bits >> k) & 1 for k in range(6, -1, -1))
        row = 8 * i5 + 4 * i4 + 2 * i3 + i2 + shift
        column = 4 * j6 + 2 * j5 + j4
        if 0 <= row < 16:
            route.append((bits, row * 8 + column))
    return route


def crop_cells(state):
    channels = state.shape[-1]
    crop = state.reshape(8, 8, 2, 2, 4, channels)[4:6, 4:6].transpose(0, 1, 3, 2, 4, 5)
    crop = lax.all_to_all(
        crop.reshape(8, 8, channels), ("y0", "x0", "zl"), 0, 0, tiled=True
    )
    crop = crop.reshape(2, 4, 2, 4, channels).transpose(0, 2, 1, 3, 4)
    return crop.reshape(4, 16, channels)


def fine_target(crop, lift_weight, fine_weight):
    width = fine_weight.shape[-1]
    low = lax.ppermute(crop[3:], AXES, crop_route(1))
    high = lax.ppermute(crop[:1], AXES, crop_route(-1))
    crop = lax.ppermute(crop, AXES, crop_route(0))
    crop = jnp.concatenate([low, crop, high], 0)
    low = lax.ppermute(crop[:, 15:], COL, line_route(8, 1))
    high = lax.ppermute(crop[:, :1], COL, line_route(8, -1))
    crop = jnp.concatenate([low, crop, high], 1)
    lifted = jnp.einsum("rcf,fg->rcg", crop, lift_weight, preferred_element_type=F32).astype(BF16)
    lifted = lifted.reshape(6, 18, 4, 4, width).transpose(0, 2, 1, 3, 4).reshape(24, 72, width)
    lifted = lifted[3:21, 3:69]
    target = lax.conv_general_dilated(
        lifted[None], fine_weight, (1, 1), ((0, 0), (0, 0)),
        dimension_numbers=("NHWC", "HWIO", "NHWC"), preferred_element_type=F32,
    )
    return target[0].astype(BF16)


def plain(hidden0, hidden1, state, kernel, ends):
    channels = hidden0.shape[-1]
    up = lax.ppermute(hidden1, ROW, band_route(1))
    down = lax.ppermute(hidden0, ROW, band_route(-1))
    padded = [((576, channels), BF16)] * 2
    to_left, to_right = kernel_call(
        edge_body,
        [((2, 128, channels), BF16)] * 2,
        padded + [((4, 3, 512, 128), F32)],
        5, 1,
    )(ends, up, down, hidden0, hidden1, kernel)
    from_left = lax.ppermute(to_right, COL, ring_route(1))
    from_right = lax.ppermute(to_left, COL, ring_route(-1))
    (partial,) = kernel_call(plain_body, [((2, 512, channels), F32)], padded, 6, 1)(
        ends, up, down, hidden0, hidden1, state, kernel
    )
    return partial, from_left, from_right


def shards(context, first_dilated_weight, first_plain_weight, second_dilated_weight,
           second_plain_weight, lift_weight, fine_weight):
    channels = context.shape[-1]
    band = 8 * lax.axis_index("core") + lax.axis_index(("zh", "y1", "y0"))
    ring = lax.axis_index(COL)
    ends = jnp.array([0, 15, 0, 7]) == jnp.array([1, 1, 0, 0]) * band + jnp.array([0, 0, 1, 1]) * ring
    ends = ends.astype(jnp.int32)
    spread = (64, 2, 8, channels)
    band_shape = ((512, channels), BF16)
    (sent,) = kernel_call(gather_body, [(spread, BF16)], (), 1)(context)
    state = lax.all_to_all(sent, SPREAD, 0, 0, tiled=True)
    hidden0, hidden1 = kernel_call(
        first_dilated_body, [band_shape] * 2, [((3, 10, 64, channels), BF16)], 2
    )(state, first_dilated_weight.reshape(9 * channels, channels))
    edges = plain(hidden0, hidden1, state, first_plain_weight, ends)
    state, hidden0, hidden1 = kernel_call(
        second_dilated_body,
        [(spread, BF16), band_shape, band_shape],
        [((2, 3, 512, 128), F32), ((3, 12, 64, channels), BF16)],
        4, 1,
    )(ends, *edges, second_dilated_weight.reshape(9 * channels, channels))
    edges = plain(hidden0, hidden1, state, second_plain_weight, ends)
    (state,) = kernel_call(
        final_body, [(spread, BF16)], [((2, 3, 512, 128), F32)], 3, 1
    )(ends, *edges)
    crop = crop_cells(state)
    landed = lax.all_to_all(state, SPREAD, 0, 0, tiled=True)
    target = fine_target(crop, lift_weight, fine_weight)
    (result,) = kernel_call(scatter_body, [((16, 64, channels), BF16)], (), 1)(landed)
    return result, target


def solution(mesh):
    fine_mesh = Mesh(mesh.devices.reshape((2,) * 7), AXES)
    return jax.shard_map(
        shards,
        mesh=fine_mesh,
        in_specs=(P(ROW, COL, None), P(), P(), P(), P(), P(), P()),
        out_specs=(P(ROW, COL, None), P(ROW, COL, None)),
        check_vma=False,
    )
```

time: 191 us -> 152 us (0.80)
  Pallas kernels: 0 us -> 23.7 us
  local copies, waits for them, and re-layouts: 31.6 us -> 8.04 us
  matrix products: 23.4 us -> 1.15 us
  waiting for transfers between devices: 53.2 us -> 38.2 us
  other arithmetic: 5.19 us -> 0.01 us
  starting transfers between devices: 40.4 us -> 44.2 us
    pallas_call x0 -> x9, Pallas kernels: none -> 23.7 us  [run(): return call(*operands[:scalars], *near)]
    reshape x14 -> x4, local copies, waits for them, and re-layouts: 17.2 us -> 1.73 us  [the longest x1 1.68 us: crop_cells(): state.reshape(8, 8, 2, 2, 4, channels)[4:6, 4:6].transpose(0, 1, 3, 2, 4, 5)]
    ppermute x13, waiting for transfers between devices: 40.2 us -> 27.4 us  [the longest x2 17 us: plain(): up = lax.ppermute(hidden1, ROW, band_route(1))]
    dot_general x6 -> x0, matrix products: 12.4 us -> none  [plain(): jnp.dot(stack, w, preferred_element_type=F32).reshape(8, 16, 2, 4, channels)]
    conv_general_dilated x2 -> x0, matrix products: 9.8 us -> none  [dilated(): lax.conv_general_dilated(cells, kernel, (1, 1), ((spacing, spacing), (spa...]
    ppermute x13, starting transfers between devices: 25 us -> 33 us  [the longest x2 10.3 us: plain(): down = lax.ppermute(hidden0, ROW, band_route(-1))]
    convert_element_type x7 -> x1, other arithmetic: 4.72 us -> 0.01 us  [shards(): ends = ends.astype(jnp.int32)]
    all_to_all x1, starting transfers between devices: 15.4 us -> 11.2 us  [shards(): landed = lax.all_to_all(state, SPREAD, 0, 0, tiled=True)]
  transfers between devices with their start and end apart: 14 -> 14, of which waited for: 10 -> 7; matrix products, arithmetic and copies ran while one was open for 11% -> 2% of each run, Pallas kernels for 0% -> 6%
where the time goes in v2:
time: 152 us
  starting transfers between devices  44.2 us (29%)
  waiting for transfers between devices  38.2 us (25%)
  blocking collectives  35.3 us (23%)
  Pallas kernels  23.7 us (16%)
  local copies, waits for them, and re-layouts  8.04 us (5%)
    all_to_all x1, blocking collectives, shards(): state = lax.all_to_all(sent, SPREAD, 0, 0, tiled=True)  26.9 us
    pallas_call x9, Pallas kernels, run(): return call(*operands[:scalars], *near)  23.7 us
    ppermute x2, waiting for transfers between devices, plain(): up = lax.ppermute(hidden1, ROW, band_route(1))  17 us
    all_to_all x1, starting transfers between devices, shards(): landed = lax.all_to_all(state, SPREAD, 0, 0, tiled=True)  11.2 us
    all_to_all x1, waiting for transfers between devices, shards(): landed = lax.all_to_all(state, SPREAD, 0, 0, tiled=True)  10.8 us
    ppermute x2, starting transfers between devices, plain(): down = lax.ppermute(hidden0, ROW, band_route(-1))  10.3 us
    ppermute x1, starting transfers between devices, fine_target(): low = lax.ppermute(crop[:, 15:], COL, line_route(8, 1))  9.11 us
    all_to_all x1, blocking collectives, crop_cells(): lax.all_to_all(crop.reshape(8, 8, channels), ('y0', 'x0', 'zl'), 0, 0, ti...  8.36 us
  transfers between devices with their start and end apart: 14, of which 7 were waited for; matrix products, arithmetic and copies ran while one was open for 2% of the time, Pallas kernels for 6%

profile of v2, /device:TPU:0, one launch (start us, length us, event | category | flops | bytes accessed | tf_op | source)
XLA Modules:
  0.0 151.5 jit_solution(1598919419605741459)
XLA Ops:
  0.6 0.0 copy-start
  0.6 0.0 copy-start.5
  0.7 0.0 copy-start.6
  0.7 1.3 copy-done.6
  1.9 0.3 shard_map.113
  2.2 26.9 %all_to_all.15.landed.state = bf16[64,2,8,384]{3,2,1,0:T(8,128)(2,1)S(1)} all-to-all(bf16[64,2,8,384]{3,2,1,0:T(8,128)(2,1)S(1)} %shard_map.113), channel_id=1, replica_groups=mesh['zh'=2,'y1'=2,'y0'=2,'core'=2,'x1'=2,'x0'=2,'zl'=2] {'zh','y1','y0'..., dimensions={0} | all-to-all | bytes 1572864 | tf_op jit(solution)/shard_map/all_to_all | solution.py:281
  29.1 0.0 copy-done.5
  29.1 4.0 %shard_map.114 = (bf16[512,384]{1,0:T(8,128)(2,1)S(1)}, bf16[512,384]{1,0:T(8,128)(2,1)S(1)}) custom-call(bf16[64,2,8,384]{3,2,1,0:T(8,128)(2,1)S(1)} %all_to_all.15.landed.state, bf16[3456,384]{1,0:T(8,128)(2,1)S(1)} %bitcast.24), custom_call_target="tpu_custom_call" | custom-call | tf_op jit(solution)/shard_map/pallas_call | solution.py:31
  33.1 0.6 collective-permute-start
  33.7 4.9 %collective-permute-start.1 = (bf16[512,384]{1,0:T(8,128)(2,1)S(1)}, bf16[512,384]{1,0:T(8,128)(2,1)S(1)}, u32[]{:S(2)}, u32[]{:S(2)}) collective-permute-start(bf16[512,384]{1,0:T(8,128)(2,1)S(1)} %get-tuple-element.12.hidden0), channel_id=1, source_target_pairs={{0,120},{16,0},{32,16},{48,32},{64,48},{80,64},{96,80},{112,96},{8... | collective-permute-start | bytes 1179656 | tf_op jit(solution)/shard_map/ppermute | solution.py:255
  38.6 0.0 copy-done.7
  38.6 0.0 copy-done.8
  38.6 0.0 copy-done.9
  38.6 7.6 %collective-permute-done.up = bf16[512,384]{1,0:T(8,128)(2,1)S(1)} collective-permute-done((bf16[512,384]{1,0:T(8,128)(2,1)S(1)}, bf16[512,384]{1,0:T(8,128)(2,1)S(1)}, u32[]{:S(2)}, u32[]{:S(2)}) %collective-permute-start) | collective-permute-done | bytes 393248 | tf_op jit(solution)/shard_map/ppermute | solution.py:254
  46.2 0.0 collective-permute-done.1.down
  46.2 1.7 %copy-done.1 = bf16[3,3,384,384]{3,2,1,0:T(8,128)(2,1)S(1)} copy-done((bf16[3,3,384,384]{3,2,1,0:T(8,128)(2,1)S(1)}, bf16[3,3,384,384]{3,2,1,0:T(8,128)(2,1)}, u32[]{:S(2)}) %copy-start.1) | copy-done | bytes 2654232
  48.0 1.5 shard_map.116
  49.4 0.7 collective-permute-start.2
  50.1 3.5 %collective-permute-start.3 = (bf16[2,128,384]{2,1,0:T(8,128)(2,1)S(1)}, bf16[2,128,384]{2,1,0:T(8,128)(2,1)S(1)}, u32[]{:S(2)}, u32[]{:S(2)}) collective-permute-start(bf16[2,128,384]{2,1,0:T(8,128)(2,1)S(1)} %get-tuple-element.14), channel_id=1, source_target_pairs={{0,7},{1,0},{2,1},{3,2},{4,3},{5,4},{6,5},{7,6},{8,15},{9,8},{10,9... | collective-permute-start | bytes 589832 | tf_op jit(solution)/shard_map/ppermute | solution.py:264
  53.6 0.0 copy-done.2
  53.6 4.7 %shard_map.115.partial = f32[2,512,384]{2,1,0:T(8,128)S(1)} custom-call(s32[4]{0:T(128)S(1)} %compare_convert_fusion.ends, bf16[512,384]{1,0:T(8,128)(2,1)S(1)} %collective-permute-done.up, bf16[512,384]{1,0:T(8,128)(2,1)S(1)} %collective-permute-done.1.down, bf16[512,384]{1,0:T(8,128)(2,1)S(1)} %get-tuple-element.12.hidden0, ...), custom_call_target="tpu_custom_call" | custom-call | tf_op jit(solution)/shard_map/pallas_call | solution.py:31
  58.4 0.0 collective-permute-done.2.from_left
  58.4 0.8 collective-permute-done.3.from_right
  59.2 0.0 copy-done.4
  59.2 4.8 %shard_map.117 = (bf16[64,2,8,384]{3,2,1,0:T(8,128)(2,1)S(1)}, bf16[512,384]{1,0:T(8,128)(2,1)S(1)}, bf16[512,384]{1,0:T(8,128)(2,1)S(1)}) custom-call(s32[4]{0:T(128)S(1)} %compare_convert_fusion.ends, f32[2,512,384]{2,1,0:T(8,128)S(1)} %shard_map.115.partial, bf16[2,128,384]{2,1,0:T(8,128)(2,1)S(1)} %collective-permute-done.2.from_left, ...), custom_call_target="tpu_custom_call" | custom-call | tf_op jit(solution)/shard_map/pallas_call | solution.py:31
  64.0 0.1 collective-permute-start.4
  64.1 5.4 %collective-permute-start.5 = (bf16[512,384]{1,0:T(8,128)(2,1)S(1)}, bf16[512,384]{1,0:T(8,128)(2,1)S(1)}, u32[]{:S(2)}, u32[]{:S(2)}) collective-permute-start(bf16[512,384]{1,0:T(8,128)(2,1)S(1)} %get-tuple-element.16.hidden0), channel_id=1, source_target_pairs={{0,120},{16,0},{32,16},{48,32},{64,48},{80,64},{96,80},{112,96},{8... | collective-permute-start | bytes 1179656 | tf_op jit(solution)/shard_map/ppermute | solution.py:255
  69.5 9.4 %collective-permute-done.4.up = bf16[512,384]{1,0:T(8,128)(2,1)S(1)} collective-permute-done((bf16[512,384]{1,0:T(8,128)(2,1)S(1)}, bf16[512,384]{1,0:T(8,128)(2,1)S(1)}, u32[]{:S(2)}, u32[]{:S(2)}) %collective-permute-start.4) | collective-permute-done | bytes 393248 | tf_op jit(solution)/shard_map/ppermute | solution.py:254
  79.0 0.0 collective-permute-done.5.down
  79.0 1.4 shard_map.119
  80.4 0.1 collective-permute-start.6
  80.5 4.1 %collective-permute-start.7 = (bf16[2,128,384]{2,1,0:T(8,128)(2,1)S(1)}, bf16[2,128,384]{2,1,0:T(8,128)(2,1)S(1)}, u32[]{:S(2)}, u32[]{:S(2)}) collective-permute-start(bf16[2,128,384]{2,1,0:T(8,128)(2,1)S(1)} %get-tuple-element.19), channel_id=1, source_target_pairs={{0,7},{1,0},{2,1},{3,2},{4,3},{5,4},{6,5},{7,6},{8,15},{9,8},{10,9... | collective-permute-start | bytes 589832 | tf_op jit(solution)/shard_map/ppermute | solution.py:264
  84.6 4.8 %shard_map.118.partial = f32[2,512,384]{2,1,0:T(8,128)S(1)} custom-call(s32[4]{0:T(128)S(1)} %compare_convert_fusion.ends, bf16[512,384]{1,0:T(8,128)(2,1)S(1)} %collective-permute-done.4.up, bf16[512,384]{1,0:T(8,128)(2,1)S(1)} %collective-permute-done.5.down, bf16[512,384]{1,0:T(8,128)(2,1)S(1)} %get-tuple-element.16.hidden0, ...), custom_call_target="tpu_custom_call" | custom-call | tf_op jit(solution)/shard_map/pallas_call | solution.py:31
  89.4 0.2 collective-permute-done.6.from_left
  89.6 2.6 %collective-permute-done.7.from_right = bf16[2,128,384]{2,1,0:T(8,128)(2,1)S(1)} collective-permute-done((bf16[2,128,384]{2,1,0:T(8,128)(2,1)S(1)}, bf16[2,128,384]{2,1,0:T(8,128)(2,1)S(1)}, u32[]{:S(2)}, u32[]{:S(2)}) %collective-permute-start.7) | collective-permute-done | bytes 196640 | tf_op jit(solution)/shard_map/ppermute | solution.py:264
  92.2 1.8 %shard_map.120 = bf16[64,2,8,384]{3,2,1,0:T(8,128)(2,1)} custom-call(s32[4]{0:T(128)S(1)} %compare_convert_fusion.ends, f32[2,512,384]{2,1,0:T(8,128)S(1)} %shard_map.118.partial, bf16[2,128,384]{2,1,0:T(8,128)(2,1)S(1)} %collective-permute-done.6.from_left, bf16[2,128,384]{2,1,0:T(8,128)(2,1)S(1)} %collective-permute-done.7.from_right), custom_call_target="tpu_custom_call" | custom-call | tf_op jit(solution)/shard_map/pallas_call | solution.py:31
  94.0 1.7 %reshape.31 = bf16[8,8,2,2,4,384]{5,4,3,2,1,0:T(4,128)(2,1)S(1)} reshape(bf16[64,2,8,384]{3,2,1,0:T(8,128)(2,1)} %shard_map.120) | data formatting | bytes 1572864 | tf_op jit(solution)/shard_map/reshape | solution.py:225
  95.8 8.4 %all_to_all.16 = bf16[8,8,384]{2,1,0:T(8,128)(2,1)S(1)} all-to-all(bf16[8,8,384]{2,1,0:T(8,128)(2,1)S(1)} %reshape.32), channel_id=1, replica_groups=mesh['zh'=2,'y1'=2,'y0'=2,'core'=2,'x1'=2,'x0'=2,'zl'=2] {'y0','x0','zl'}, dimensions={0} | all-to-all | bytes 98304 | tf_op jit(solution)/shard_map/all_to_all | solution.py:226
  104.2 1.3 collective-permute-start.8
  105.5 0.7 collective-permute-start.9
  106.2 1.3 collective-permute-start.10
  107.5 0.0 collective-permute-done.8
  107.5 0.0 collective-permute-done.9
  107.5 6.7 %collective-permute-done.10 = bf16[1,16,384]{2,1,0:T(8,128)(2,1)S(1)} collective-permute-done((bf16[1,16,384]{2,1,0:T(8,128)(2,1)S(1)}, bf16[1,16,384]{2,1,0:T(8,128)(2,1)S(1)}, u32[]{:S(2)}, u32[]{:S(2)}) %collective-permute-start.10) | collective-permute-done | bytes 12320 | tf_op jit(solution)/shard_map/ppermute | solution.py:236
  114.3 1.3 collective-permute-start.12
  115.6 9.1 %collective-permute-start.11 = (bf16[6,1,384]{2,1,0:T(2,128)(2,1)S(1)}, bf16[6,1,384]{2,1,0:T(2,128)(2,1)S(1)}, u32[]{:S(2)}, u32[]{:S(2)}) collective-permute-start(bf16[6,1,384]{2,1,0:T(2,128)(2,1)S(1)} %get-tuple-element.22), channel_id=1, source_target_pairs={{0,1},{1,2},{2,3},{3,4},{4,5},{5,6},{6,7},{8,9},{9,10},{10,11},{11... | collective-permute-start | bytes 13832 | tf_op jit(solution)/shard_map/ppermute | solution.py:239
  124.7 11.2 %all-to-all-start.1 = ((bf16[64,2,8,384]{3,2,1,0:T(8,128)(2,1)}), bf16[64,2,8,384]{3,2,1,0:T(8,128)(2,1)S(1)}, u32[]{:S(2)}, u32[]{:S(2)}) async-start(bf16[64,2,8,384]{3,2,1,0:T(8,128)(2,1)} %shard_map.120), calls=%async_computation.1 | async-start | bytes 1572864 | tf_op jit(solution)/shard_map/all_to_all | solution.py:297
  136.0 0.0 collective-permute-done.12
  136.0 0.0 collective-permute-done.11
  136.0 0.4 convolution_convert_fusion
  136.4 0.4 reshape.35
  136.8 0.2 copy.14
  137.0 0.0 copy-start.10
  137.0 0.0 copy-start.11
  137.0 0.1 slice_bitcast_fusion
  137.1 0.1 copy.21
  137.2 0.1 pad.clone
  137.3 0.6 copy-done.10
  137.9 0.0 copy-done.11
  137.9 0.8 fusion
  138.7 0.8 copy.19
  139.5 10.8 %all-to-all-done.1.landed = bf16[64,2,8,384]{3,2,1,0:T(8,128)(2,1)S(1)} async-done(((bf16[64,2,8,384]{3,2,1,0:T(8,128)(2,1)}), bf16[64,2,8,384]{3,2,1,0:T(8,128)(2,1)S(1)}, u32[]{:S(2)}, u32[]{:S(2)}) %all-to-all-start.1) | async-done | bytes 786464 | tf_op jit(solution)/shard_map/all_to_all | solution.py:297
  150.3 0.4 shard_map.121
  150.7 0.9 copy.25
  (24 shorter events, 0.3 us)
Async XLA Ops:
  0.6 135.3 %copy-start = (bf16[384,1536]{1,0:T(8,128)(2,1)S(1)}, bf16[384,1536]{1,0:T(8,128)(2,1)}, u32[]{:S(2)}) copy-start(bf16[384,1536]{1,0:T(8,128)(2,1)} %param.15) | copy-start | bytes 3538948
  0.6 28.5 %copy-start.5 = (bf16[3,3,384,384]{3,2,1,0:T(8,128)(2,1)S(1)}, bf16[3,3,384,384]{3,2,1,0:T(8,128)(2,1)}, u32[]{:S(2)}) copy-start(bf16[3,3,384,384]{3,2,1,0:T(8,128)(2,1)} %param.11) | copy-start | bytes 7962628
  0.7 1.3 copy-start.6
  29.1 9.5 %copy-start.7 = (s32[4]{0:T(128)S(1)}, s32[4]{0:T(128)}, u32[]{:S(2)}) copy-start(s32[4]{0:T(128)} %constant.38.clone) | copy-start | bytes 52
  29.1 9.5 %copy-start.8 = (s32[4]{0:T(128)S(1)}, s32[4]{0:T(128)}, u32[]{:S(2)}) copy-start(s32[4]{0:T(128)} %constant.40.clone) | copy-start | bytes 52
  29.1 9.5 %copy-start.9 = (s32[4]{0:T(128)S(1)}, s32[4]{0:T(128)}, u32[]{:S(2)}) copy-start(s32[4]{0:T(128)} %constant.39.clone) | copy-start | bytes 52
  33.1 13.1 %collective-permute-start = (bf16[512,384]{1,0:T(8,128)(2,1)S(1)}, bf16[512,384]{1,0:T(8,128)(2,1)S(1)}, u32[]{:S(2)}, u32[]{:S(2)}) collective-permute-start(bf16[512,384]{1,0:T(8,128)(2,1)S(1)} %get-tuple-element.11.hidden1), channel_id=1, source_target_pairs={{0,16},{16,32},{32,48},{48,64},{64,80},{80,96},{96,112},{112,8},{8... | collective-permute-start | bytes 1179656 | tf_op jit(solution)/shard_map/ppermute | solution.py:254
  33.7 12.5 %collective-permute-start.1 = (bf16[512,384]{1,0:T(8,128)(2,1)S(1)}, bf16[512,384]{1,0:T(8,128)(2,1)S(1)}, u32[]{:S(2)}, u32[]{:S(2)}) collective-permute-start(bf16[512,384]{1,0:T(8,128)(2,1)S(1)} %get-tuple-element.12.hidden0), channel_id=1, source_target_pairs={{0,120},{16,0},{32,16},{48,32},{64,48},{80,64},{96,80},{112,96},{8... | collective-permute-start | bytes 1179656 | tf_op jit(solution)/shard_map/ppermute | solution.py:255
  46.2 1.8 %copy-start.1 = (bf16[3,3,384,384]{3,2,1,0:T(8,128)(2,1)S(1)}, bf16[3,3,384,384]{3,2,1,0:T(8,128)(2,1)}, u32[]{:S(2)}) copy-start(bf16[3,3,384,384]{3,2,1,0:T(8,128)(2,1)} %kernel.5) | copy-start | bytes 7962628
  48.0 5.7 %copy-start.2 = (bf16[3,3,384,384]{3,2,1,0:T(8,128)(2,1)S(1)}, bf16[3,3,384,384]{3,2,1,0:T(8,128)(2,1)}, u32[]{:S(2)}) copy-start(bf16[3,3,384,384]{3,2,1,0:T(8,128)(2,1)} %kernel.5) | copy-start | bytes 7962628
  49.4 9.0 %collective-permute-start.2 = (bf16[2,128,384]{2,1,0:T(8,128)(2,1)S(1)}, bf16[2,128,384]{2,1,0:T(8,128)(2,1)S(1)}, u32[]{:S(2)}, u32[]{:S(2)}) collective-permute-start(bf16[2,128,384]{2,1,0:T(8,128)(2,1)S(1)} %get-tuple-element.13), channel_id=1, source_target_pairs={{0,1},{1,2},{2,3},{3,4},{4,5},{5,6},{6,7},{7,0},{8,9},{9,10},{10,1... | collective-permute-start | bytes 589832 | tf_op jit(solution)/shard_map/ppermute | solution.py:263
  50.1 9.1 %collective-permute-start.3 = (bf16[2,128,384]{2,1,0:T(8,128)(2,1)S(1)}, bf16[2,128,384]{2,1,0:T(8,128)(2,1)S(1)}, u32[]{:S(2)}, u32[]{:S(2)}) collective-permute-start(bf16[2,128,384]{2,1,0:T(8,128)(2,1)S(1)} %get-tuple-element.14), channel_id=1, source_target_pairs={{0,7},{1,0},{2,1},{3,2},{4,3},{5,4},{6,5},{7,6},{8,15},{9,8},{10,9... | collective-permute-start | bytes 589832 | tf_op jit(solution)/shard_map/ppermute | solution.py:264
  53.6 5.6 %copy-start.4 = (bf16[3,3,384,384]{3,2,1,0:T(8,128)(2,1)S(1)}, bf16[3,3,384,384]{3,2,1,0:T(8,128)(2,1)}, u32[]{:S(2)}) copy-start(bf16[3,3,384,384]{3,2,1,0:T(8,128)(2,1)} %param.13) | copy-start | bytes 7962628
  59.2 19.7 %copy-start.3 = (bf16[3,3,384,384]{3,2,1,0:T(8,128)(2,1)S(1)}, bf16[3,3,384,384]{3,2,1,0:T(8,128)(2,1)}, u32[]{:S(2)}) copy-start(bf16[3,3,384,384]{3,2,1,0:T(8,128)(2,1)} %kernel.7) | copy-start | bytes 7962628
  64.0 14.9 %collective-permute-start.4 = (bf16[512,384]{1,0:T(8,128)(2,1)S(1)}, bf16[512,384]{1,0:T(8,128)(2,1)S(1)}, u32[]{:S(2)}, u32[]{:S(2)}) collective-permute-start(bf16[512,384]{1,0:T(8,128)(2,1)S(1)} %get-tuple-element.15.hidden1), channel_id=1, source_target_pairs={{0,16},{16,32},{32,48},{48,64},{64,80},{80,96},{96,112},{112,8},{8... | collective-permute-start | bytes 1179656 | tf_op jit(solution)/shard_map/ppermute | solution.py:254
  64.1 14.8 %collective-permute-start.5 = (bf16[512,384]{1,0:T(8,128)(2,1)S(1)}, bf16[512,384]{1,0:T(8,128)(2,1)S(1)}, u32[]{:S(2)}, u32[]{:S(2)}) collective-permute-start(bf16[512,384]{1,0:T(8,128)(2,1)S(1)} %get-tuple-element.16.hidden0), channel_id=1, source_target_pairs={{0,120},{16,0},{32,16},{48,32},{64,48},{80,64},{96,80},{112,96},{8... | collective-permute-start | bytes 1179656 | tf_op jit(solution)/shard_map/ppermute | solution.py:255
  80.4 9.2 %collective-permute-start.6 = (bf16[2,128,384]{2,1,0:T(8,128)(2,1)S(1)}, bf16[2,128,384]{2,1,0:T(8,128)(2,1)S(1)}, u32[]{:S(2)}, u32[]{:S(2)}) collective-permute-start(bf16[2,128,384]{2,1,0:T(8,128)(2,1)S(1)} %get-tuple-element.18), channel_id=1, source_target_pairs={{0,1},{1,2},{2,3},{3,4},{4,5},{5,6},{6,7},{7,0},{8,9},{9,10},{10,1... | collective-permute-start | bytes 589832 | tf_op jit(solution)/shard_map/ppermute | solution.py:263
  80.5 11.7 %collective-permute-start.7 = (bf16[2,128,384]{2,1,0:T(8,128)(2,1)S(1)}, bf16[2,128,384]{2,1,0:T(8,128)(2,1)S(1)}, u32[]{:S(2)}, u32[]{:S(2)}) collective-permute-start(bf16[2,128,384]{2,1,0:T(8,128)(2,1)S(1)} %get-tuple-element.19), channel_id=1, source_target_pairs={{0,7},{1,0},{2,1},{3,2},{4,3},{5,4},{6,5},{7,6},{8,15},{9,8},{10,9... | collective-permute-start | bytes 589832 | tf_op jit(solution)/shard_map/ppermute | solution.py:264
  104.2 3.3 %collective-permute-start.8 = (bf16[1,16,384]{2,1,0:T(8,128)(2,1)S(1)}, bf16[1,16,384]{2,1,0:T(8,128)(2,1)S(1)}, u32[]{:S(2)}, u32[]{:S(2)}) collective-permute-start(bf16[1,16,384]{2,1,0:T(8,128)(2,1)S(1)} %get-tuple-element.25), channel_id=1, source_target_pairs={{0,8},{1,10},{2,12},{3,14},{4,9},{5,11},{6,13},{7,15},{8,40},{9,42... | collective-permute-start | bytes 36872 | tf_op jit(solution)/shard_map/ppermute | solution.py:235
  105.5 2.0 %collective-permute-start.9 = (bf16[4,16,384]{2,1,0:T(8,128)(2,1)S(1)}, bf16[4,16,384]{2,1,0:T(8,128)(2,1)S(1)}, u32[]{:S(2)}, u32[]{:S(2)}) collective-permute-start(bf16[4,16,384]{2,1,0:T(8,128)(2,1)S(1)} %reshape.34), channel_id=1, source_target_pairs={{0,0},{1,2},{2,4},{3,6},{4,1},{5,3},{6,5},{7,7},{8,32},{9,34},{10,... | collective-permute-start | bytes 147464 | tf_op jit(solution)/shard_map/ppermute | solution.py:237
  106.2 8.1 %collective-permute-start.10 = (bf16[1,16,384]{2,1,0:T(8,128)(2,1)S(1)}, bf16[1,16,384]{2,1,0:T(8,128)(2,1)S(1)}, u32[]{:S(2)}, u32[]{:S(2)}) collective-permute-start(bf16[1,16,384]{2,1,0:T(8,128)(2,1)S(1)} %get-tuple-element.24), channel_id=1, source_target_pairs={{8,24},{9,26},{10,28},{11,30},{12,25},{13,27},{14,29},{15,31},{16,... | collective-permute-start | bytes 36872 | tf_op jit(solution)/shard_map/ppermute | solution.py:236
  114.3 21.7 %collective-permute-start.12 = (bf16[6,1,384]{2,1,0:T(2,128)(2,1)S(1)}, bf16[6,1,384]{2,1,0:T(2,128)(2,1)S(1)}, u32[]{:S(2)}, u32[]{:S(2)}) collective-permute-start(bf16[6,1,384]{2,1,0:T(2,128)(2,1)S(1)} %get-tuple-element.23), channel_id=1, source_target_pairs={{1,0},{2,1},{3,2},{4,3},{5,4},{6,5},{7,6},{9,8},{10,9},{11,10},{12... | collective-permute-start | bytes 13832 | tf_op jit(solution)/shard_map/ppermute | solution.py:240
  115.6 20.4 %collective-permute-start.11 = (bf16[6,1,384]{2,1,0:T(2,128)(2,1)S(1)}, bf16[6,1,384]{2,1,0:T(2,128)(2,1)S(1)}, u32[]{:S(2)}, u32[]{:S(2)}) collective-permute-start(bf16[6,1,384]{2,1,0:T(2,128)(2,1)S(1)} %get-tuple-element.22), channel_id=1, source_target_pairs={{0,1},{1,2},{2,3},{3,4},{4,5},{5,6},{6,7},{8,9},{9,10},{10,11},{11... | collective-permute-start | bytes 13832 | tf_op jit(solution)/shard_map/ppermute | solution.py:239
  124.7 25.6 %all-to-all-start.1 = ((bf16[64,2,8,384]{3,2,1,0:T(8,128)(2,1)}), bf16[64,2,8,384]{3,2,1,0:T(8,128)(2,1)S(1)}, u32[]{:S(2)}, u32[]{:S(2)}) async-start(bf16[64,2,8,384]{3,2,1,0:T(8,128)(2,1)} %shard_map.120), calls=%async_computation.1 | async-start | bytes 1572864 | tf_op jit(solution)/shard_map/all_to_all | solution.py:297
  137.0 0.9 copy-start.10
  137.0 0.9 copy-start.11

commit v3 on v2

--- a/solution.py
+++ b/solution.py
@@ -33,24 +33,51 @@
     return run
 
 
-def device_of_band(band):
-    core, rest = divmod(band, 8)
-    return rest * 2 + core
-
-
-def band_route(step):
-    return [(device_of_band(b), device_of_band((b + step) % 16)) for b in range(16)]
-
-
-def ring_route(step):
-    return [(i, (i + step) % 8) for i in range(8)]
+def chip(core, band, ring):
+    turn = (band + 1) % 8
+    y, side = divmod(turn, 2)
+    z = (side + y) % 2
+    if ring < 4:
+        return ring, y, core + z
+    return 7 - ring, (y + 1) % 4, (3 + core - z) % 4
+
+
+def slot(core, band, ring):
+    x, y, z = chip(core, band, ring)
+    return (((z // 2) * 4 + y) * 4 + x) * 2 + z % 2
+
+
+def device(core, band, ring):
+    x, y, z = chip(core, band, ring)
+    return ((((z // 2) * 4 + y) * 2 + core) * 4 + x) * 2 + z % 2
+
+
+BLOCKS = [(core, band, ring) for core in range(2) for band in range(8) for ring in range(8)]
+
+
+def block_route(row_step, column_step):
+    route = []
+    for core, band, ring in BLOCKS:
+        row = (8 * core + band + row_step) % 16
+        target = device(row // 8, row % 8, (ring + column_step) % 8)
+        route.append((device(core, band, ring), target))
+    return route
+
+
+def notes():
+    table = [None] * 128
+    for core, band, ring in BLOCKS:
+        slots = [slot(core, other // 8, other % 8) for other in range(64)]
+        row = 8 * core + band
+        table[device(core, band, ring)] = slots + [row == 0, row == 15, ring == 0, ring == 7]
+    return jnp.array(table, jnp.int32)
 
 
 def line_route(count, step):
     return [(i, i + step) for i in range(count) if 0 <= i + step < count]
 
 
-def gather_body(context, sent):
+def gather_body(notes, context, sent):
     channels = context.shape[-1]
     first = lax.broadcasted_iota(jnp.int32, (4, 8, channels), 1) < 4
 
@@ -62,22 +89,22 @@
         odd = jnp.where(first, pltpu.roll(low, 4, 1), high)
         for pair in range(4):
             place = 8 * (row // 2) + 2 * pair
-            sent[place, row % 2] = even[pair].astype(BF16)
-            sent[place + 1, row % 2] = odd[pair].astype(BF16)
+            sent[notes[place], row % 2] = even[pair].astype(BF16)
+            sent[notes[place + 1], row % 2] = odd[pair].astype(BF16)
         return carry
 
     lax.fori_loop(0, 16, step, 0)
 
 
-def scatter_body(landed, result):
+def scatter_body(notes, landed, result):
     channels = result.shape[-1]
     first = lax.broadcasted_iota(jnp.int32, (8, channels), 0) < 4
 
     def step(row, carry):
         for pair in range(4):
             place = 8 * (row // 2) + 2 * pair
-            even = landed[place, row % 2].astype(F32)
-            odd = landed[place + 1, row % 2].astype(F32)
+            even = landed[notes[place], row % 2].astype(F32)
+            odd = landed[notes[place + 1], row % 2].astype(F32)
             low = jnp.where(first, even, pltpu.roll(odd, 4, 0))
             high = jnp.where(first, pltpu.roll(even, 4, 0), odd)
             result[row, 8 * pair : 8 * pair + 8] = low.astype(BF16)
@@ -117,15 +144,15 @@
         dilated_band(cells, kernel, hidden, shelves, 1)
 
 
-def settle(partial, sums, from_left, from_right, ends, i0, channels):
+def settle(partial, sums, from_left, from_right, notes, i0, channels):
     place = lax.broadcasted_iota(jnp.int32, (128, channels), 0) % 16
     left = from_left[i0].astype(F32)
     right = from_right[i0].astype(F32)
     left = jnp.where(
-        ends[2] == 1, jnp.where(place == 0, 0.0, pltpu.roll(left, 1, 0)), left
+        notes[66] == 1, jnp.where(place == 0, 0.0, pltpu.roll(left, 1, 0)), left
     )
     right = jnp.where(
-        ends[3] == 1, jnp.where(place == 15, 0.0, pltpu.roll(right, 127, 0)), right
+        notes[67] == 1, jnp.where(place == 15, 0.0, pltpu.roll(right, 127, 0)), right
     )
     pieces = []
     for lane in range(0, channels, 128):
@@ -137,31 +164,38 @@
     return jnp.concatenate(pieces, 1)
 
 
-def second_dilated_body(ends, partial, from_left, from_right, kernel, state, hidden0, hidden1, sums, shelves):
+def second_dilated_body(notes, partial, from_left, from_right, kernel, state, hidden0, hidden1, sums, shelves):
     channels = state.shape[-1]
     for i0, hidden in enumerate((hidden0, hidden1)):
-        cells = settle(partial, sums, from_left, from_right, ends, i0, channels)
+        cells = settle(partial, sums, from_left, from_right, notes, i0, channels)
         state[:, i0] = cells.reshape(64, 8, channels)
         dilated_band(cells.astype(F32).reshape(8, 64, channels), kernel, hidden, shelves, 2)
 
 
-def final_body(ends, partial, from_left, from_right, state, sums):
+def final_body(notes, partial, from_left, from_right, state, crop, sums):
     channels = state.shape[-1]
     for i0 in range(2):
-        cells = settle(partial, sums, from_left, from_right, ends, i0, channels)
+        cells = settle(partial, sums, from_left, from_right, notes, i0, channels)
         state[:, i0] = cells.reshape(64, 8, channels)
-
-
-def edge_body(ends, up, down, hidden0, hidden1, kernel, to_left, to_right, above, below, wide):
+    first = lax.broadcasted_iota(jnp.int32, (8, channels), 0) < 4
+    for pair in range(4):
+        place = 8 * (4 + pair // 2) + 4 + pair % 2
+        top = state[place, 0].astype(F32)
+        bottom = state[place, 1].astype(F32)
+        crop[2 * pair] = jnp.where(first, top, pltpu.roll(bottom, 4, 0)).astype(BF16)
+        crop[2 * pair + 1] = jnp.where(first, pltpu.roll(top, 4, 0), bottom).astype(BF16)
+
+
+def edge_body(notes, up, down, hidden0, hidden1, kernel, to_left, to_right, above, below, wide):
     channels = up.shape[-1]
     blank = jnp.zeros((64, channels), BF16)
     above[:64] = blank
     above[64:] = up[...]
     below[:512] = down[...]
     below[512:] = blank
-    start = pl.multiple_of(64 - 64 * ends[0], 64)
+    start = pl.multiple_of(64 - 64 * notes[64], 64)
     lines = [above[pl.ds(start, 512)], hidden0[...], hidden1[...]]
-    start = pl.multiple_of(64 * ends[1], 64)
+    start = pl.multiple_of(64 * notes[65], 64)
     lines.append(below[pl.ds(start, 512)])
     for index, line in enumerate(lines):
         for lane in range(0, channels, 128):
@@ -186,15 +220,15 @@
         sums[1] = product[128:]
 
 
-def plain_body(ends, up, down, hidden0, hidden1, state, kernel, partial, above, below):
+def plain_body(notes, up, down, hidden0, hidden1, state, kernel, partial, above, below):
     channels = up.shape[-1]
     blank = jnp.zeros((64, channels), BF16)
     above[:64] = blank
     above[64:] = up[...]
     below[:512] = down[...]
     below[512:] = blank
-    over = above[pl.ds(pl.multiple_of(64 - 64 * ends[0], 64), 512)]
-    under = below[pl.ds(pl.multiple_of(64 * ends[1], 64), 512)]
+    over = above[pl.ds(pl.multiple_of(64 - 64 * notes[64], 64), 512)]
+    under = below[pl.ds(pl.multiple_of(64 * notes[65], 64), 512)]
     lines = (over, hidden0[...], hidden1[...], under)
     place = lax.broadcasted_iota(jnp.int32, (512, channels), 0) % 4
     for i0 in range(2):
@@ -211,20 +245,28 @@
 
 def crop_route(shift):
     route = []
-    for bits in range(128):
-        i3, i2, i5, i4, j4, j6, j5 = ((bits >> k) & 1 for k in range(6, -1, -1))
-        row = 8 * i5 + 4 * i4 + 2 * i3 + i2 + shift
-        column = 4 * j6 + 2 * j5 + j4
-        if 0 <= row < 16:
-            route.append((bits, row * 8 + column))
+    for row in range(16):
+        for column in range(8):
+            i5, i4, i32 = row // 8, row // 4 % 2, row % 4
+            source = device(i4, 2 * i32 + i5, 4 * (column % 2) + column // 2)
+            if 0 <= row + shift < 16:
+                route.append((source, (row + shift) * 8 + column))
     return route
 
 
-def crop_cells(state):
-    channels = state.shape[-1]
-    crop = state.reshape(8, 8, 2, 2, 4, channels)[4:6, 4:6].transpose(0, 1, 3, 2, 4, 5)
+def crop_groups():
+    return [
+        [device(core, 2 * rows + i1, 4 * j4 + j32) for i1 in range(2) for j32 in range(4)]
+        for core in range(2)
+        for rows in range(4)
+        for j4 in range(2)
+    ]
+
+
+def crop_cells(crop):
+    channels = crop.shape[-1]
     crop = lax.all_to_all(
-        crop.reshape(8, 8, channels), ("y0", "x0", "zl"), 0, 0, tiled=True
+        crop, AXES, 0, 0, axis_index_groups=crop_groups(), tiled=True
     )
     crop = crop.reshape(2, 4, 2, 4, channels).transpose(0, 2, 1, 3, 4)
     return crop.reshape(4, 16, channels)
@@ -249,21 +291,21 @@
     return target[0].astype(BF16)
 
 
-def plain(hidden0, hidden1, state, kernel, ends):
+def plain(hidden0, hidden1, state, kernel, own):
     channels = hidden0.shape[-1]
-    up = lax.ppermute(hidden1, ROW, band_route(1))
-    down = lax.ppermute(hidden0, ROW, band_route(-1))
+    up = lax.ppermute(hidden1, AXES, block_route(1, 0))
+    down = lax.ppermute(hidden0, AXES, block_route(-1, 0))
     padded = [((576, channels), BF16)] * 2
     to_left, to_right = kernel_call(
         edge_body,
         [((2, 128, channels), BF16)] * 2,
         padded + [((4, 3, 512, 128), F32)],
         5, 1,
-    )(ends, up, down, hidden0, hidden1, kernel)
-    from_left = lax.ppermute(to_right, COL, ring_route(1))
-    from_right = lax.ppermute(to_left, COL, ring_route(-1))
+    )(own, up, down, hidden0, hidden1, kernel)
+    from_left = lax.ppermute(to_right, AXES, block_route(0, 1))
+    from_right = lax.ppermute(to_left, AXES, block_route(0, -1))
     (partial,) = kernel_call(plain_body, [((2, 512, channels), F32)], padded, 6, 1)(
-        ends, up, down, hidden0, hidden1, state, kernel
+        own, up, down, hidden0, hidden1, state, kernel
     )
     return partial, from_left, from_right
 
@@ -271,32 +313,29 @@
 def shards(context, first_dilated_weight, first_plain_weight, second_dilated_weight,
            second_plain_weight, lift_weight, fine_weight):
     channels = context.shape[-1]
-    band = 8 * lax.axis_index("core") + lax.axis_index(("zh", "y1", "y0"))
-    ring = lax.axis_index(COL)
-    ends = jnp.array([0, 15, 0, 7]) == jnp.array([1, 1, 0, 0]) * band + jnp.array([0, 0, 1, 1]) * ring
-    ends = ends.astype(jnp.int32)
+    own = notes()[lax.axis_index(AXES)]
     spread = (64, 2, 8, channels)
     band_shape = ((512, channels), BF16)
-    (sent,) = kernel_call(gather_body, [(spread, BF16)], (), 1)(context)
+    (sent,) = kernel_call(gather_body, [(spread, BF16)], (), 1, 1)(own, context)
     state = lax.all_to_all(sent, SPREAD, 0, 0, tiled=True)
     hidden0, hidden1 = kernel_call(
         first_dilated_body, [band_shape] * 2, [((3, 10, 64, channels), BF16)], 2
     )(state, first_dilated_weight.reshape(9 * channels, channels))
-    edges = plain(hidden0, hidden1, state, first_plain_weight, ends)
+    edges = plain(hidden0, hidden1, state, first_plain_weight, own)
     state, hidden0, hidden1 = kernel_call(
         second_dilated_body,
         [(spread, BF16), band_shape, band_shape],
         [((2, 3, 512, 128), F32), ((3, 12, 64, channels), BF16)],
         4, 1,
-    )(ends, *edges, second_dilated_weight.reshape(9 * channels, channels))
-    edges = plain(hidden0, hidden1, state, second_plain_weight, ends)
-    (state,) = kernel_call(
-        final_body, [(spread, BF16)], [((2, 3, 512, 128), F32)], 3, 1
-    )(ends, *edges)
-    crop = crop_cells(state)
+    )(own, *edges, second_dilated_weight.reshape(9 * channels, channels))
+    edges = plain(hidden0, hidden1, state, second_plain_weight, own)
+    state, crop = kernel_call(
+        final_body, [(spread, BF16), ((8, 8, channels), BF16)], [((2, 3, 512, 128), F32)], 3, 1
+    )(own, *edges)
+    crop = crop_cells(crop)
     landed = lax.all_to_all(state, SPREAD, 0, 0, tiled=True)
     target = fine_target(crop, lift_weight, fine_weight)
-    (result,) = kernel_call(scatter_body, [((16, 64, channels), BF16)], (), 1)(landed)
+    (result,) = kernel_call(scatter_body, [((16, 64, channels), BF16)], (), 1, 1)(own, landed)
     return result, target
 
 

time: 152 us -> 140 us (0.921)
  waiting for transfers between devices: 38.2 us -> 31.9 us
  starting transfers between devices: 44.2 us -> 38.9 us
  local copies, waits for them, and re-layouts: 8.04 us -> 5.2 us
    all_to_all x1, starting transfers between devices: 11.2 us -> 6.13 us  [shards(): landed = lax.all_to_all(state, SPREAD, 0, 0, tiled=True)]
    ppermute x1, waiting for transfers between devices: 6.73 us -> 2.33 us  [fine_target(): high = lax.ppermute(crop[:1], AXES, crop_route(-1))]
    ppermute x8, starting transfers between devices: 19.3 us -> 15 us  [the longest x2 7.55 us: plain(): from_right = lax.ppermute(to_left, AXES, block_route(0, -1))]
    ppermute x1, starting transfers between devices: 1.29 us -> 4.69 us  [fine_target(): low = lax.ppermute(crop[3:], AXES, crop_route(1))]
    ppermute x8, waiting for transfers between devices: 20.7 us -> 18 us  [the longest x2 11.5 us: plain(): up = lax.ppermute(hidden1, AXES, block_route(1, 0))]
    ppermute x1, waiting for transfers between devices: 0.01 us -> 2.13 us  [fine_target(): crop = lax.ppermute(crop, AXES, crop_route(0))]
    unnamed x29 -> x21, local copies, waits for them, and re-layouts: 5.37 us -> 3.46 us
    reshape x2 -> x0, local copies, waits for them, and re-layouts: 1.7 us -> none  [the longest x1 1.68 us: crop_cells(): state.reshape(8, 8, 2, 2, 4, channels)[4:6, 4:6].transpose(0, 1, 3, 2, 4, 5)]
  transfers between devices with their start and end apart: 14 -> 14, of which waited for: 7 -> 7; matrix products, arithmetic and copies ran while one was open for 2% -> 2% of each run, Pallas kernels for 6% -> 7%
where the time goes in v3:
time: 140 us
  starting transfers between devices  38.9 us (28%)
  blocking collectives  36.8 us (26%)
  waiting for transfers between devices  31.9 us (23%)
  Pallas kernels  25 us (18%)
  local copies, waits for them, and re-layouts  5.2 us (4%)
    all_to_all x1, blocking collectives, shards(): state = lax.all_to_all(sent, SPREAD, 0, 0, tiled=True)  26.9 us
    pallas_call x9, Pallas kernels, run(): return call(*operands[:scalars], *near)  25 us
    ppermute x2, waiting for transfers between devices, plain(): up = lax.ppermute(hidden1, AXES, block_route(1, 0))  11.5 us
    all_to_all x1, blocking collectives, crop_cells(): lax.all_to_all(crop, AXES, 0, 0, axis_index_groups=crop_groups(), tiled=T...  9.87 us
    ppermute x1, starting transfers between devices, fine_target(): low = lax.ppermute(crop[:, 15:], COL, line_route(8, 1))  9.72 us
    all_to_all x1, waiting for transfers between devices, shards(): landed = lax.all_to_all(state, SPREAD, 0, 0, tiled=True)  9.47 us
    ppermute x2, starting transfers between devices, plain(): from_right = lax.ppermute(to_left, AXES, block_route(0, -1))  7.55 us
    ppermute x2, waiting for transfers between devices, plain(): down = lax.ppermute(hidden0, AXES, block_route(-1, 0))  6.46 us
  transfers between devices with their start and end apart: 14, of which 7 were waited for; matrix products, arithmetic and copies ran while one was open for 2% of the time, Pallas kernels for 7%

profile of v3, /device:TPU:0, one launch (start us, length us, event | category | flops | bytes accessed | tf_op | source)
XLA Modules:
  0.0 139.9 jit_solution(16584359262944110362)
XLA Ops:
  0.6 0.0 copy-start
  0.7 0.8 dynamic-slice_bitcast_fusion.notes
  1.5 0.0 copy-start.5
  1.5 1.1 copy-done.5
  2.6 0.0 copy-start.4
  2.6 0.9 shard_map.95
  3.5 26.9 %all_to_all.15.landed.state = bf16[64,2,8,384]{3,2,1,0:T(8,128)(2,1)S(1)} all-to-all(bf16[64,2,8,384]{3,2,1,0:T(8,128)(2,1)S(1)} %shard_map.95), channel_id=1, replica_groups=mesh['zh'=2,'y1'=2,'y0'=2,'core'=2,'x1'=2,'x0'=2,'zl'=2] {'zh','y1','y0'..., dimensions={0} | all-to-all | bytes 1572864 | tf_op jit(solution)/shard_map/all_to_all | solution.py:320
  30.4 0.0 copy-done.4
  30.4 4.0 %shard_map.96 = (bf16[512,384]{1,0:T(8,128)(2,1)S(1)}, bf16[512,384]{1,0:T(8,128)(2,1)S(1)}) custom-call(bf16[64,2,8,384]{3,2,1,0:T(8,128)(2,1)S(1)} %all_to_all.15.landed.state, bf16[3456,384]{1,0:T(8,128)(2,1)S(1)} %bitcast.22), custom_call_target="tpu_custom_call" | custom-call | tf_op jit(solution)/shard_map/pallas_call | solution.py:31
  34.5 0.1 collective-permute-start
  34.6 3.2 %collective-permute-start.1 = (bf16[512,384]{1,0:T(8,128)(2,1)S(1)}, bf16[512,384]{1,0:T(8,128)(2,1)S(1)}, u32[]{:S(2)}, u32[]{:S(2)}) collective-permute-start(bf16[512,384]{1,0:T(8,128)(2,1)S(1)} %get-tuple-element.14.hidden0), channel_id=1, source_target_pairs={{1,9},{3,11},{5,13},{7,15},{86,30},{84,28},{82,26},{80,24},{17,1},... | collective-permute-start | bytes 1179656 | tf_op jit(solution)/shard_map/ppermute | solution.py:297
  37.8 5.8 %collective-permute-done.up = bf16[512,384]{1,0:T(8,128)(2,1)S(1)} collective-permute-done((bf16[512,384]{1,0:T(8,128)(2,1)S(1)}, bf16[512,384]{1,0:T(8,128)(2,1)S(1)}, u32[]{:S(2)}, u32[]{:S(2)}) %collective-permute-start) | collective-permute-done | bytes 393248 | tf_op jit(solution)/shard_map/ppermute | solution.py:296
  43.5 3.4 %collective-permute-done.1.down = bf16[512,384]{1,0:T(8,128)(2,1)S(1)} collective-permute-done((bf16[512,384]{1,0:T(8,128)(2,1)S(1)}, bf16[512,384]{1,0:T(8,128)(2,1)S(1)}, u32[]{:S(2)}, u32[]{:S(2)}) %collective-permute-start.1) | collective-permute-done | bytes 393248 | tf_op jit(solution)/shard_map/ppermute | solution.py:297
  46.9 0.0 copy-done.1
  46.9 1.4 %shard_map.98 = (bf16[2,128,384]{2,1,0:T(8,128)(2,1)S(1)}, bf16[2,128,384]{2,1,0:T(8,128)(2,1)S(1)}) custom-call(s32[68]{0:T(128)S(1)} %dynamic-slice_bitcast_fusion.notes, bf16[512,384]{1,0:T(8,128)(2,1)S(1)} %collective-permute-done.up, bf16[512,384]{1,0:T(8,128)(2,1)S(1)} %collective-permute-done.1.down, bf16[512,384]{1,0:T(8,128)(2,1)S(1)} %get-tuple-element.14.hidden0, ...), custom_call_target="tpu_custom_call" | custom-call | tf_op jit(solution)/shard_map/pallas_call | solution.py:31
  48.4 0.8 collective-permute-start.2
  49.1 3.4 %collective-permute-start.3 = (bf16[2,128,384]{2,1,0:T(8,128)(2,1)S(1)}, bf16[2,128,384]{2,1,0:T(8,128)(2,1)S(1)}, u32[]{:S(2)}, u32[]{:S(2)}) collective-permute-start(bf16[2,128,384]{2,1,0:T(8,128)(2,1)S(1)} %get-tuple-element.16), channel_id=1, source_target_pairs={{1,80},{3,1},{5,3},{7,5},{86,7},{84,86},{82,84},{80,82},{17,96},{1... | collective-permute-start | bytes 589832 | tf_op jit(solution)/shard_map/ppermute | solution.py:306
  52.6 0.0 copy-start.3
  52.6 4.8 %shard_map.97.partial = f32[2,512,384]{2,1,0:T(8,128)S(1)} custom-call(s32[68]{0:T(128)S(1)} %dynamic-slice_bitcast_fusion.notes, bf16[512,384]{1,0:T(8,128)(2,1)S(1)} %collective-permute-done.up, bf16[512,384]{1,0:T(8,128)(2,1)S(1)} %collective-permute-done.1.down, bf16[512,384]{1,0:T(8,128)(2,1)S(1)} %get-tuple-element.14.hidden0, ...), custom_call_target="tpu_custom_call" | custom-call | tf_op jit(solution)/shard_map/pallas_call | solution.py:31
  57.4 0.0 collective-permute-done.2.from_left
  57.4 0.0 collective-permute-done.3.from_right
  57.4 0.0 copy-done.3
  57.4 0.0 copy-start.2
  57.4 4.8 %shard_map.99 = (bf16[64,2,8,384]{3,2,1,0:T(8,128)(2,1)S(1)}, bf16[512,384]{1,0:T(8,128)(2,1)S(1)}, bf16[512,384]{1,0:T(8,128)(2,1)S(1)}) custom-call(s32[68]{0:T(128)S(1)} %dynamic-slice_bitcast_fusion.notes, f32[2,512,384]{2,1,0:T(8,128)S(1)} %shard_map.97.partial, bf16[2,128,384]{2,1,0:T(8,128)(2,1)S(1)} %collective-permute-done.2.from_left, ...), custom_call_target="tpu_custom_call" | custom-call | tf_op jit(solution)/shard_map/pallas_call | solution.py:31
  62.2 0.1 collective-permute-start.4
  62.3 3.2 %collective-permute-start.5 = (bf16[512,384]{1,0:T(8,128)(2,1)S(1)}, bf16[512,384]{1,0:T(8,128)(2,1)S(1)}, u32[]{:S(2)}, u32[]{:S(2)}) collective-permute-start(bf16[512,384]{1,0:T(8,128)(2,1)S(1)} %get-tuple-element.18.hidden0), channel_id=1, source_target_pairs={{1,9},{3,11},{5,13},{7,15},{86,30},{84,28},{82,26},{80,24},{17,1},... | collective-permute-start | bytes 1179656 | tf_op jit(solution)/shard_map/ppermute | solution.py:297
  65.5 5.8 %collective-permute-done.4.up = bf16[512,384]{1,0:T(8,128)(2,1)S(1)} collective-permute-done((bf16[512,384]{1,0:T(8,128)(2,1)S(1)}, bf16[512,384]{1,0:T(8,128)(2,1)S(1)}, u32[]{:S(2)}, u32[]{:S(2)}) %collective-permute-start.4) | collective-permute-done | bytes 393248 | tf_op jit(solution)/shard_map/ppermute | solution.py:296
  71.3 3.1 %collective-permute-done.5.down = bf16[512,384]{1,0:T(8,128)(2,1)S(1)} collective-permute-done((bf16[512,384]{1,0:T(8,128)(2,1)S(1)}, bf16[512,384]{1,0:T(8,128)(2,1)S(1)}, u32[]{:S(2)}, u32[]{:S(2)}) %collective-permute-start.5) | collective-permute-done | bytes 393248 | tf_op jit(solution)/shard_map/ppermute | solution.py:297
  74.3 0.0 copy-done.2
  74.4 1.4 %shard_map.101 = (bf16[2,128,384]{2,1,0:T(8,128)(2,1)S(1)}, bf16[2,128,384]{2,1,0:T(8,128)(2,1)S(1)}) custom-call(s32[68]{0:T(128)S(1)} %dynamic-slice_bitcast_fusion.notes, bf16[512,384]{1,0:T(8,128)(2,1)S(1)} %collective-permute-done.4.up, bf16[512,384]{1,0:T(8,128)(2,1)S(1)} %collective-permute-done.5.down, ...), custom_call_target="tpu_custom_call" | custom-call | tf_op jit(solution)/shard_map/pallas_call | solution.py:31
  75.8 0.1 collective-permute-start.6
  75.9 4.1 %collective-permute-start.7 = (bf16[2,128,384]{2,1,0:T(8,128)(2,1)S(1)}, bf16[2,128,384]{2,1,0:T(8,128)(2,1)S(1)}, u32[]{:S(2)}, u32[]{:S(2)}) collective-permute-start(bf16[2,128,384]{2,1,0:T(8,128)(2,1)S(1)} %get-tuple-element.21), channel_id=1, source_target_pairs={{1,80},{3,1},{5,3},{7,5},{86,7},{84,86},{82,84},{80,82},{17,96},{1... | collective-permute-start | bytes 589832 | tf_op jit(solution)/shard_map/ppermute | solution.py:306
  80.0 4.8 %shard_map.100.partial = f32[2,512,384]{2,1,0:T(8,128)S(1)} custom-call(s32[68]{0:T(128)S(1)} %dynamic-slice_bitcast_fusion.notes, bf16[512,384]{1,0:T(8,128)(2,1)S(1)} %collective-permute-done.4.up, bf16[512,384]{1,0:T(8,128)(2,1)S(1)} %collective-permute-done.5.down, bf16[512,384]{1,0:T(8,128)(2,1)S(1)} %get-tuple-element.18.hidden0, ...), custom_call_target="tpu_custom_call" | custom-call | tf_op jit(solution)/shard_map/pallas_call | solution.py:31
  84.8 0.0 collective-permute-done.6.from_left
  84.8 0.0 collective-permute-done.7.from_right
  84.8 1.8 %shard_map.102 = (bf16[64,2,8,384]{3,2,1,0:T(8,128)(2,1)}, bf16[8,8,384]{2,1,0:T(8,128)(2,1)S(1)}) custom-call(s32[68]{0:T(128)S(1)} %dynamic-slice_bitcast_fusion.notes, f32[2,512,384]{2,1,0:T(8,128)S(1)} %shard_map.100.partial, bf16[2,128,384]{2,1,0:T(8,128)(2,1)S(1)} %collective-permute-done.6.from_left, ...), custom_call_target="tpu_custom_call" | custom-call | tf_op jit(solution)/shard_map/pallas_call | solution.py:31
  86.7 9.9 %all_to_all.16 = bf16[8,8,384]{2,1,0:T(8,128)(2,1)S(1)} all-to-all(bf16[8,8,384]{2,1,0:T(8,128)(2,1)S(1)} %get-tuple-element.23), channel_id=1, replica_groups={{1,3,5,7,17,19,21,23},{86,84,82,80,102,100,98,96},{16,18,20,22,32,34,36..., dimensions={0} | all-to-all | bytes 98304 | tf_op jit(solution)/shard_map/all_to_all | solution.py:268
  96.6 4.7 %collective-permute-start.8 = (bf16[1,16,384]{2,1,0:T(8,128)(2,1)S(1)}, bf16[1,16,384]{2,1,0:T(8,128)(2,1)S(1)}, u32[]{:S(2)}, u32[]{:S(2)}) collective-permute-start(bf16[1,16,384]{2,1,0:T(8,128)(2,1)S(1)} %get-tuple-element.29), channel_id=1, source_target_pairs={{1,8},{86,9},{3,10},{84,11},{5,12},{82,13},{7,14},{80,15},{16,16},... | collective-permute-start | bytes 36872 | tf_op jit(solution)/shard_map/ppermute | solution.py:277
  101.3 0.1 collective-permute-start.9
  101.4 1.9 %collective-permute-start.10 = (bf16[1,16,384]{2,1,0:T(8,128)(2,1)S(1)}, bf16[1,16,384]{2,1,0:T(8,128)(2,1)S(1)}, u32[]{:S(2)}, u32[]{:S(2)}) collective-permute-start(bf16[1,16,384]{2,1,0:T(8,128)(2,1)S(1)} %get-tuple-element.28), channel_id=1, source_target_pairs={{16,0},{103,1},{18,2},{101,3},{20,4},{99,5},{22,6},{97,7},{33,8},{... | collective-permute-start | bytes 36872 | tf_op jit(solution)/shard_map/ppermute | solution.py:278
  103.3 0.0 collective-permute-done.8
  103.3 2.1 %collective-permute-done.9 = bf16[4,16,384]{2,1,0:T(8,128)(2,1)S(1)} collective-permute-done((bf16[4,16,384]{2,1,0:T(8,128)(2,1)S(1)}, bf16[4,16,384]{2,1,0:T(8,128)(2,1)S(1)}, u32[]{:S(2)}, u32[]{:S(2)}) %collective-permute-start.9) | collective-permute-done | bytes 49184 | tf_op jit(solution)/shard_map/ppermute | solution.py:279
  105.5 2.3 %collective-permute-done.10 = bf16[1,16,384]{2,1,0:T(8,128)(2,1)S(1)} collective-permute-done((bf16[1,16,384]{2,1,0:T(8,128)(2,1)S(1)}, bf16[1,16,384]{2,1,0:T(8,128)(2,1)S(1)}, u32[]{:S(2)}, u32[]{:S(2)}) %collective-permute-start.10) | collective-permute-done | bytes 12320 | tf_op jit(solution)/shard_map/ppermute | solution.py:278
  107.8 1.3 collective-permute-start.12
  109.1 9.7 %collective-permute-start.11 = (bf16[6,1,384]{2,1,0:T(2,128)(2,1)S(1)}, bf16[6,1,384]{2,1,0:T(2,128)(2,1)S(1)}, u32[]{:S(2)}, u32[]{:S(2)}) collective-permute-start(bf16[6,1,384]{2,1,0:T(2,128)(2,1)S(1)} %get-tuple-element.26), channel_id=1, source_target_pairs={{0,1},{1,2},{2,3},{3,4},{4,5},{5,6},{6,7},{8,9},{9,10},{10,11},{11... | collective-permute-start | bytes 13832 | tf_op jit(solution)/shard_map/ppermute | solution.py:281
  118.9 6.1 %all-to-all-start.1 = ((bf16[64,2,8,384]{3,2,1,0:T(8,128)(2,1)}), bf16[64,2,8,384]{3,2,1,0:T(8,128)(2,1)S(1)}, u32[]{:S(2)}, u32[]{:S(2)}) async-start(bf16[64,2,8,384]{3,2,1,0:T(8,128)(2,1)} %get-tuple-element.22), calls=%async_computation.1 | async-start | bytes 1572864 | tf_op jit(solution)/shard_map/all_to_all | solution.py:336
  125.0 0.0 collective-permute-done.12
  125.0 0.0 collective-permute-done.11
  125.0 0.0 copy-done
  125.0 0.4 convolution_convert_fusion
  125.5 0.4 reshape.27
  125.9 0.2 copy.12
  126.0 0.0 copy-start.6
  126.0 0.0 copy-start.7
  126.0 0.1 slice_bitcast_fusion
  126.1 0.1 copy.18
  126.2 0.1 pad.clone
  126.4 0.6 copy-done.6
  127.0 0.0 copy-done.7
  127.0 0.8 fusion
  127.8 0.8 copy.17
  128.6 9.5 %all-to-all-done.1.landed = bf16[64,2,8,384]{3,2,1,0:T(8,128)(2,1)S(1)} async-done(((bf16[64,2,8,384]{3,2,1,0:T(8,128)(2,1)}), bf16[64,2,8,384]{3,2,1,0:T(8,128)(2,1)S(1)}, u32[]{:S(2)}, u32[]{:S(2)}) %all-to-all-start.1) | async-done | bytes 786464 | tf_op jit(solution)/shard_map/all_to_all | solution.py:336
  138.0 1.0 shard_map.103
  139.0 0.9 copy.21
  (13 shorter events, 0.2 us)
Async XLA Ops:
  0.6 124.4 %copy-start = (bf16[384,1536]{1,0:T(8,128)(2,1)S(1)}, bf16[384,1536]{1,0:T(8,128)(2,1)}, u32[]{:S(2)}) copy-start(bf16[384,1536]{1,0:T(8,128)(2,1)} %param.13) | copy-start | bytes 3538948
  1.5 1.1 copy-start.5
  2.6 27.8 %copy-start.4 = (bf16[3,3,384,384]{3,2,1,0:T(8,128)(2,1)S(1)}, bf16[3,3,384,384]{3,2,1,0:T(8,128)(2,1)}, u32[]{:S(2)}) copy-start(bf16[3,3,384,384]{3,2,1,0:T(8,128)(2,1)} %param.9) | copy-start | bytes 7962628
  30.4 16.5 %copy-start.1 = (bf16[3,3,384,384]{3,2,1,0:T(8,128)(2,1)S(1)}, bf16[3,3,384,384]{3,2,1,0:T(8,128)(2,1)}, u32[]{:S(2)}) copy-start(bf16[3,3,384,384]{3,2,1,0:T(8,128)(2,1)} %kernel.5) | copy-start | bytes 7962628
  34.5 9.1 %collective-permute-start = (bf16[512,384]{1,0:T(8,128)(2,1)S(1)}, bf16[512,384]{1,0:T(8,128)(2,1)S(1)}, u32[]{:S(2)}, u32[]{:S(2)}) collective-permute-start(bf16[512,384]{1,0:T(8,128)(2,1)S(1)} %get-tuple-element.13.hidden1), channel_id=1, source_target_pairs={{1,17},{3,19},{5,21},{7,23},{86,102},{84,100},{82,98},{80,96},{17,... | collective-permute-start | bytes 1179656 | tf_op jit(solution)/shard_map/ppermute | solution.py:296
  34.6 12.4 %collective-permute-start.1 = (bf16[512,384]{1,0:T(8,128)(2,1)S(1)}, bf16[512,384]{1,0:T(8,128)(2,1)S(1)}, u32[]{:S(2)}, u32[]{:S(2)}) collective-permute-start(bf16[512,384]{1,0:T(8,128)(2,1)S(1)} %get-tuple-element.14.hidden0), channel_id=1, source_target_pairs={{1,9},{3,11},{5,13},{7,15},{86,30},{84,28},{82,26},{80,24},{17,1},... | collective-permute-start | bytes 1179656 | tf_op jit(solution)/shard_map/ppermute | solution.py:297
  48.4 9.0 %collective-permute-start.2 = (bf16[2,128,384]{2,1,0:T(8,128)(2,1)S(1)}, bf16[2,128,384]{2,1,0:T(8,128)(2,1)S(1)}, u32[]{:S(2)}, u32[]{:S(2)}) collective-permute-start(bf16[2,128,384]{2,1,0:T(8,128)(2,1)S(1)} %get-tuple-element.15), channel_id=1, source_target_pairs={{1,3},{3,5},{5,7},{7,86},{86,84},{84,82},{82,80},{80,1},{17,19},{1... | collective-permute-start | bytes 589832 | tf_op jit(solution)/shard_map/ppermute | solution.py:305
  49.1 8.2 %collective-permute-start.3 = (bf16[2,128,384]{2,1,0:T(8,128)(2,1)S(1)}, bf16[2,128,384]{2,1,0:T(8,128)(2,1)S(1)}, u32[]{:S(2)}, u32[]{:S(2)}) collective-permute-start(bf16[2,128,384]{2,1,0:T(8,128)(2,1)S(1)} %get-tuple-element.16), channel_id=1, source_target_pairs={{1,80},{3,1},{5,3},{7,5},{86,7},{84,86},{82,84},{80,82},{17,96},{1... | collective-permute-start | bytes 589832 | tf_op jit(solution)/shard_map/ppermute | solution.py:306
  52.6 4.8 %copy-start.3 = (bf16[3,3,384,384]{3,2,1,0:T(8,128)(2,1)S(1)}, bf16[3,3,384,384]{3,2,1,0:T(8,128)(2,1)}, u32[]{:S(2)}) copy-start(bf16[3,3,384,384]{3,2,1,0:T(8,128)(2,1)} %param.11) | copy-start | bytes 7962628
  57.4 16.9 %copy-start.2 = (bf16[3,3,384,384]{3,2,1,0:T(8,128)(2,1)S(1)}, bf16[3,3,384,384]{3,2,1,0:T(8,128)(2,1)}, u32[]{:S(2)}) copy-start(bf16[3,3,384,384]{3,2,1,0:T(8,128)(2,1)} %kernel.7) | copy-start | bytes 7962628
  62.2 9.1 %collective-permute-start.4 = (bf16[512,384]{1,0:T(8,128)(2,1)S(1)}, bf16[512,384]{1,0:T(8,128)(2,1)S(1)}, u32[]{:S(2)}, u32[]{:S(2)}) collective-permute-start(bf16[512,384]{1,0:T(8,128)(2,1)S(1)} %get-tuple-element.17.hidden1), channel_id=1, source_target_pairs={{1,17},{3,19},{5,21},{7,23},{86,102},{84,100},{82,98},{80,96},{17,... | collective-permute-start | bytes 1179656 | tf_op jit(solution)/shard_map/ppermute | solution.py:296
  62.3 12.0 %collective-permute-start.5 = (bf16[512,384]{1,0:T(8,128)(2,1)S(1)}, bf16[512,384]{1,0:T(8,128)(2,1)S(1)}, u32[]{:S(2)}, u32[]{:S(2)}) collective-permute-start(bf16[512,384]{1,0:T(8,128)(2,1)S(1)} %get-tuple-element.18.hidden0), channel_id=1, source_target_pairs={{1,9},{3,11},{5,13},{7,15},{86,30},{84,28},{82,26},{80,24},{17,1},... | collective-permute-start | bytes 1179656 | tf_op jit(solution)/shard_map/ppermute | solution.py:297
  75.8 9.0 %collective-permute-start.6 = (bf16[2,128,384]{2,1,0:T(8,128)(2,1)S(1)}, bf16[2,128,384]{2,1,0:T(8,128)(2,1)S(1)}, u32[]{:S(2)}, u32[]{:S(2)}) collective-permute-start(bf16[2,128,384]{2,1,0:T(8,128)(2,1)S(1)} %get-tuple-element.20), channel_id=1, source_target_pairs={{1,3},{3,5},{5,7},{7,86},{86,84},{84,82},{82,80},{80,1},{17,19},{1... | collective-permute-start | bytes 589832 | tf_op jit(solution)/shard_map/ppermute | solution.py:305
  75.9 8.9 %collective-permute-start.7 = (bf16[2,128,384]{2,1,0:T(8,128)(2,1)S(1)}, bf16[2,128,384]{2,1,0:T(8,128)(2,1)S(1)}, u32[]{:S(2)}, u32[]{:S(2)}) collective-permute-start(bf16[2,128,384]{2,1,0:T(8,128)(2,1)S(1)} %get-tuple-element.21), channel_id=1, source_target_pairs={{1,80},{3,1},{5,3},{7,5},{86,7},{84,86},{82,84},{80,82},{17,96},{1... | collective-permute-start | bytes 589832 | tf_op jit(solution)/shard_map/ppermute | solution.py:306
  96.6 6.7 %collective-permute-start.8 = (bf16[1,16,384]{2,1,0:T(8,128)(2,1)S(1)}, bf16[1,16,384]{2,1,0:T(8,128)(2,1)S(1)}, u32[]{:S(2)}, u32[]{:S(2)}) collective-permute-start(bf16[1,16,384]{2,1,0:T(8,128)(2,1)S(1)} %get-tuple-element.29), channel_id=1, source_target_pairs={{1,8},{86,9},{3,10},{84,11},{5,12},{82,13},{7,14},{80,15},{16,16},... | collective-permute-start | bytes 36872 | tf_op jit(solution)/shard_map/ppermute | solution.py:277
  101.3 4.2 %collective-permute-start.9 = (bf16[4,16,384]{2,1,0:T(8,128)(2,1)S(1)}, bf16[4,16,384]{2,1,0:T(8,128)(2,1)S(1)}, u32[]{:S(2)}, u32[]{:S(2)}) collective-permute-start(bf16[4,16,384]{2,1,0:T(8,128)(2,1)S(1)} %reshape.26), channel_id=1, source_target_pairs={{1,0},{86,1},{3,2},{84,3},{5,4},{82,5},{7,6},{80,7},{16,8},{103,9}... | collective-permute-start | bytes 147464 | tf_op jit(solution)/shard_map/ppermute | solution.py:279
  101.4 6.4 %collective-permute-start.10 = (bf16[1,16,384]{2,1,0:T(8,128)(2,1)S(1)}, bf16[1,16,384]{2,1,0:T(8,128)(2,1)S(1)}, u32[]{:S(2)}, u32[]{:S(2)}) collective-permute-start(bf16[1,16,384]{2,1,0:T(8,128)(2,1)S(1)} %get-tuple-element.28), channel_id=1, source_target_pairs={{16,0},{103,1},{18,2},{101,3},{20,4},{99,5},{22,6},{97,7},{33,8},{... | collective-permute-start | bytes 36872 | tf_op jit(solution)/shard_map/ppermute | solution.py:278
  107.8 17.2 %collective-permute-start.12 = (bf16[6,1,384]{2,1,0:T(2,128)(2,1)S(1)}, bf16[6,1,384]{2,1,0:T(2,128)(2,1)S(1)}, u32[]{:S(2)}, u32[]{:S(2)}) collective-permute-start(bf16[6,1,384]{2,1,0:T(2,128)(2,1)S(1)} %get-tuple-element.27), channel_id=1, source_target_pairs={{1,0},{2,1},{3,2},{4,3},{5,4},{6,5},{7,6},{9,8},{10,9},{11,10},{12... | collective-permute-start | bytes 13832 | tf_op jit(solution)/shard_map/ppermute | solution.py:282
  109.1 15.9 %collective-permute-start.11 = (bf16[6,1,384]{2,1,0:T(2,128)(2,1)S(1)}, bf16[6,1,384]{2,1,0:T(2,128)(2,1)S(1)}, u32[]{:S(2)}, u32[]{:S(2)}) collective-permute-start(bf16[6,1,384]{2,1,0:T(2,128)(2,1)S(1)} %get-tuple-element.26), channel_id=1, source_target_pairs={{0,1},{1,2},{2,3},{3,4},{4,5},{5,6},{6,7},{8,9},{9,10},{10,11},{11... | collective-permute-start | bytes 13832 | tf_op jit(solution)/shard_map/ppermute | solution.py:281
  118.9 19.2 %all-to-all-start.1 = ((bf16[64,2,8,384]{3,2,1,0:T(8,128)(2,1)}), bf16[64,2,8,384]{3,2,1,0:T(8,128)(2,1)S(1)}, u32[]{:S(2)}, u32[]{:S(2)}) async-start(bf16[64,2,8,384]{3,2,1,0:T(8,128)(2,1)} %get-tuple-element.22), calls=%async_computation.1 | async-start | bytes 1572864 | tf_op jit(solution)/shard_map/all_to_all | solution.py:336
  126.0 0.9 copy-start.6
  126.0 0.9 copy-start.7

commit v4 on v3

--- a/solution.py
+++ b/solution.py
@@ -34,12 +34,13 @@
 
 
 def chip(core, band, ring):
-    turn = (band + 1) % 8
-    y, side = divmod(turn, 2)
-    z = (side + y) % 2
+    y, side = divmod((band + 1 - core) % 8, 2)
+    z = core + (side + y) % 2
     if ring < 4:
-        return ring, y, core + z
-    return 7 - ring, (y + 1) % 4, (3 + core - z) % 4
+        return ring, y, z
+    if core == 0:
+        return 7 - ring, (y - 1) % 4, 3 - z
+    return 7 - ring, y, (z + 2) % 4
 
 
 def slot(core, band, ring):

time: 140 us -> 136 us (0.971)
  waiting for transfers between devices: 31.9 us -> 26.8 us
    ppermute x2, waiting for transfers between devices: 6.46 us -> 0.01 us  [plain(): down = lax.ppermute(hidden0, AXES, block_route(-1, 0))]
    ppermute x1, starting transfers between devices: 9.72 us -> 5.5 us  [fine_target(): low = lax.ppermute(crop[:, 15:], COL, line_route(8, 1))]
    ppermute x1, starting transfers between devices: 0.08 us -> 2.83 us  [fine_target(): crop = lax.ppermute(crop, AXES, crop_route(0))]
    ppermute x2, starting transfers between devices: 7.55 us -> 10.2 us  [plain(): from_right = lax.ppermute(to_left, AXES, block_route(0, -1))]
    all_to_all x1, waiting for transfers between devices: 9.47 us -> 11.7 us  [shards(): landed = lax.all_to_all(state, SPREAD, 0, 0, tiled=True)]
    ppermute x1, waiting for transfers between devices: 2.13 us -> 0.23 us  [fine_target(): crop = lax.ppermute(crop, AXES, crop_route(0))]
  transfers between devices with their start and end apart: 14 -> 14, of which waited for: 7 -> 5; matrix products, arithmetic and copies ran while one was open for 2% -> 2% of each run, Pallas kernels for 7% -> 7%
where the time goes in v4:
time: 136 us
  starting transfers between devices  40 us (29%)
  blocking collectives  36.3 us (27%)
  waiting for transfers between devices  26.8 us (20%)
  Pallas kernels  25 us (18%)
  local copies, waits for them, and re-layouts  5.2 us (4%)
    all_to_all x1, blocking collectives, shards(): state = lax.all_to_all(sent, SPREAD, 0, 0, tiled=True)  26.9 us
    pallas_call x9, Pallas kernels, run(): return call(*operands[:scalars], *near)  25 us
    all_to_all x1, waiting for transfers between devices, shards(): landed = lax.all_to_all(state, SPREAD, 0, 0, tiled=True)  11.7 us
    ppermute x2, waiting for transfers between devices, plain(): up = lax.ppermute(hidden1, AXES, block_route(1, 0))  11.5 us
    ppermute x2, starting transfers between devices, plain(): from_right = lax.ppermute(to_left, AXES, block_route(0, -1))  10.2 us
    all_to_all x1, blocking collectives, crop_cells(): lax.all_to_all(crop, AXES, 0, 0, axis_index_groups=crop_groups(), tiled=T...  9.43 us
    ppermute x2, starting transfers between devices, plain(): down = lax.ppermute(hidden0, AXES, block_route(-1, 0))  6.45 us
    all_to_all x1, starting transfers between devices, shards(): landed = lax.all_to_all(state, SPREAD, 0, 0, tiled=True)  6.24 us
  transfers between devices with their start and end apart: 14, of which 5 were waited for; matrix products, arithmetic and copies ran while one was open for 2% of the time, Pallas kernels for 7%

profile of v4, /device:TPU:0, one launch (start us, length us, event | category | flops | bytes accessed | tf_op | source)
XLA Modules:
  0.0 135.5 jit_solution(2584214888976394910)
XLA Ops:
  0.6 0.0 copy-start
  0.7 0.8 dynamic-slice_bitcast_fusion.notes
  1.5 0.0 copy-start.5
  1.5 1.1 copy-done.5
  2.6 0.0 copy-start.4
  2.6 0.9 shard_map.95
  3.5 26.9 %all_to_all.15.landed.state = bf16[64,2,8,384]{3,2,1,0:T(8,128)(2,1)S(1)} all-to-all(bf16[64,2,8,384]{3,2,1,0:T(8,128)(2,1)S(1)} %shard_map.95), channel_id=1, replica_groups=mesh['zh'=2,'y1'=2,'y0'=2,'core'=2,'x1'=2,'x0'=2,'zl'=2] {'zh','y1','y0'..., dimensions={0} | all-to-all | bytes 1572864 | tf_op jit(solution)/shard_map/all_to_all | solution.py:321
  30.4 0.0 copy-done.4
  30.4 4.0 %shard_map.96 = (bf16[512,384]{1,0:T(8,128)(2,1)S(1)}, bf16[512,384]{1,0:T(8,128)(2,1)S(1)}) custom-call(bf16[64,2,8,384]{3,2,1,0:T(8,128)(2,1)S(1)} %all_to_all.15.landed.state, bf16[3456,384]{1,0:T(8,128)(2,1)S(1)} %bitcast.22), custom_call_target="tpu_custom_call" | custom-call | tf_op jit(solution)/shard_map/pallas_call | solution.py:31
  34.5 0.1 collective-permute-start
  34.6 3.2 %collective-permute-start.1 = (bf16[512,384]{1,0:T(8,128)(2,1)S(1)}, bf16[512,384]{1,0:T(8,128)(2,1)S(1)}, u32[]{:S(2)}, u32[]{:S(2)}) collective-permute-start(bf16[512,384]{1,0:T(8,128)(2,1)S(1)} %get-tuple-element.14.hidden0), channel_id=1, source_target_pairs={{1,57},{3,59},{5,61},{7,63},{118,127},{116,125},{114,123},{112,121... | collective-permute-start | bytes 1179656 | tf_op jit(solution)/shard_map/ppermute | solution.py:298
  37.8 5.8 %collective-permute-done.up = bf16[512,384]{1,0:T(8,128)(2,1)S(1)} collective-permute-done((bf16[512,384]{1,0:T(8,128)(2,1)S(1)}, bf16[512,384]{1,0:T(8,128)(2,1)S(1)}, u32[]{:S(2)}, u32[]{:S(2)}) %collective-permute-start) | collective-permute-done | bytes 393248 | tf_op jit(solution)/shard_map/ppermute | solution.py:297
  43.5 0.0 collective-permute-done.1.down
  43.5 0.0 copy-done.1
  43.5 1.4 %shard_map.98 = (bf16[2,128,384]{2,1,0:T(8,128)(2,1)S(1)}, bf16[2,128,384]{2,1,0:T(8,128)(2,1)S(1)}) custom-call(s32[68]{0:T(128)S(1)} %dynamic-slice_bitcast_fusion.notes, bf16[512,384]{1,0:T(8,128)(2,1)S(1)} %collective-permute-done.up, bf16[512,384]{1,0:T(8,128)(2,1)S(1)} %collective-permute-done.1.down, bf16[512,384]{1,0:T(8,128)(2,1)S(1)} %get-tuple-element.14.hidden0, ...), custom_call_target="tpu_custom_call" | custom-call | tf_op jit(solution)/shard_map/pallas_call | solution.py:31
  45.0 0.6 collective-permute-start.2
  45.5 4.9 %collective-permute-start.3 = (bf16[2,128,384]{2,1,0:T(8,128)(2,1)S(1)}, bf16[2,128,384]{2,1,0:T(8,128)(2,1)S(1)}, u32[]{:S(2)}, u32[]{:S(2)}) collective-permute-start(bf16[2,128,384]{2,1,0:T(8,128)(2,1)S(1)} %get-tuple-element.16), channel_id=1, source_target_pairs={{1,112},{3,1},{5,3},{7,5},{118,7},{116,118},{114,116},{112,114},{1... | collective-permute-start | bytes 589832 | tf_op jit(solution)/shard_map/ppermute | solution.py:307
  50.4 0.0 copy-start.3
  50.4 4.8 %shard_map.97.partial = f32[2,512,384]{2,1,0:T(8,128)S(1)} custom-call(s32[68]{0:T(128)S(1)} %dynamic-slice_bitcast_fusion.notes, bf16[512,384]{1,0:T(8,128)(2,1)S(1)} %collective-permute-done.up, bf16[512,384]{1,0:T(8,128)(2,1)S(1)} %collective-permute-done.1.down, bf16[512,384]{1,0:T(8,128)(2,1)S(1)} %get-tuple-element.14.hidden0, ...), custom_call_target="tpu_custom_call" | custom-call | tf_op jit(solution)/shard_map/pallas_call | solution.py:31
  55.2 0.0 collective-permute-done.2.from_left
  55.2 0.0 collective-permute-done.3.from_right
  55.2 0.0 copy-done.3
  55.2 0.0 copy-start.2
  55.2 4.8 %shard_map.99 = (bf16[64,2,8,384]{3,2,1,0:T(8,128)(2,1)S(1)}, bf16[512,384]{1,0:T(8,128)(2,1)S(1)}, bf16[512,384]{1,0:T(8,128)(2,1)S(1)}) custom-call(s32[68]{0:T(128)S(1)} %dynamic-slice_bitcast_fusion.notes, f32[2,512,384]{2,1,0:T(8,128)S(1)} %shard_map.97.partial, bf16[2,128,384]{2,1,0:T(8,128)(2,1)S(1)} %collective-permute-done.2.from_left, ...), custom_call_target="tpu_custom_call" | custom-call | tf_op jit(solution)/shard_map/pallas_call | solution.py:31
  60.0 0.1 collective-permute-start.4
  60.1 3.2 %collective-permute-start.5 = (bf16[512,384]{1,0:T(8,128)(2,1)S(1)}, bf16[512,384]{1,0:T(8,128)(2,1)S(1)}, u32[]{:S(2)}, u32[]{:S(2)}) collective-permute-start(bf16[512,384]{1,0:T(8,128)(2,1)S(1)} %get-tuple-element.18.hidden0), channel_id=1, source_target_pairs={{1,57},{3,59},{5,61},{7,63},{118,127},{116,125},{114,123},{112,121... | collective-permute-start | bytes 1179656 | tf_op jit(solution)/shard_map/ppermute | solution.py:298
  63.3 5.8 %collective-permute-done.4.up = bf16[512,384]{1,0:T(8,128)(2,1)S(1)} collective-permute-done((bf16[512,384]{1,0:T(8,128)(2,1)S(1)}, bf16[512,384]{1,0:T(8,128)(2,1)S(1)}, u32[]{:S(2)}, u32[]{:S(2)}) %collective-permute-start.4) | collective-permute-done | bytes 393248 | tf_op jit(solution)/shard_map/ppermute | solution.py:297
  69.1 0.0 collective-permute-done.5.down
  69.1 0.0 copy-done.2
  69.1 1.4 %shard_map.101 = (bf16[2,128,384]{2,1,0:T(8,128)(2,1)S(1)}, bf16[2,128,384]{2,1,0:T(8,128)(2,1)S(1)}) custom-call(s32[68]{0:T(128)S(1)} %dynamic-slice_bitcast_fusion.notes, bf16[512,384]{1,0:T(8,128)(2,1)S(1)} %collective-permute-done.4.up, bf16[512,384]{1,0:T(8,128)(2,1)S(1)} %collective-permute-done.5.down, ...), custom_call_target="tpu_custom_call" | custom-call | tf_op jit(solution)/shard_map/pallas_call | solution.py:31
  70.5 0.1 collective-permute-start.6
  70.6 5.3 %collective-permute-start.7 = (bf16[2,128,384]{2,1,0:T(8,128)(2,1)S(1)}, bf16[2,128,384]{2,1,0:T(8,128)(2,1)S(1)}, u32[]{:S(2)}, u32[]{:S(2)}) collective-permute-start(bf16[2,128,384]{2,1,0:T(8,128)(2,1)S(1)} %get-tuple-element.21), channel_id=1, source_target_pairs={{1,112},{3,1},{5,3},{7,5},{118,7},{116,118},{114,116},{112,114},{1... | collective-permute-start | bytes 589832 | tf_op jit(solution)/shard_map/ppermute | solution.py:307
  76.0 4.8 %shard_map.100.partial = f32[2,512,384]{2,1,0:T(8,128)S(1)} custom-call(s32[68]{0:T(128)S(1)} %dynamic-slice_bitcast_fusion.notes, bf16[512,384]{1,0:T(8,128)(2,1)S(1)} %collective-permute-done.4.up, bf16[512,384]{1,0:T(8,128)(2,1)S(1)} %collective-permute-done.5.down, bf16[512,384]{1,0:T(8,128)(2,1)S(1)} %get-tuple-element.18.hidden0, ...), custom_call_target="tpu_custom_call" | custom-call | tf_op jit(solution)/shard_map/pallas_call | solution.py:31
  80.8 0.0 collective-permute-done.6.from_left
  80.8 0.0 collective-permute-done.7.from_right
  80.8 1.8 %shard_map.102 = (bf16[64,2,8,384]{3,2,1,0:T(8,128)(2,1)}, bf16[8,8,384]{2,1,0:T(8,128)(2,1)S(1)}) custom-call(s32[68]{0:T(128)S(1)} %dynamic-slice_bitcast_fusion.notes, f32[2,512,384]{2,1,0:T(8,128)S(1)} %shard_map.100.partial, bf16[2,128,384]{2,1,0:T(8,128)(2,1)S(1)} %collective-permute-done.6.from_left, ...), custom_call_target="tpu_custom_call" | custom-call | tf_op jit(solution)/shard_map/pallas_call | solution.py:31
  82.6 9.4 %all_to_all.16 = bf16[8,8,384]{2,1,0:T(8,128)(2,1)S(1)} all-to-all(bf16[8,8,384]{2,1,0:T(8,128)(2,1)S(1)} %get-tuple-element.23), channel_id=1, replica_groups={{1,3,5,7,17,19,21,23},{118,116,114,112,70,68,66,64},{16,18,20,22,32,34,..., dimensions={0} | all-to-all | bytes 98304 | tf_op jit(solution)/shard_map/all_to_all | solution.py:269
  92.1 4.8 %collective-permute-start.8 = (bf16[1,16,384]{2,1,0:T(8,128)(2,1)S(1)}, bf16[1,16,384]{2,1,0:T(8,128)(2,1)S(1)}, u32[]{:S(2)}, u32[]{:S(2)}) collective-permute-start(bf16[1,16,384]{2,1,0:T(8,128)(2,1)S(1)} %get-tuple-element.29), channel_id=1, source_target_pairs={{1,8},{118,9},{3,10},{116,11},{5,12},{114,13},{7,14},{112,15},{16,... | collective-permute-start | bytes 36872 | tf_op jit(solution)/shard_map/ppermute | solution.py:278
  97.0 2.8 %collective-permute-start.9 = (bf16[4,16,384]{2,1,0:T(8,128)(2,1)S(1)}, bf16[4,16,384]{2,1,0:T(8,128)(2,1)S(1)}, u32[]{:S(2)}, u32[]{:S(2)}) collective-permute-start(bf16[4,16,384]{2,1,0:T(8,128)(2,1)S(1)} %reshape.26), channel_id=1, source_target_pairs={{1,0},{118,1},{3,2},{116,3},{5,4},{114,5},{7,6},{112,7},{16,8},{71... | collective-permute-start | bytes 147464 | tf_op jit(solution)/shard_map/ppermute | solution.py:280
  99.8 1.9 %collective-permute-start.10 = (bf16[1,16,384]{2,1,0:T(8,128)(2,1)S(1)}, bf16[1,16,384]{2,1,0:T(8,128)(2,1)S(1)}, u32[]{:S(2)}, u32[]{:S(2)}) collective-permute-start(bf16[1,16,384]{2,1,0:T(8,128)(2,1)S(1)} %get-tuple-element.28), channel_id=1, source_target_pairs={{16,0},{71,1},{18,2},{69,3},{20,4},{67,5},{22,6},{65,7},{33,8},{86... | collective-permute-start | bytes 36872 | tf_op jit(solution)/shard_map/ppermute | solution.py:279
  101.7 0.0 collective-permute-done.8
  101.7 0.2 collective-permute-done.9
  102.0 3.4 %collective-permute-done.10 = bf16[1,16,384]{2,1,0:T(8,128)(2,1)S(1)} collective-permute-done((bf16[1,16,384]{2,1,0:T(8,128)(2,1)S(1)}, bf16[1,16,384]{2,1,0:T(8,128)(2,1)S(1)}, u32[]{:S(2)}, u32[]{:S(2)}) %collective-permute-start.10) | collective-permute-done | bytes 12320 | tf_op jit(solution)/shard_map/ppermute | solution.py:279
  105.4 1.3 collective-permute-start.12
  106.7 5.5 %collective-permute-start.11 = (bf16[6,1,384]{2,1,0:T(2,128)(2,1)S(1)}, bf16[6,1,384]{2,1,0:T(2,128)(2,1)S(1)}, u32[]{:S(2)}, u32[]{:S(2)}) collective-permute-start(bf16[6,1,384]{2,1,0:T(2,128)(2,1)S(1)} %get-tuple-element.26), channel_id=1, source_target_pairs={{0,1},{1,2},{2,3},{3,4},{4,5},{5,6},{6,7},{8,9},{9,10},{10,11},{11... | collective-permute-start | bytes 13832 | tf_op jit(solution)/shard_map/ppermute | solution.py:282
  112.2 6.2 %all-to-all-start.1 = ((bf16[64,2,8,384]{3,2,1,0:T(8,128)(2,1)}), bf16[64,2,8,384]{3,2,1,0:T(8,128)(2,1)S(1)}, u32[]{:S(2)}, u32[]{:S(2)}) async-start(bf16[64,2,8,384]{3,2,1,0:T(8,128)(2,1)} %get-tuple-element.22), calls=%async_computation.1 | async-start | bytes 1572864 | tf_op jit(solution)/shard_map/all_to_all | solution.py:337
  118.4 0.0 collective-permute-done.12
  118.5 0.0 collective-permute-done.11
  118.5 0.0 copy-done
  118.5 0.4 convolution_convert_fusion
  118.9 0.4 reshape.27
  119.3 0.2 copy.12
  119.5 0.0 copy-start.6
  119.5 0.0 copy-start.7
  119.5 0.1 slice_bitcast_fusion
  119.6 0.1 copy.18
  119.6 0.1 pad.clone
  119.8 0.6 copy-done.6
  120.4 0.0 copy-done.7
  120.4 0.8 fusion
  121.2 0.8 copy.17
  122.0 11.7 %all-to-all-done.1.landed = bf16[64,2,8,384]{3,2,1,0:T(8,128)(2,1)S(1)} async-done(((bf16[64,2,8,384]{3,2,1,0:T(8,128)(2,1)}), bf16[64,2,8,384]{3,2,1,0:T(8,128)(2,1)S(1)}, u32[]{:S(2)}, u32[]{:S(2)}) %all-to-all-start.1) | async-done | bytes 786464 | tf_op jit(solution)/shard_map/all_to_all | solution.py:337
  133.7 1.0 shard_map.103
  134.7 0.9 copy.21
  (13 shorter events, 0.2 us)
Async XLA Ops:
  0.6 117.8 %copy-start = (bf16[384,1536]{1,0:T(8,128)(2,1)S(1)}, bf16[384,1536]{1,0:T(8,128)(2,1)}, u32[]{:S(2)}) copy-start(bf16[384,1536]{1,0:T(8,128)(2,1)} %param.13) | copy-start | bytes 3538948
  1.5 1.1 copy-start.5
  2.6 27.8 %copy-start.4 = (bf16[3,3,384,384]{3,2,1,0:T(8,128)(2,1)S(1)}, bf16[3,3,384,384]{3,2,1,0:T(8,128)(2,1)}, u32[]{:S(2)}) copy-start(bf16[3,3,384,384]{3,2,1,0:T(8,128)(2,1)} %param.9) | copy-start | bytes 7962628
  30.4 13.1 %copy-start.1 = (bf16[3,3,384,384]{3,2,1,0:T(8,128)(2,1)S(1)}, bf16[3,3,384,384]{3,2,1,0:T(8,128)(2,1)}, u32[]{:S(2)}) copy-start(bf16[3,3,384,384]{3,2,1,0:T(8,128)(2,1)} %kernel.5) | copy-start | bytes 7962628
  34.5 9.1 %collective-permute-start = (bf16[512,384]{1,0:T(8,128)(2,1)S(1)}, bf16[512,384]{1,0:T(8,128)(2,1)S(1)}, u32[]{:S(2)}, u32[]{:S(2)}) collective-permute-start(bf16[512,384]{1,0:T(8,128)(2,1)S(1)} %get-tuple-element.13.hidden1), channel_id=1, source_target_pairs={{1,17},{3,19},{5,21},{7,23},{118,70},{116,68},{114,66},{112,64},{1... | collective-permute-start | bytes 1179656 | tf_op jit(solution)/shard_map/ppermute | solution.py:297
  34.6 9.0 %collective-permute-start.1 = (bf16[512,384]{1,0:T(8,128)(2,1)S(1)}, bf16[512,384]{1,0:T(8,128)(2,1)S(1)}, u32[]{:S(2)}, u32[]{:S(2)}) collective-permute-start(bf16[512,384]{1,0:T(8,128)(2,1)S(1)} %get-tuple-element.14.hidden0), channel_id=1, source_target_pairs={{1,57},{3,59},{5,61},{7,63},{118,127},{116,125},{114,123},{112,121... | collective-permute-start | bytes 1179656 | tf_op jit(solution)/shard_map/ppermute | solution.py:298
  45.0 10.2 %collective-permute-start.2 = (bf16[2,128,384]{2,1,0:T(8,128)(2,1)S(1)}, bf16[2,128,384]{2,1,0:T(8,128)(2,1)S(1)}, u32[]{:S(2)}, u32[]{:S(2)}) collective-permute-start(bf16[2,128,384]{2,1,0:T(8,128)(2,1)S(1)} %get-tuple-element.15), channel_id=1, source_target_pairs={{1,3},{3,5},{5,7},{7,118},{118,116},{116,114},{114,112},{112,1},{1... | collective-permute-start | bytes 589832 | tf_op jit(solution)/shard_map/ppermute | solution.py:306
  45.5 9.7 %collective-permute-start.3 = (bf16[2,128,384]{2,1,0:T(8,128)(2,1)S(1)}, bf16[2,128,384]{2,1,0:T(8,128)(2,1)S(1)}, u32[]{:S(2)}, u32[]{:S(2)}) collective-permute-start(bf16[2,128,384]{2,1,0:T(8,128)(2,1)S(1)} %get-tuple-element.16), channel_id=1, source_target_pairs={{1,112},{3,1},{5,3},{7,5},{118,7},{116,118},{114,116},{112,114},{1... | collective-permute-start | bytes 589832 | tf_op jit(solution)/shard_map/ppermute | solution.py:307
  50.4 4.8 %copy-start.3 = (bf16[3,3,384,384]{3,2,1,0:T(8,128)(2,1)S(1)}, bf16[3,3,384,384]{3,2,1,0:T(8,128)(2,1)}, u32[]{:S(2)}) copy-start(bf16[3,3,384,384]{3,2,1,0:T(8,128)(2,1)} %param.11) | copy-start | bytes 7962628
  55.2 13.9 %copy-start.2 = (bf16[3,3,384,384]{3,2,1,0:T(8,128)(2,1)S(1)}, bf16[3,3,384,384]{3,2,1,0:T(8,128)(2,1)}, u32[]{:S(2)}) copy-start(bf16[3,3,384,384]{3,2,1,0:T(8,128)(2,1)} %kernel.7) | copy-start | bytes 7962628
  60.0 9.1 %collective-permute-start.4 = (bf16[512,384]{1,0:T(8,128)(2,1)S(1)}, bf16[512,384]{1,0:T(8,128)(2,1)S(1)}, u32[]{:S(2)}, u32[]{:S(2)}) collective-permute-start(bf16[512,384]{1,0:T(8,128)(2,1)S(1)} %get-tuple-element.17.hidden1), channel_id=1, source_target_pairs={{1,17},{3,19},{5,21},{7,23},{118,70},{116,68},{114,66},{112,64},{1... | collective-permute-start | bytes 1179656 | tf_op jit(solution)/shard_map/ppermute | solution.py:297
  60.1 9.0 %collective-permute-start.5 = (bf16[512,384]{1,0:T(8,128)(2,1)S(1)}, bf16[512,384]{1,0:T(8,128)(2,1)S(1)}, u32[]{:S(2)}, u32[]{:S(2)}) collective-permute-start(bf16[512,384]{1,0:T(8,128)(2,1)S(1)} %get-tuple-element.18.hidden0), channel_id=1, source_target_pairs={{1,57},{3,59},{5,61},{7,63},{118,127},{116,125},{114,123},{112,121... | collective-permute-start | bytes 1179656 | tf_op jit(solution)/shard_map/ppermute | solution.py:298
  70.5 10.2 %collective-permute-start.6 = (bf16[2,128,384]{2,1,0:T(8,128)(2,1)S(1)}, bf16[2,128,384]{2,1,0:T(8,128)(2,1)S(1)}, u32[]{:S(2)}, u32[]{:S(2)}) collective-permute-start(bf16[2,128,384]{2,1,0:T(8,128)(2,1)S(1)} %get-tuple-element.20), channel_id=1, source_target_pairs={{1,3},{3,5},{5,7},{7,118},{118,116},{116,114},{114,112},{112,1},{1... | collective-permute-start | bytes 589832 | tf_op jit(solution)/shard_map/ppermute | solution.py:306
  70.6 10.2 %collective-permute-start.7 = (bf16[2,128,384]{2,1,0:T(8,128)(2,1)S(1)}, bf16[2,128,384]{2,1,0:T(8,128)(2,1)S(1)}, u32[]{:S(2)}, u32[]{:S(2)}) collective-permute-start(bf16[2,128,384]{2,1,0:T(8,128)(2,1)S(1)} %get-tuple-element.21), channel_id=1, source_target_pairs={{1,112},{3,1},{5,3},{7,5},{118,7},{116,118},{114,116},{112,114},{1... | collective-permute-start | bytes 589832 | tf_op jit(solution)/shard_map/ppermute | solution.py:307
  92.1 9.6 %collective-permute-start.8 = (bf16[1,16,384]{2,1,0:T(8,128)(2,1)S(1)}, bf16[1,16,384]{2,1,0:T(8,128)(2,1)S(1)}, u32[]{:S(2)}, u32[]{:S(2)}) collective-permute-start(bf16[1,16,384]{2,1,0:T(8,128)(2,1)S(1)} %get-tuple-element.29), channel_id=1, source_target_pairs={{1,8},{118,9},{3,10},{116,11},{5,12},{114,13},{7,14},{112,15},{16,... | collective-permute-start | bytes 36872 | tf_op jit(solution)/shard_map/ppermute | solution.py:278
  97.0 5.0 %collective-permute-start.9 = (bf16[4,16,384]{2,1,0:T(8,128)(2,1)S(1)}, bf16[4,16,384]{2,1,0:T(8,128)(2,1)S(1)}, u32[]{:S(2)}, u32[]{:S(2)}) collective-permute-start(bf16[4,16,384]{2,1,0:T(8,128)(2,1)S(1)} %reshape.26), channel_id=1, source_target_pairs={{1,0},{118,1},{3,2},{116,3},{5,4},{114,5},{7,6},{112,7},{16,8},{71... | collective-permute-start | bytes 147464 | tf_op jit(solution)/shard_map/ppermute | solution.py:280
  99.8 5.6 %collective-permute-start.10 = (bf16[1,16,384]{2,1,0:T(8,128)(2,1)S(1)}, bf16[1,16,384]{2,1,0:T(8,128)(2,1)S(1)}, u32[]{:S(2)}, u32[]{:S(2)}) collective-permute-start(bf16[1,16,384]{2,1,0:T(8,128)(2,1)S(1)} %get-tuple-element.28), channel_id=1, source_target_pairs={{16,0},{71,1},{18,2},{69,3},{20,4},{67,5},{22,6},{65,7},{33,8},{86... | collective-permute-start | bytes 36872 | tf_op jit(solution)/shard_map/ppermute | solution.py:279
  105.4 13.1 %collective-permute-start.12 = (bf16[6,1,384]{2,1,0:T(2,128)(2,1)S(1)}, bf16[6,1,384]{2,1,0:T(2,128)(2,1)S(1)}, u32[]{:S(2)}, u32[]{:S(2)}) collective-permute-start(bf16[6,1,384]{2,1,0:T(2,128)(2,1)S(1)} %get-tuple-element.27), channel_id=1, source_target_pairs={{1,0},{2,1},{3,2},{4,3},{5,4},{6,5},{7,6},{9,8},{10,9},{11,10},{12... | collective-permute-start | bytes 13832 | tf_op jit(solution)/shard_map/ppermute | solution.py:283
  106.7 11.8 %collective-permute-start.11 = (bf16[6,1,384]{2,1,0:T(2,128)(2,1)S(1)}, bf16[6,1,384]{2,1,0:T(2,128)(2,1)S(1)}, u32[]{:S(2)}, u32[]{:S(2)}) collective-permute-start(bf16[6,1,384]{2,1,0:T(2,128)(2,1)S(1)} %get-tuple-element.26), channel_id=1, source_target_pairs={{0,1},{1,2},{2,3},{3,4},{4,5},{5,6},{6,7},{8,9},{9,10},{10,11},{11... | collective-permute-start | bytes 13832 | tf_op jit(solution)/shard_map/ppermute | solution.py:282
  112.2 21.5 %all-to-all-start.1 = ((bf16[64,2,8,384]{3,2,1,0:T(8,128)(2,1)}), bf16[64,2,8,384]{3,2,1,0:T(8,128)(2,1)S(1)}, u32[]{:S(2)}, u32[]{:S(2)}) async-start(bf16[64,2,8,384]{3,2,1,0:T(8,128)(2,1)} %get-tuple-element.22), calls=%async_computation.1 | async-start | bytes 1572864 | tf_op jit(solution)/shard_map/all_to_all | solution.py:337
  119.5 0.9 copy-start.6
  119.5 0.9 copy-start.7

commit v5 on v4

--- a/solution.py
+++ b/solution.py
@@ -65,17 +65,55 @@
     return route
 
 
+def meets(start, length, low, high):
+    return start <= high and start + length > low
+
+
+def crop_picks(core, band, ring):
+    first_row = 16 * core + 2 * band
+    rows = [
+        4 * int(meets(first_row + 32, 2, 8 * m - 1, 8 * m + 8)) for m in range(8)
+    ]
+    columns = [
+        sum(g for g in range(4) if meets(4 * ring + 32 * g, 4, 16 * c - 1, 16 * c + 16))
+        for c in range(8)
+    ]
+    return rows + columns
+
+
+def window_rows(row, core):
+    bands = []
+    for line in range(4 * row - 1, 4 * row + 5):
+        owner, band = divmod(line % 32 // 2, 8)
+        bands.append(band if 0 <= line < 64 and owner == core else -1)
+    return bands
+
+
+def window_rings(column):
+    starts = range(16 * column - 4, 16 * column + 20, 4)
+    return [start % 32 // 4 if 0 <= start < 128 else -1 for start in starts]
+
+
+FIRST_ROW, LAST_ROW, FIRST_RING, LAST_RING = range(64, 68)
+PICK_ROW, PICK_COLUMN, OWN_ROWS, OTHER_ROWS, RINGS = 68, 76, 84, 90, 96
+
+
 def notes():
     table = [None] * 128
     for core, band, ring in BLOCKS:
         slots = [slot(core, other // 8, other % 8) for other in range(64)]
-        row = 8 * core + band
-        table[device(core, band, ring)] = slots + [row == 0, row == 15, ring == 0, ring == 7]
+        line = 8 * core + band
+        place = device(core, band, ring)
+        row, column = divmod(place, 8)
+        table[place] = (
+            slots
+            + [line == 0, line == 15, ring == 0, ring == 7]
+            + crop_picks(core, band, ring)
+            + window_rows(row, core)
+            + window_rows(row ^ 1, core)
+            + window_rings(column)
+        )
     return jnp.array(table, jnp.int32)
-
-
-def line_route(count, step):
-    return [(i, i + step) for i in range(count) if 0 <= i + step < count]
 
 
 def gather_body(notes, context, sent):
@@ -150,10 +188,10 @@
     left = from_left[i0].astype(F32)
     right = from_right[i0].astype(F32)
     left = jnp.where(
-        notes[66] == 1, jnp.where(place == 0, 0.0, pltpu.roll(left, 1, 0)), left
+        notes[FIRST_RING] == 1, jnp.where(place == 0, 0.0, pltpu.roll(left, 1, 0)), left
     )
     right = jnp.where(
-        notes[67] == 1, jnp.where(place == 15, 0.0, pltpu.roll(right, 127, 0)), right
+        notes[LAST_RING] == 1, jnp.where(place == 15, 0.0, pltpu.roll(right, 127, 0)), right
     )
     pieces = []
     for lane in range(0, channels, 128):
@@ -173,18 +211,48 @@
         dilated_band(cells.astype(F32).reshape(8, 64, channels), kernel, hidden, shelves, 2)
 
 
-def final_body(notes, partial, from_left, from_right, state, crop, sums):
-    channels = state.shape[-1]
+def final_body(notes, partial, from_left, from_right, outgoing, sums, crop):
+    channels = outgoing.shape[-1]
     for i0 in range(2):
         cells = settle(partial, sums, from_left, from_right, notes, i0, channels)
-        state[:, i0] = cells.reshape(64, 8, channels)
+        outgoing[:, i0] = cells.reshape(64, 8, channels)
     first = lax.broadcasted_iota(jnp.int32, (8, channels), 0) < 4
     for pair in range(4):
         place = 8 * (4 + pair // 2) + 4 + pair % 2
-        top = state[place, 0].astype(F32)
-        bottom = state[place, 1].astype(F32)
+        top = outgoing[place, 0].astype(F32)
+        bottom = outgoing[place, 1].astype(F32)
         crop[2 * pair] = jnp.where(first, top, pltpu.roll(bottom, 4, 0)).astype(BF16)
         crop[2 * pair + 1] = jnp.where(first, pltpu.roll(top, 4, 0), bottom).astype(BF16)
+
+    def step(chip_row, carry):
+        for column in range(8):
+            pick = notes[PICK_ROW + chip_row] + notes[PICK_COLUMN + column]
+            outgoing[8 * chip_row + column, 2] = crop[pick]
+        return carry
+
+    lax.fori_loop(0, 8, step, 0)
+
+
+def window_body(notes, landed, own, other):
+    channels = own.shape[-1]
+    first = lax.broadcasted_iota(jnp.int32, (8, channels), 0) < 4
+    for window, rows in ((own, OWN_ROWS), (other, OTHER_ROWS)):
+        for line in range(6):
+            band = notes[rows + line]
+            for tile in range(3):
+                halves = []
+                for side in range(2):
+                    ring = notes[RINGS + 2 * tile + side]
+                    there = jnp.logical_and(band >= 0, ring >= 0)
+                    place = notes[jnp.where(there, 8 * band + ring, 0)]
+                    block = landed[place, 2].astype(F32)
+                    halves.append(jnp.where(there, block, 0.0))
+                even, odd = halves
+                if line % 2:
+                    joined = jnp.where(first, even, pltpu.roll(odd, 4, 0))
+                else:
+                    joined = jnp.where(first, pltpu.roll(even, 4, 0), odd)
+                window[line, 8 * tile : 8 * tile + 8] = joined.astype(BF16)
 
 
 def edge_body(notes, up, down, hidden0, hidden1, kernel, to_left, to_right, above, below, wide):
@@ -194,9 +262,9 @@
     above[64:] = up[...]
     below[:512] = down[...]
     below[512:] = blank
-    start = pl.multiple_of(64 - 64 * notes[64], 64)
+    start = pl.multiple_of(64 - 64 * notes[FIRST_ROW], 64)
     lines = [above[pl.ds(start, 512)], hidden0[...], hidden1[...]]
-    start = pl.multiple_of(64 * notes[65], 64)
+    start = pl.multiple_of(64 * notes[LAST_ROW], 64)
     lines.append(below[pl.ds(start, 512)])
     for index, line in enumerate(lines):
         for lane in range(0, channels, 128):
@@ -228,8 +296,8 @@
     above[64:] = up[...]
     below[:512] = down[...]
     below[512:] = blank
-    over = above[pl.ds(pl.multiple_of(64 - 64 * notes[64], 64), 512)]
-    under = below[pl.ds(pl.multiple_of(64 * notes[65], 64), 512)]
+    over = above[pl.ds(pl.multiple_of(64 - 64 * notes[FIRST_ROW], 64), 512)]
+    under = below[pl.ds(pl.multiple_of(64 * notes[LAST_ROW], 64), 512)]
     lines = (over, hidden0[...], hidden1[...], under)
     place = lax.broadcasted_iota(jnp.int32, (512, channels), 0) % 4
     for i0 in range(2):
@@ -244,47 +312,11 @@
         partial[i0] = total
 
 
-def crop_route(shift):
-    route = []
-    for row in range(16):
-        for column in range(8):
-            i5, i4, i32 = row // 8, row // 4 % 2, row % 4
-            source = device(i4, 2 * i32 + i5, 4 * (column % 2) + column // 2)
-            if 0 <= row + shift < 16:
-                route.append((source, (row + shift) * 8 + column))
-    return route
-
-
-def crop_groups():
-    return [
-        [device(core, 2 * rows + i1, 4 * j4 + j32) for i1 in range(2) for j32 in range(4)]
-        for core in range(2)
-        for rows in range(4)
-        for j4 in range(2)
-    ]
-
-
-def crop_cells(crop):
-    channels = crop.shape[-1]
-    crop = lax.all_to_all(
-        crop, AXES, 0, 0, axis_index_groups=crop_groups(), tiled=True
-    )
-    crop = crop.reshape(2, 4, 2, 4, channels).transpose(0, 2, 1, 3, 4)
-    return crop.reshape(4, 16, channels)
-
-
 def fine_target(crop, lift_weight, fine_weight):
     width = fine_weight.shape[-1]
-    low = lax.ppermute(crop[3:], AXES, crop_route(1))
-    high = lax.ppermute(crop[:1], AXES, crop_route(-1))
-    crop = lax.ppermute(crop, AXES, crop_route(0))
-    crop = jnp.concatenate([low, crop, high], 0)
-    low = lax.ppermute(crop[:, 15:], COL, line_route(8, 1))
-    high = lax.ppermute(crop[:, :1], COL, line_route(8, -1))
-    crop = jnp.concatenate([low, crop, high], 1)
     lifted = jnp.einsum("rcf,fg->rcg", crop, lift_weight, preferred_element_type=F32).astype(BF16)
-    lifted = lifted.reshape(6, 18, 4, 4, width).transpose(0, 2, 1, 3, 4).reshape(24, 72, width)
-    lifted = lifted[3:21, 3:69]
+    lifted = lifted.reshape(6, 24, 4, 4, width).transpose(0, 2, 1, 3, 4).reshape(24, 96, width)
+    lifted = lifted[3:21, 15:81]
     target = lax.conv_general_dilated(
         lifted[None], fine_weight, (1, 1), ((0, 0), (0, 0)),
         dimension_numbers=("NHWC", "HWIO", "NHWC"), preferred_element_type=F32,
@@ -330,13 +362,19 @@
         4, 1,
     )(own, *edges, second_dilated_weight.reshape(9 * channels, channels))
     edges = plain(hidden0, hidden1, state, second_plain_weight, own)
-    state, crop = kernel_call(
-        final_body, [(spread, BF16), ((8, 8, channels), BF16)], [((2, 3, 512, 128), F32)], 3, 1
+    (outgoing,) = kernel_call(
+        final_body,
+        [((64, 3, 8, channels), BF16)],
+        [((2, 3, 512, 128), F32), ((8, 8, channels), BF16)],
+        3, 1,
     )(own, *edges)
-    crop = crop_cells(crop)
-    landed = lax.all_to_all(state, SPREAD, 0, 0, tiled=True)
-    target = fine_target(crop, lift_weight, fine_weight)
+    landed = lax.all_to_all(outgoing, SPREAD, 0, 0, tiled=True)
+    window, other = kernel_call(window_body, [((6, 24, channels), BF16)] * 2, (), 1, 1)(
+        own, landed
+    )
+    swapped = lax.ppermute(other, "core", [(0, 1), (1, 0)])
     (result,) = kernel_call(scatter_body, [((16, 64, channels), BF16)], (), 1, 1)(own, landed)
+    target = fine_target(window + swapped, lift_weight, fine_weight)
     return result, target
 
 

time: 136 us -> 114 us (0.84); the launches traced: 136 us -> 112 us
  starting transfers between devices: 40 us -> 17.5 us
  waiting for transfers between devices: 26.8 us -> 11.5 us
  blocking collectives: 36.3 us -> 50.7 us
    ppermute x5 -> x1, starting transfers between devices: 16.3 us -> 0.09 us  [shards(): swapped = lax.ppermute(other, 'core', [(0, 1), (1, 0)])]
    all_to_all x1, blocking collectives: 9.43 us -> 23.8 us  [shards(): landed = lax.all_to_all(outgoing, SPREAD, 0, 0, tiled=True)]
    all_to_all x1 -> x0, waiting for transfers between devices: 11.7 us -> none  [shards(): landed = lax.all_to_all(state, SPREAD, 0, 0, tiled=True)]
    all_to_all x1 -> x0, starting transfers between devices: 6.24 us -> none  [shards(): landed = lax.all_to_all(state, SPREAD, 0, 0, tiled=True)]
    ppermute x5 -> x1, waiting for transfers between devices: 3.63 us -> 0.01 us  [shards(): swapped = lax.ppermute(other, 'core', [(0, 1), (1, 0)])]
    unnamed x21 -> x19, local copies, waits for them, and re-layouts: 3.46 us -> 3.45 us
    pallas_call x9 -> x10, Pallas kernels: 25 us -> 25 us  [run(): return call(*operands[:scalars], *near)]
  transfers between devices with their start and end apart: 14 -> 9, of which waited for: 5 -> 2; matrix products, arithmetic and copies ran while one was open for 2% -> 1% of each run, Pallas kernels for 7% -> 9%
where the time goes in v5:
time: 114 us; the launch traced here: 112 us
  blocking collectives  50.7 us (44%)
  Pallas kernels  25 us (22%)
  starting transfers between devices  17.5 us (15%)
  waiting for transfers between devices  11.5 us (10%)
  local copies, waits for them, and re-layouts  5.27 us (5%)
  matrix products  1.15 us (1%)
    all_to_all x1, blocking collectives, shards(): state = lax.all_to_all(sent, SPREAD, 0, 0, tiled=True)  26.9 us
    pallas_call x10, Pallas kernels, run(): return call(*operands[:scalars], *near)  25 us
    all_to_all x1, blocking collectives, shards(): landed = lax.all_to_all(outgoing, SPREAD, 0, 0, tiled=True)  23.8 us
    ppermute x2, waiting for transfers between devices, plain(): up = lax.ppermute(hidden1, AXES, block_route(1, 0))  11.5 us
    ppermute x2, starting transfers between devices, plain(): from_right = lax.ppermute(to_left, AXES, block_route(0, -1))  10.2 us
    ppermute x2, starting transfers between devices, plain(): down = lax.ppermute(hidden0, AXES, block_route(-1, 0))  6.45 us
    unnamed x19, local copies, waits for them, and re-layouts  3.45 us
  transfers between devices with their start and end apart: 9, of which 2 were waited for; matrix products, arithmetic and copies ran while one was open for 1% of the time, Pallas kernels for 9%

profile of v5, /device:TPU:0, one launch (start us, length us, event | category | flops | bytes accessed | tf_op | source)
XLA Modules:
  0.0 112.0 jit_solution(11672212233731575540)
XLA Ops:
  0.6 0.0 copy-start
  0.7 0.8 dynamic-slice_bitcast_fusion.notes
  1.5 0.0 copy-start.5
  1.5 1.1 %copy-done.5 = bf16[16,64,384]{2,1,0:T(8,128)(2,1)S(1)} copy-done((bf16[16,64,384]{2,1,0:T(8,128)(2,1)S(1)}, bf16[16,64,384]{2,1,0:T(8,128)(2,1)}, u32[]{:S(2)}) %copy-start.5) | copy-done | bytes 786456
  2.6 0.0 copy-start.4
  2.6 0.9 shard_map.95
  3.5 26.9 %all_to_all.10.landed.state = bf16[64,2,8,384]{3,2,1,0:T(8,128)(2,1)S(1)} all-to-all(bf16[64,2,8,384]{3,2,1,0:T(8,128)(2,1)S(1)} %shard_map.95), channel_id=1, replica_groups=mesh['zh'=2,'y1'=2,'y0'=2,'core'=2,'x1'=2,'x0'=2,'zl'=2] {'zh','y1','y0'..., dimensions={0} | all-to-all | bytes 1572864 | tf_op jit(solution)/shard_map/all_to_all | solution.py:353
  30.4 0.0 copy-done.4
  30.4 0.0 copy-start.1
  30.4 4.0 %shard_map.96 = (bf16[512,384]{1,0:T(8,128)(2,1)S(1)}, bf16[512,384]{1,0:T(8,128)(2,1)S(1)}) custom-call(bf16[64,2,8,384]{3,2,1,0:T(8,128)(2,1)S(1)} %all_to_all.10.landed.state, bf16[3456,384]{1,0:T(8,128)(2,1)S(1)} %bitcast.21), custom_call_target="tpu_custom_call" | custom-call | tf_op jit(solution)/shard_map/pallas_call | solution.py:31
  34.5 0.1 collective-permute-start
  34.6 3.2 %collective-permute-start.1 = (bf16[512,384]{1,0:T(8,128)(2,1)S(1)}, bf16[512,384]{1,0:T(8,128)(2,1)S(1)}, u32[]{:S(2)}, u32[]{:S(2)}) collective-permute-start(bf16[512,384]{1,0:T(8,128)(2,1)S(1)} %get-tuple-element.14.hidden0), channel_id=1, source_target_pairs={{1,57},{3,59},{5,61},{7,63},{118,127},{116,125},{114,123},{112,121... | collective-permute-start | bytes 1179656 | tf_op jit(solution)/shard_map/ppermute | solution.py:330
  37.8 5.8 %collective-permute-done.up = bf16[512,384]{1,0:T(8,128)(2,1)S(1)} collective-permute-done((bf16[512,384]{1,0:T(8,128)(2,1)S(1)}, bf16[512,384]{1,0:T(8,128)(2,1)S(1)}, u32[]{:S(2)}, u32[]{:S(2)}) %collective-permute-start) | collective-permute-done | bytes 393248 | tf_op jit(solution)/shard_map/ppermute | solution.py:329
  43.5 0.0 collective-permute-done.1.down
  43.5 0.0 copy-done.1
  43.5 1.4 %shard_map.98 = (bf16[2,128,384]{2,1,0:T(8,128)(2,1)S(1)}, bf16[2,128,384]{2,1,0:T(8,128)(2,1)S(1)}) custom-call(s32[102]{0:T(128)S(1)} %dynamic-slice_bitcast_fusion.notes, bf16[512,384]{1,0:T(8,128)(2,1)S(1)} %collective-permute-done.up, bf16[512,384]{1,0:T(8,128)(2,1)S(1)} %collective-permute-done.1.down, bf16[512,384]{1,0:T(8,128)(2,1)S(1)} %get-tuple-element.14.hidden0, ...), custom_call_target="tpu_custom_call" | custom-call | tf_op jit(solution)/shard_map/pallas_call | solution.py:31
  45.0 0.6 collective-permute-start.2
  45.5 4.9 %collective-permute-start.3 = (bf16[2,128,384]{2,1,0:T(8,128)(2,1)S(1)}, bf16[2,128,384]{2,1,0:T(8,128)(2,1)S(1)}, u32[]{:S(2)}, u32[]{:S(2)}) collective-permute-start(bf16[2,128,384]{2,1,0:T(8,128)(2,1)S(1)} %get-tuple-element.16), channel_id=1, source_target_pairs={{1,112},{3,1},{5,3},{7,5},{118,7},{116,118},{114,116},{112,114},{1... | collective-permute-start | bytes 589832 | tf_op jit(solution)/shard_map/ppermute | solution.py:339
  50.4 0.0 copy-start.3
  50.4 4.8 %shard_map.97.partial = f32[2,512,384]{2,1,0:T(8,128)S(1)} custom-call(s32[102]{0:T(128)S(1)} %dynamic-slice_bitcast_fusion.notes, bf16[512,384]{1,0:T(8,128)(2,1)S(1)} %collective-permute-done.up, bf16[512,384]{1,0:T(8,128)(2,1)S(1)} %collective-permute-done.1.down, bf16[512,384]{1,0:T(8,128)(2,1)S(1)} %get-tuple-element.14.hidden0, ...), custom_call_target="tpu_custom_call" | custom-call | tf_op jit(solution)/shard_map/pallas_call | solution.py:31
  55.2 0.0 collective-permute-done.2.from_left
  55.2 0.0 collective-permute-done.3.from_right
  55.2 0.0 copy-done.3
  55.2 0.0 copy-start.2
  55.2 4.8 %shard_map.99 = (bf16[64,2,8,384]{3,2,1,0:T(8,128)(2,1)S(1)}, bf16[512,384]{1,0:T(8,128)(2,1)S(1)}, bf16[512,384]{1,0:T(8,128)(2,1)S(1)}) custom-call(s32[102]{0:T(128)S(1)} %dynamic-slice_bitcast_fusion.notes, f32[2,512,384]{2,1,0:T(8,128)S(1)} %shard_map.97.partial, bf16[2,128,384]{2,1,0:T(8,128)(2,1)S(1)} %collective-permute-done.2.from_left, ...), custom_call_target="tpu_custom_call" | custom-call | tf_op jit(solution)/shard_map/pallas_call | solution.py:31
  60.0 0.1 collective-permute-start.4
  60.1 3.2 %collective-permute-start.5 = (bf16[512,384]{1,0:T(8,128)(2,1)S(1)}, bf16[512,384]{1,0:T(8,128)(2,1)S(1)}, u32[]{:S(2)}, u32[]{:S(2)}) collective-permute-start(bf16[512,384]{1,0:T(8,128)(2,1)S(1)} %get-tuple-element.18.hidden0), channel_id=1, source_target_pairs={{1,57},{3,59},{5,61},{7,63},{118,127},{116,125},{114,123},{112,121... | collective-permute-start | bytes 1179656 | tf_op jit(solution)/shard_map/ppermute | solution.py:330
  63.3 5.8 %collective-permute-done.4.up = bf16[512,384]{1,0:T(8,128)(2,1)S(1)} collective-permute-done((bf16[512,384]{1,0:T(8,128)(2,1)S(1)}, bf16[512,384]{1,0:T(8,128)(2,1)S(1)}, u32[]{:S(2)}, u32[]{:S(2)}) %collective-permute-start.4) | collective-permute-done | bytes 393248 | tf_op jit(solution)/shard_map/ppermute | solution.py:329
  69.1 0.0 collective-permute-done.5.down
  69.1 0.0 copy-done.2
  69.1 1.4 %shard_map.101 = (bf16[2,128,384]{2,1,0:T(8,128)(2,1)S(1)}, bf16[2,128,384]{2,1,0:T(8,128)(2,1)S(1)}) custom-call(s32[102]{0:T(128)S(1)} %dynamic-slice_bitcast_fusion.notes, bf16[512,384]{1,0:T(8,128)(2,1)S(1)} %collective-permute-done.4.up, bf16[512,384]{1,0:T(8,128)(2,1)S(1)} %collective-permute-done.5.down, ...), custom_call_target="tpu_custom_call" | custom-call | tf_op jit(solution)/shard_map/pallas_call | solution.py:31
  70.5 0.1 collective-permute-start.6
  70.6 5.3 %collective-permute-start.7 = (bf16[2,128,384]{2,1,0:T(8,128)(2,1)S(1)}, bf16[2,128,384]{2,1,0:T(8,128)(2,1)S(1)}, u32[]{:S(2)}, u32[]{:S(2)}) collective-permute-start(bf16[2,128,384]{2,1,0:T(8,128)(2,1)S(1)} %get-tuple-element.21), channel_id=1, source_target_pairs={{1,112},{3,1},{5,3},{7,5},{118,7},{116,118},{114,116},{112,114},{1... | collective-permute-start | bytes 589832 | tf_op jit(solution)/shard_map/ppermute | solution.py:339
  76.0 4.8 %shard_map.100.partial = f32[2,512,384]{2,1,0:T(8,128)S(1)} custom-call(s32[102]{0:T(128)S(1)} %dynamic-slice_bitcast_fusion.notes, bf16[512,384]{1,0:T(8,128)(2,1)S(1)} %collective-permute-done.4.up, bf16[512,384]{1,0:T(8,128)(2,1)S(1)} %collective-permute-done.5.down, bf16[512,384]{1,0:T(8,128)(2,1)S(1)} %get-tuple-element.18.hidden0, ...), custom_call_target="tpu_custom_call" | custom-call | tf_op jit(solution)/shard_map/pallas_call | solution.py:31
  80.8 0.0 collective-permute-done.6.from_left
  80.8 0.0 collective-permute-done.7.from_right
  80.8 1.1 shard_map.102
  81.9 23.8 %all_to_all.11.landed = bf16[64,3,8,384]{3,2,1,0:T(8,128)(2,1)S(1)} all-to-all(bf16[64,3,8,384]{3,2,1,0:T(8,128)(2,1)S(1)} %shard_map.102), channel_id=1, replica_groups=mesh['zh'=2,'y1'=2,'y0'=2,'core'=2,'x1'=2,'x0'=2,'zl'=2] {'zh','y1','y0'..., dimensions={0} | all-to-all | bytes 2359296 | tf_op jit(solution)/shard_map/all_to_all | solution.py:371
  105.6 0.7 shard_map.104
  106.4 0.1 collective-permute-start.8
  106.5 1.0 shard_map.103
  107.5 0.9 copy.17
  108.3 0.0 collective-permute-done.8
  108.3 0.0 copy-done
  108.3 0.4 convolution_convert_fusion
  108.8 0.5 reshape.19
  109.3 0.2 copy.10
  109.5 0.0 copy-start.6
  109.5 0.0 copy-start.7
  109.5 0.1 slice_bitcast_fusion
  109.6 0.1 copy.16
  109.7 0.1 pad.clone
  109.9 0.6 copy-done.6
  110.4 0.0 copy-done.7
  110.4 0.8 fusion
  111.3 0.8 copy.15
  (4 shorter events, 0.1 us)
Async XLA Ops:
  0.6 107.7 %copy-start = (bf16[384,1536]{1,0:T(8,128)(2,1)S(1)}, bf16[384,1536]{1,0:T(8,128)(2,1)}, u32[]{:S(2)}) copy-start(bf16[384,1536]{1,0:T(8,128)(2,1)} %param.13) | copy-start | bytes 3538948
  1.5 1.1 %copy-start.5 = (bf16[16,64,384]{2,1,0:T(8,128)(2,1)S(1)}, bf16[16,64,384]{2,1,0:T(8,128)(2,1)}, u32[]{:S(2)}) copy-start(bf16[16,64,384]{2,1,0:T(8,128)(2,1)} %context.1) | copy-start | bytes 2359300
  2.6 27.8 %copy-start.4 = (bf16[3,3,384,384]{3,2,1,0:T(8,128)(2,1)S(1)}, bf16[3,3,384,384]{3,2,1,0:T(8,128)(2,1)}, u32[]{:S(2)}) copy-start(bf16[3,3,384,384]{3,2,1,0:T(8,128)(2,1)} %param.9) | copy-start | bytes 7962628
  30.4 13.1 %copy-start.1 = (bf16[3,3,384,384]{3,2,1,0:T(8,128)(2,1)S(1)}, bf16[3,3,384,384]{3,2,1,0:T(8,128)(2,1)}, u32[]{:S(2)}) copy-start(bf16[3,3,384,384]{3,2,1,0:T(8,128)(2,1)} %kernel.5) | copy-start | bytes 7962628
  34.5 9.1 %collective-permute-start = (bf16[512,384]{1,0:T(8,128)(2,1)S(1)}, bf16[512,384]{1,0:T(8,128)(2,1)S(1)}, u32[]{:S(2)}, u32[]{:S(2)}) collective-permute-start(bf16[512,384]{1,0:T(8,128)(2,1)S(1)} %get-tuple-element.13.hidden1), channel_id=1, source_target_pairs={{1,17},{3,19},{5,21},{7,23},{118,70},{116,68},{114,66},{112,64},{1... | collective-permute-start | bytes 1179656 | tf_op jit(solution)/shard_map/ppermute | solution.py:329
  34.6 9.0 %collective-permute-start.1 = (bf16[512,384]{1,0:T(8,128)(2,1)S(1)}, bf16[512,384]{1,0:T(8,128)(2,1)S(1)}, u32[]{:S(2)}, u32[]{:S(2)}) collective-permute-start(bf16[512,384]{1,0:T(8,128)(2,1)S(1)} %get-tuple-element.14.hidden0), channel_id=1, source_target_pairs={{1,57},{3,59},{5,61},{7,63},{118,127},{116,125},{114,123},{112,121... | collective-permute-start | bytes 1179656 | tf_op jit(solution)/shard_map/ppermute | solution.py:330
  45.0 10.2 %collective-permute-start.2 = (bf16[2,128,384]{2,1,0:T(8,128)(2,1)S(1)}, bf16[2,128,384]{2,1,0:T(8,128)(2,1)S(1)}, u32[]{:S(2)}, u32[]{:S(2)}) collective-permute-start(bf16[2,128,384]{2,1,0:T(8,128)(2,1)S(1)} %get-tuple-element.15), channel_id=1, source_target_pairs={{1,3},{3,5},{5,7},{7,118},{118,116},{116,114},{114,112},{112,1},{1... | collective-permute-start | bytes 589832 | tf_op jit(solution)/shard_map/ppermute | solution.py:338
  45.5 9.7 %collective-permute-start.3 = (bf16[2,128,384]{2,1,0:T(8,128)(2,1)S(1)}, bf16[2,128,384]{2,1,0:T(8,128)(2,1)S(1)}, u32[]{:S(2)}, u32[]{:S(2)}) collective-permute-start(bf16[2,128,384]{2,1,0:T(8,128)(2,1)S(1)} %get-tuple-element.16), channel_id=1, source_target_pairs={{1,112},{3,1},{5,3},{7,5},{118,7},{116,118},{114,116},{112,114},{1... | collective-permute-start | bytes 589832 | tf_op jit(solution)/shard_map/ppermute | solution.py:339
  50.4 4.8 %copy-start.3 = (bf16[3,3,384,384]{3,2,1,0:T(8,128)(2,1)S(1)}, bf16[3,3,384,384]{3,2,1,0:T(8,128)(2,1)}, u32[]{:S(2)}) copy-start(bf16[3,3,384,384]{3,2,1,0:T(8,128)(2,1)} %param.11) | copy-start | bytes 7962628
  55.2 13.9 %copy-start.2 = (bf16[3,3,384,384]{3,2,1,0:T(8,128)(2,1)S(1)}, bf16[3,3,384,384]{3,2,1,0:T(8,128)(2,1)}, u32[]{:S(2)}) copy-start(bf16[3,3,384,384]{3,2,1,0:T(8,128)(2,1)} %kernel.7) | copy-start | bytes 7962628
  60.0 9.1 %collective-permute-start.4 = (bf16[512,384]{1,0:T(8,128)(2,1)S(1)}, bf16[512,384]{1,0:T(8,128)(2,1)S(1)}, u32[]{:S(2)}, u32[]{:S(2)}) collective-permute-start(bf16[512,384]{1,0:T(8,128)(2,1)S(1)} %get-tuple-element.17.hidden1), channel_id=1, source_target_pairs={{1,17},{3,19},{5,21},{7,23},{118,70},{116,68},{114,66},{112,64},{1... | collective-permute-start | bytes 1179656 | tf_op jit(solution)/shard_map/ppermute | solution.py:329
  60.1 9.0 %collective-permute-start.5 = (bf16[512,384]{1,0:T(8,128)(2,1)S(1)}, bf16[512,384]{1,0:T(8,128)(2,1)S(1)}, u32[]{:S(2)}, u32[]{:S(2)}) collective-permute-start(bf16[512,384]{1,0:T(8,128)(2,1)S(1)} %get-tuple-element.18.hidden0), channel_id=1, source_target_pairs={{1,57},{3,59},{5,61},{7,63},{118,127},{116,125},{114,123},{112,121... | collective-permute-start | bytes 1179656 | tf_op jit(solution)/shard_map/ppermute | solution.py:330
  70.5 10.2 %collective-permute-start.6 = (bf16[2,128,384]{2,1,0:T(8,128)(2,1)S(1)}, bf16[2,128,384]{2,1,0:T(8,128)(2,1)S(1)}, u32[]{:S(2)}, u32[]{:S(2)}) collective-permute-start(bf16[2,128,384]{2,1,0:T(8,128)(2,1)S(1)} %get-tuple-element.20), channel_id=1, source_target_pairs={{1,3},{3,5},{5,7},{7,118},{118,116},{116,114},{114,112},{112,1},{1... | collective-permute-start | bytes 589832 | tf_op jit(solution)/shard_map/ppermute | solution.py:338
  70.6 10.2 %collective-permute-start.7 = (bf16[2,128,384]{2,1,0:T(8,128)(2,1)S(1)}, bf16[2,128,384]{2,1,0:T(8,128)(2,1)S(1)}, u32[]{:S(2)}, u32[]{:S(2)}) collective-permute-start(bf16[2,128,384]{2,1,0:T(8,128)(2,1)S(1)} %get-tuple-element.21), channel_id=1, source_target_pairs={{1,112},{3,1},{5,3},{7,5},{118,7},{116,118},{114,116},{112,114},{1... | collective-permute-start | bytes 589832 | tf_op jit(solution)/shard_map/ppermute | solution.py:339
  106.4 2.0 %collective-permute-start.8 = (bf16[6,24,384]{2,1,0:T(8,128)(2,1)S(1)}, bf16[6,24,384]{2,1,0:T(8,128)(2,1)S(1)}, u32[]{:S(2)}, u32[]{:S(2)}) collective-permute-start(bf16[6,24,384]{2,1,0:T(8,128)(2,1)S(1)} %get-tuple-element.23), channel_id=1, source_target_pairs={{0,8},{8,0},{1,9},{9,1},{2,10},{10,2},{3,11},{11,3},{4,12},{12,4},... | collective-permute-start | bytes 331784 | tf_op jit(solution)/shard_map/ppermute | solution.py:375
  109.5 0.9 copy-start.6
  109.5 0.9 copy-start.7

commit v6 on v5

--- a/solution.py
+++ b/solution.py
@@ -135,9 +135,13 @@
     lax.fori_loop(0, 16, step, 0)
 
 
-def scatter_body(notes, landed, result):
+def scatter_body(notes, landed, result, near, departures):
     channels = result.shape[-1]
     first = lax.broadcasted_iota(jnp.int32, (8, channels), 0) < 4
+
+    def send(part):
+        rows = pl.ds(4 * part, 4)
+        return pltpu.make_async_copy(near.at[rows], result.at[rows], departures.at[part])
 
     def step(row, carry):
         for pair in range(4):
@@ -146,11 +150,27 @@
             odd = landed[notes[place + 1], row % 2].astype(F32)
             low = jnp.where(first, even, pltpu.roll(odd, 4, 0))
             high = jnp.where(first, pltpu.roll(even, 4, 0), odd)
-            result[row, 8 * pair : 8 * pair + 8] = low.astype(BF16)
-            result[row, 32 + 8 * pair : 40 + 8 * pair] = high.astype(BF16)
+            near[row, 8 * pair : 8 * pair + 8] = low.astype(BF16)
+            near[row, 32 + 8 * pair : 40 + 8 * pair] = high.astype(BF16)
         return carry
 
-    lax.fori_loop(0, 16, step, 0)
+    for part in range(4):
+        lax.fori_loop(4 * part, 4 * part + 4, step, 0)
+        send(part).start()
+    for part in range(4):
+        send(part).wait()
+
+
+def scatter(notes, landed):
+    shape = (16, 64, landed.shape[-1])
+    return pl.pallas_call(
+        scatter_body,
+        out_shape=jax.ShapeDtypeStruct(shape, BF16),
+        in_specs=[SMEM, VMEM],
+        out_specs=pl.BlockSpec(memory_space=pltpu.HBM),
+        scratch_shapes=[pltpu.VMEM(shape, BF16), pltpu.SemaphoreType.DMA((4,))],
+        compiler_params=pltpu.CompilerParams(vmem_limit_bytes=24 << 20),
+    )(notes, pltpu.with_memory_space_constraint(landed, pltpu.VMEM))
 
 
 def dilated_band(cells, kernel, hidden, shelves, spacing):
@@ -255,41 +275,53 @@
                 window[line, 8 * tile : 8 * tile + 8] = joined.astype(BF16)
 
 
-def edge_body(notes, up, down, hidden0, hidden1, kernel, to_left, to_right, above, below, wide):
+def shifted_products(products, place):
+    left, centre, right = products
+    total = centre + jnp.where(place == 0, 0.0, pltpu.roll(left, 1, 0))
+    return total + jnp.where(place == 3, 0.0, pltpu.roll(right, 511, 0))
+
+
+def own_body(hidden0, hidden1, state, kernel, partial, own_left, own_right, wide):
+    channels = hidden0.shape[-1]
+    place = lax.broadcasted_iota(jnp.int32, (512, channels), 0) % 4
+    lines = jnp.concatenate([hidden0[...], hidden1[...]], 1)
+    for i0 in range(2):
+        products = [
+            jnp.dot(
+                lines,
+                kernel[1 - i0 : 3 - i0, tap].reshape(2 * channels, channels),
+                preferred_element_type=F32,
+            )
+            for tap in range(3)
+        ]
+        for product, start, sums in ((products[0], 3, own_right), (products[2], 0, own_left)):
+            for lane in range(0, channels, 128):
+                wide[...] = product[:, lane : lane + 128]
+                sums[i0, :, lane : lane + 128] = wide[pl.ds(start, 128, stride=4)]
+        total = shifted_products(products, place)
+        partial[i0] = state[:, i0].reshape(512, channels).astype(F32) + total
+
+
+def edge_body(notes, up, down, own_left, own_right, kernel, to_left, to_right, wide):
     channels = up.shape[-1]
-    blank = jnp.zeros((64, channels), BF16)
-    above[:64] = blank
-    above[64:] = up[...]
-    below[:512] = down[...]
-    below[512:] = blank
-    start = pl.multiple_of(64 - 64 * notes[FIRST_ROW], 64)
-    lines = [above[pl.ds(start, 512)], hidden0[...], hidden1[...]]
-    start = pl.multiple_of(64 * notes[LAST_ROW], 64)
-    lines.append(below[pl.ds(start, 512)])
-    for index, line in enumerate(lines):
+    place = lax.broadcasted_iota(jnp.int32, (128, channels), 0)
+    for i0, line, wrap, far, turn in (
+        (0, up, notes[FIRST_ROW], place < 16, 16),
+        (1, down, notes[LAST_ROW], place >= 112, 112),
+    ):
         for lane in range(0, channels, 128):
-            wide[index, lane // 128] = line[:, lane : lane + 128].astype(F32)
-    for column, tap, sums in ((3, 0, to_right), (0, 2, to_left)):
-        weights = kernel[:, tap].reshape(3 * channels, channels)
-        lines = [
-            jnp.concatenate(
-                [
-                    wide.at[line, lane][pl.ds(column, 128, stride=4)].astype(BF16)
-                    for lane in range(channels // 128)
-                ],
-                1,
+            wide[lane // 128] = line[:, lane : lane + 128].astype(F32)
+        for start, tap, own, sums in ((3, 0, own_right, to_right), (0, 2, own_left, to_left)):
+            cells = jnp.concatenate(
+                [wide.at[lane][pl.ds(start, 128, stride=4)] for lane in range(channels // 128)], 1
             )
-            for line in range(4)
-        ]
-        stack = jnp.concatenate(
-            [jnp.concatenate(lines[:3], 1), jnp.concatenate(lines[1:], 1)], 0
-        )
-        product = jnp.dot(stack, weights, preferred_element_type=F32).astype(BF16)
-        sums[0] = product[:128]
-        sums[1] = product[128:]
-
-
-def plain_body(notes, up, down, hidden0, hidden1, state, kernel, partial, above, below):
+            moved = jnp.where(far, 0.0, pltpu.roll(cells, turn, 0))
+            cells = jnp.where(wrap == 1, moved, cells).astype(BF16)
+            product = jnp.dot(cells, kernel[2 * i0, tap], preferred_element_type=F32)
+            sums[i0] = (own[i0] + product).astype(BF16)
+
+
+def rest_body(notes, up, down, partial, kernel, total, above, below):
     channels = up.shape[-1]
     blank = jnp.zeros((64, channels), BF16)
     above[:64] = blank
@@ -298,49 +330,87 @@
     below[512:] = blank
     over = above[pl.ds(pl.multiple_of(64 - 64 * notes[FIRST_ROW], 64), 512)]
     under = below[pl.ds(pl.multiple_of(64 * notes[LAST_ROW], 64), 512)]
-    lines = (over, hidden0[...], hidden1[...], under)
     place = lax.broadcasted_iota(jnp.int32, (512, channels), 0) % 4
-    for i0 in range(2):
-        stack = jnp.concatenate(lines[i0 : i0 + 3], 1)
+    for i0, line in enumerate((over, under)):
         products = [
-            jnp.dot(stack, kernel[:, tap].reshape(3 * channels, channels), preferred_element_type=F32)
-            for tap in range(3)
+            jnp.dot(line, kernel[2 * i0, tap], preferred_element_type=F32) for tap in range(3)
         ]
-        total = state[:, i0].reshape(512, channels).astype(F32) + products[1]
-        total = total + jnp.where(place == 0, 0.0, pltpu.roll(products[0], 1, 0))
-        total = total + jnp.where(place == 3, 0.0, pltpu.roll(products[2], 511, 0))
-        partial[i0] = total
-
-
-def fine_target(crop, lift_weight, fine_weight):
+        total[i0] = partial[i0] + shifted_products(products, place)
+
+
+def fine_body(own, swapped, lift, fine, target, image, taps, merged):
+    channels, width = own.shape[-1], fine.shape[-1]
+    window = own[...].astype(F32) + swapped[...].astype(F32)
+    window = window.astype(BF16).reshape(144, channels)
+    lifted = jnp.dot(window, lift[...], preferred_element_type=F32)
+    lifted = lifted.astype(BF16).astype(F32).reshape(6, 24, 16 * width)
+    image[...] = jnp.zeros(image.shape, BF16)
+    taps[...] = jnp.zeros(taps.shape, BF16)
+    for a in range(3):
+        for b in range(3):
+            row = 128 * (3 * a + b)
+            taps[row : row + width, :width] = fine[a, b]
+    for phase, v, shift in ((0, 3, 3), (1, 0, 4), (2, 1, 4), (3, 2, 4), (4, 3, 4), (5, 0, 5)):
+        for u in range(4):
+            lane = width * (4 * u + v)
+            block = pltpu.roll(lifted[:, :, lane : lane + width], 24 - shift, 1)
+            block = block[:, :16].astype(BF16)
+            for line in range(6):
+                row = 4 * (line - 1) + u + 1
+                if 0 <= row < 18:
+                    image[row, phase, :, :width] = block[line]
+    for v in range(4):
+        stack = jnp.concatenate(
+            [
+                image[a : a + 16, v + b].reshape(256, 128)
+                for a in range(3)
+                for b in range(3)
+            ],
+            1,
+        )
+        merged[pl.ds(v, 256, stride=4)] = jnp.dot(
+            stack, taps[...], preferred_element_type=F32
+        )
+    target[...] = merged[...].astype(BF16)[:, :width].reshape(target.shape)
+
+
+def fine_target(own, swapped, lift_weight, fine_weight):
     width = fine_weight.shape[-1]
-    lifted = jnp.einsum("rcf,fg->rcg", crop, lift_weight, preferred_element_type=F32).astype(BF16)
-    lifted = lifted.reshape(6, 24, 4, 4, width).transpose(0, 2, 1, 3, 4).reshape(24, 96, width)
-    lifted = lifted[3:21, 15:81]
-    target = lax.conv_general_dilated(
-        lifted[None], fine_weight, (1, 1), ((0, 0), (0, 0)),
-        dimension_numbers=("NHWC", "HWIO", "NHWC"), preferred_element_type=F32,
-    )
-    return target[0].astype(BF16)
+    near = [
+        pltpu.with_memory_space_constraint(x, pltpu.VMEM)
+        for x in (own, swapped, lift_weight, fine_weight)
+    ]
+    return pl.pallas_call(
+        fine_body,
+        out_shape=jax.ShapeDtypeStruct((16, 64, width), BF16),
+        in_specs=[VMEM] * 4,
+        scratch_shapes=[
+            pltpu.VMEM((18, 6, 16, 128), BF16),
+            pltpu.VMEM((9 * 128, 128), BF16),
+            pltpu.VMEM((1024, 128), F32),
+        ],
+        compiler_params=pltpu.CompilerParams(vmem_limit_bytes=24 << 20),
+    )(*near)
 
 
 def plain(hidden0, hidden1, state, kernel, own):
     channels = hidden0.shape[-1]
     up = lax.ppermute(hidden1, AXES, block_route(1, 0))
     down = lax.ppermute(hidden0, AXES, block_route(-1, 0))
-    padded = [((576, channels), BF16)] * 2
+    edge = (2, 128, channels)
+    body = (2, 512, channels)
+    partial, own_left, own_right = kernel_call(
+        own_body, [(body, F32), (edge, F32), (edge, F32)], [((512, 128), F32)], 4
+    )(hidden0, hidden1, state, kernel)
     to_left, to_right = kernel_call(
-        edge_body,
-        [((2, 128, channels), BF16)] * 2,
-        padded + [((4, 3, 512, 128), F32)],
-        5, 1,
-    )(own, up, down, hidden0, hidden1, kernel)
+        edge_body, [(edge, BF16)] * 2, [((3, 512, 128), F32)], 5, 1
+    )(own, up, down, own_left, own_right, kernel)
     from_left = lax.ppermute(to_right, AXES, block_route(0, 1))
     from_right = lax.ppermute(to_left, AXES, block_route(0, -1))
-    (partial,) = kernel_call(plain_body, [((2, 512, channels), F32)], padded, 6, 1)(
-        own, up, down, hidden0, hidden1, state, kernel
-    )
-    return partial, from_left, from_right
+    (total,) = kernel_call(rest_body, [(body, F32)], [((576, channels), BF16)] * 2, 4, 1)(
+        own, up, down, partial, kernel
+    )
+    return total, from_left, from_right
 
 
 def shards(context, first_dilated_weight, first_plain_weight, second_dilated_weight,
@@ -373,8 +443,8 @@
         own, landed
     )
     swapped = lax.ppermute(other, "core", [(0, 1), (1, 0)])
-    (result,) = kernel_call(scatter_body, [((16, 64, channels), BF16)], (), 1, 1)(own, landed)
-    target = fine_target(window + swapped, lift_weight, fine_weight)
+    result = scatter(own, landed)
+    target = fine_target(window, swapped, lift_weight, fine_weight)
     return result, target
 
 

time: 114 us -> 110 us (0.965)
  waiting for transfers between devices: 11.5 us -> 8.04 us
  local copies, waits for them, and re-layouts: 5.27 us -> 1.85 us
  Pallas kernels: 25 us -> 27.9 us
  blocking collectives: 50.7 us -> 52.4 us
  matrix products: 1.15 us -> 0 us
    ppermute x2, waiting for transfers between devices: 11.5 us -> 5.47 us  [plain(): up = lax.ppermute(hidden1, AXES, block_route(1, 0))]
    pallas_call x0 -> x2, Pallas kernels: none -> 3.66 us  [the longest x1 1.97 us: fine_target(): pl.pallas_call(fine_body, out_shape=jax.ShapeDtypeStruct((16, 64, width),...]
    ppermute x2, waiting for transfers between devices: 0.01 us -> 2.55 us  [plain(): from_left = lax.ppermute(to_right, AXES, block_route(0, 1))]
    unnamed x19 -> x14, local copies, waits for them, and re-layouts: 3.45 us -> 1.15 us
    all_to_all x1, blocking collectives: 23.8 us -> 25.5 us  [shards(): landed = lax.all_to_all(outgoing, SPREAD, 0, 0, tiled=True)]
    pallas_call x10 -> x11, Pallas kernels: 25 us -> 24.2 us  [run(): return call(*operands[:scalars], *near)]
  transfers between devices with their start and end apart: 9 -> 9, of which waited for: 2 -> 4; matrix products, arithmetic and copies ran while one was open for 1% -> 0% of each run, Pallas kernels for 9% -> 11%
where the time goes in v6:
time: 110 us; the launch traced here: 108 us
  blocking collectives  52.4 us (48%)
  Pallas kernels  27.9 us (25%)
  starting transfers between devices  17.5 us (16%)
  waiting for transfers between devices  8.04 us (7%)
  local copies, waits for them, and re-layouts  1.85 us (2%)
    all_to_all x1, blocking collectives, shards(): state = lax.all_to_all(sent, SPREAD, 0, 0, tiled=True)  26.9 us
    all_to_all x1, blocking collectives, shards(): landed = lax.all_to_all(outgoing, SPREAD, 0, 0, tiled=True)  25.5 us
    pallas_call x11, Pallas kernels, run(): return call(*operands[:scalars], *near)  24.2 us
    ppermute x2, starting transfers between devices, plain(): from_right = lax.ppermute(to_left, AXES, block_route(0, -1))  10.2 us
    ppermute x2, starting transfers between devices, plain(): down = lax.ppermute(hidden0, AXES, block_route(-1, 0))  6.45 us
    ppermute x2, waiting for transfers between devices, plain(): up = lax.ppermute(hidden1, AXES, block_route(1, 0))  5.47 us
    ppermute x2, waiting for transfers between devices, plain(): from_left = lax.ppermute(to_right, AXES, block_route(0, 1))  2.55 us
  transfers between devices with their start and end apart: 9, of which 4 were waited for; matrix products, arithmetic and copies ran while one was open for 0% of the time, Pallas kernels for 11%

profile of v6, /device:TPU:0, one launch (start us, length us, event | category | flops | bytes accessed | tf_op | source)
XLA Modules:
  0.0 108.5 jit_solution(722145308244373326)
XLA Ops:
  0.6 0.7 dynamic-slice_bitcast_fusion.notes
  1.3 0.0 copy-start.5
  1.3 1.1 %copy-done.5 = bf16[16,64,384]{2,1,0:T(8,128)(2,1)S(1)} copy-done((bf16[16,64,384]{2,1,0:T(8,128)(2,1)S(1)}, bf16[16,64,384]{2,1,0:T(8,128)(2,1)}, u32[]{:S(2)}) %copy-start.5) | copy-done | bytes 786456
  2.5 0.0 copy-start.3
  2.5 0.9 shard_map.95
  3.4 26.9 %all_to_all.10.landed.state = bf16[64,2,8,384]{3,2,1,0:T(8,128)(2,1)S(1)} all-to-all(bf16[64,2,8,384]{3,2,1,0:T(8,128)(2,1)S(1)} %shard_map.95), channel_id=1, replica_groups=mesh['zh'=2,'y1'=2,'y0'=2,'core'=2,'x1'=2,'x0'=2,'zl'=2] {'zh','y1','y0'..., dimensions={0} | all-to-all | bytes 1572864 | tf_op jit(solution)/shard_map/all_to_all | solution.py:423
  30.3 0.0 copy-done.3
  30.3 0.0 copy-start
  30.3 4.0 %shard_map.96 = (bf16[512,384]{1,0:T(8,128)(2,1)S(1)}, bf16[512,384]{1,0:T(8,128)(2,1)S(1)}) custom-call(bf16[64,2,8,384]{3,2,1,0:T(8,128)(2,1)S(1)} %all_to_all.10.landed.state, bf16[3456,384]{1,0:T(8,128)(2,1)S(1)} %bitcast.5), custom_call_target="tpu_custom_call" | custom-call | tf_op jit(solution)/shard_map/pallas_call | solution.py:31
  34.4 0.1 collective-permute-start
  34.5 3.2 %collective-permute-start.1 = (bf16[512,384]{1,0:T(8,128)(2,1)S(1)}, bf16[512,384]{1,0:T(8,128)(2,1)S(1)}, u32[]{:S(2)}, u32[]{:S(2)}) collective-permute-start(bf16[512,384]{1,0:T(8,128)(2,1)S(1)} %get-tuple-element.20.hidden0), channel_id=1, source_target_pairs={{1,57},{3,59},{5,61},{7,63},{118,127},{116,125},{114,123},{112,121... | collective-permute-start | bytes 1179656 | tf_op jit(solution)/shard_map/ppermute | solution.py:399
  37.7 0.0 copy-done
  37.7 3.0 %shard_map.97 = (f32[2,512,384]{2,1,0:T(8,128)S(1)}, f32[2,128,384]{2,1,0:T(8,128)S(1)}, f32[2,128,384]{2,1,0:T(8,128)S(1)}) custom-call(bf16[512,384]{1,0:T(8,128)(2,1)S(1)} %get-tuple-element.20.hidden0, bf16[512,384]{1,0:T(8,128)(2,1)S(1)} %get-tuple-element.19.hidden1, bf16[64,2,8,384]{3,2,1,0:T(8,128)(2,1)S(1)} %all_to_all.10.landed.state, ...), custom_call_target="tpu_custom_call" | custom-call | tf_op jit(solution)/shard_map/pallas_call | solution.py:31
  40.7 2.7 %collective-permute-done.up = bf16[512,384]{1,0:T(8,128)(2,1)S(1)} collective-permute-done((bf16[512,384]{1,0:T(8,128)(2,1)S(1)}, bf16[512,384]{1,0:T(8,128)(2,1)S(1)}, u32[]{:S(2)}, u32[]{:S(2)}) %collective-permute-start) | collective-permute-done | bytes 393248 | tf_op jit(solution)/shard_map/ppermute | solution.py:398
  43.4 0.0 collective-permute-done.1.down
  43.4 1.0 shard_map.99
  44.4 0.6 collective-permute-start.2
  45.0 4.9 %collective-permute-start.3 = (bf16[2,128,384]{2,1,0:T(8,128)(2,1)S(1)}, bf16[2,128,384]{2,1,0:T(8,128)(2,1)S(1)}, u32[]{:S(2)}, u32[]{:S(2)}) collective-permute-start(bf16[2,128,384]{2,1,0:T(8,128)(2,1)S(1)} %get-tuple-element.25), channel_id=1, source_target_pairs={{1,112},{3,1},{5,3},{7,5},{118,7},{116,118},{114,116},{112,114},{1... | collective-permute-start | bytes 589832 | tf_op jit(solution)/shard_map/ppermute | solution.py:409
  49.8 0.0 copy-start.2
  49.8 2.4 %shard_map.98.partial = f32[2,512,384]{2,1,0:T(8,128)S(1)} custom-call(s32[102]{0:T(128)S(1)} %dynamic-slice_bitcast_fusion.notes, bf16[512,384]{1,0:T(8,128)(2,1)S(1)} %collective-permute-done.up, bf16[512,384]{1,0:T(8,128)(2,1)S(1)} %collective-permute-done.1.down, f32[2,512,384]{2,1,0:T(8,128)S(1)} %get-tuple-element.21.partial, ...), custom_call_target="tpu_custom_call" | custom-call | tf_op jit(solution)/shard_map/pallas_call | solution.py:31
  52.2 1.3 %collective-permute-done.2.from_left = bf16[2,128,384]{2,1,0:T(8,128)(2,1)S(1)} collective-permute-done((bf16[2,128,384]{2,1,0:T(8,128)(2,1)S(1)}, bf16[2,128,384]{2,1,0:T(8,128)(2,1)S(1)}, u32[]{:S(2)}, u32[]{:S(2)}) %collective-permute-start.2) | collective-permute-done | bytes 196640 | tf_op jit(solution)/shard_map/ppermute | solution.py:408
  53.5 0.0 collective-permute-done.3.from_right
  53.5 0.0 copy-done.2
  53.5 0.0 copy-start.1
  53.5 4.8 %shard_map.100 = (bf16[64,2,8,384]{3,2,1,0:T(8,128)(2,1)S(1)}, bf16[512,384]{1,0:T(8,128)(2,1)S(1)}, bf16[512,384]{1,0:T(8,128)(2,1)S(1)}) custom-call(s32[102]{0:T(128)S(1)} %dynamic-slice_bitcast_fusion.notes, f32[2,512,384]{2,1,0:T(8,128)S(1)} %shard_map.98.partial, bf16[2,128,384]{2,1,0:T(8,128)(2,1)S(1)} %collective-permute-done.2.from_left, ...), custom_call_target="tpu_custom_call" | custom-call | tf_op jit(solution)/shard_map/pallas_call | solution.py:31
  58.3 0.1 collective-permute-start.4
  58.4 3.2 %collective-permute-start.5 = (bf16[512,384]{1,0:T(8,128)(2,1)S(1)}, bf16[512,384]{1,0:T(8,128)(2,1)S(1)}, u32[]{:S(2)}, u32[]{:S(2)}) collective-permute-start(bf16[512,384]{1,0:T(8,128)(2,1)S(1)} %get-tuple-element.27.hidden0), channel_id=1, source_target_pairs={{1,57},{3,59},{5,61},{7,63},{118,127},{116,125},{114,123},{112,121... | collective-permute-start | bytes 1179656 | tf_op jit(solution)/shard_map/ppermute | solution.py:399
  61.6 0.0 copy-done.1
  61.6 3.0 %shard_map.101 = (f32[2,512,384]{2,1,0:T(8,128)S(1)}, f32[2,128,384]{2,1,0:T(8,128)S(1)}, f32[2,128,384]{2,1,0:T(8,128)S(1)}) custom-call(bf16[512,384]{1,0:T(8,128)(2,1)S(1)} %get-tuple-element.27.hidden0, bf16[512,384]{1,0:T(8,128)(2,1)S(1)} %get-tuple-element.26.hidden1, bf16[64,2,8,384]{3,2,1,0:T(8,128)(2,1)S(1)} %get-tuple-element.28.state, ...), custom_call_target="tpu_custom_call" | custom-call | tf_op jit(solution)/shard_map/pallas_call | solution.py:31
  64.6 2.7 %collective-permute-done.4.up = bf16[512,384]{1,0:T(8,128)(2,1)S(1)} collective-permute-done((bf16[512,384]{1,0:T(8,128)(2,1)S(1)}, bf16[512,384]{1,0:T(8,128)(2,1)S(1)}, u32[]{:S(2)}, u32[]{:S(2)}) %collective-permute-start.4) | collective-permute-done | bytes 393248 | tf_op jit(solution)/shard_map/ppermute | solution.py:398
  67.3 0.0 collective-permute-done.5.down
  67.3 1.0 shard_map.103
  68.3 0.1 collective-permute-start.6
  68.4 5.3 %collective-permute-start.7 = (bf16[2,128,384]{2,1,0:T(8,128)(2,1)S(1)}, bf16[2,128,384]{2,1,0:T(8,128)(2,1)S(1)}, u32[]{:S(2)}, u32[]{:S(2)}) collective-permute-start(bf16[2,128,384]{2,1,0:T(8,128)(2,1)S(1)} %get-tuple-element.33), channel_id=1, source_target_pairs={{1,112},{3,1},{5,3},{7,5},{118,7},{116,118},{114,116},{112,114},{1... | collective-permute-start | bytes 589832 | tf_op jit(solution)/shard_map/ppermute | solution.py:409
  73.7 2.4 %shard_map.102.partial = f32[2,512,384]{2,1,0:T(8,128)S(1)} custom-call(s32[102]{0:T(128)S(1)} %dynamic-slice_bitcast_fusion.notes, bf16[512,384]{1,0:T(8,128)(2,1)S(1)} %collective-permute-done.4.up, bf16[512,384]{1,0:T(8,128)(2,1)S(1)} %collective-permute-done.5.down, f32[2,512,384]{2,1,0:T(8,128)S(1)} %get-tuple-element.29.partial, ...), custom_call_target="tpu_custom_call" | custom-call | tf_op jit(solution)/shard_map/pallas_call | solution.py:31
  76.1 1.3 %collective-permute-done.6.from_left = bf16[2,128,384]{2,1,0:T(8,128)(2,1)S(1)} collective-permute-done((bf16[2,128,384]{2,1,0:T(8,128)(2,1)S(1)}, bf16[2,128,384]{2,1,0:T(8,128)(2,1)S(1)}, u32[]{:S(2)}, u32[]{:S(2)}) %collective-permute-start.6) | collective-permute-done | bytes 196640 | tf_op jit(solution)/shard_map/ppermute | solution.py:408
  77.4 0.0 collective-permute-done.7.from_right
  77.4 1.1 %shard_map.104 = bf16[64,3,8,384]{3,2,1,0:T(8,128)(2,1)S(1)} custom-call(s32[102]{0:T(128)S(1)} %dynamic-slice_bitcast_fusion.notes, f32[2,512,384]{2,1,0:T(8,128)S(1)} %shard_map.102.partial, bf16[2,128,384]{2,1,0:T(8,128)(2,1)S(1)} %collective-permute-done.6.from_left, bf16[2,128,384]{2,1,0:T(8,128)(2,1)S(1)} %collective-permute-done.7.from_right), custom_call_target="tpu_custom_call" | custom-call | tf_op jit(solution)/shard_map/pallas_call | solution.py:31
  78.5 25.5 %all_to_all.11.landed = bf16[64,3,8,384]{3,2,1,0:T(8,128)(2,1)S(1)} all-to-all(bf16[64,3,8,384]{3,2,1,0:T(8,128)(2,1)S(1)} %shard_map.104), channel_id=1, replica_groups=mesh['zh'=2,'y1'=2,'y0'=2,'core'=2,'x1'=2,'x0'=2,'zl'=2] {'zh','y1','y0'..., dimensions={0} | all-to-all | bytes 2359296 | tf_op jit(solution)/shard_map/all_to_all | solution.py:441
  104.0 0.0 copy-start.4
  104.0 0.0 copy-start.6
  104.0 0.7 shard_map.106
  104.7 0.1 collective-permute-start.8
  104.8 1.7 %shard_map.105 = bf16[16,64,384]{2,1,0:T(8,128)(2,1)} custom-call(s32[102]{0:T(128)S(1)} %dynamic-slice_bitcast_fusion.notes, bf16[64,3,8,384]{3,2,1,0:T(8,128)(2,1)S(1)} %all_to_all.11.landed), custom_call_target="tpu_custom_call" | custom-call | tf_op jit(solution)/shard_map/pallas_call | solution.py:166
  106.5 0.0 collective-permute-done.8.swapped
  106.5 0.0 copy-done.4
  106.5 0.0 copy-done.6
  106.5 2.0 %shard_map.107 = bf16[16,64,96]{2,1,0:T(8,128)(2,1)} custom-call(bf16[6,24,384]{2,1,0:T(8,128)(2,1)S(1)} %get-tuple-element.34.own, bf16[6,24,384]{2,1,0:T(8,128)(2,1)S(1)} %collective-permute-done.8.swapped, bf16[384,1536]{1,0:T(8,128)(2,1)S(1)} %copy-done.4, bf16[3,3,96,96]{3,2,1,0:T(8,128)(2,1)S(1)} %copy-done.6), custom_call_target="tpu_custom_call" | custom-call | tf_op jit(solution)/shard_map/pallas_call | solution.py:383
Async XLA Ops:
  1.3 1.1 %copy-start.5 = (bf16[16,64,384]{2,1,0:T(8,128)(2,1)S(1)}, bf16[16,64,384]{2,1,0:T(8,128)(2,1)}, u32[]{:S(2)}) copy-start(bf16[16,64,384]{2,1,0:T(8,128)(2,1)} %context.1) | copy-start | bytes 2359300
  2.5 27.8 %copy-start.3 = (bf16[3,3,384,384]{3,2,1,0:T(8,128)(2,1)S(1)}, bf16[3,3,384,384]{3,2,1,0:T(8,128)(2,1)}, u32[]{:S(2)}) copy-start(bf16[3,3,384,384]{3,2,1,0:T(8,128)(2,1)} %param.9) | copy-start | bytes 7962628
  30.3 7.4 %copy-start = (bf16[3,3,384,384]{3,2,1,0:T(8,128)(2,1)S(1)}, bf16[3,3,384,384]{3,2,1,0:T(8,128)(2,1)}, u32[]{:S(2)}) copy-start(bf16[3,3,384,384]{3,2,1,0:T(8,128)(2,1)} %kernel.8) | copy-start | bytes 7962628
  34.4 9.1 %collective-permute-start = (bf16[512,384]{1,0:T(8,128)(2,1)S(1)}, bf16[512,384]{1,0:T(8,128)(2,1)S(1)}, u32[]{:S(2)}, u32[]{:S(2)}) collective-permute-start(bf16[512,384]{1,0:T(8,128)(2,1)S(1)} %get-tuple-element.19.hidden1), channel_id=1, source_target_pairs={{1,17},{3,19},{5,21},{7,23},{118,70},{116,68},{114,66},{112,64},{1... | collective-permute-start | bytes 1179656 | tf_op jit(solution)/shard_map/ppermute | solution.py:398
  34.5 9.0 %collective-permute-start.1 = (bf16[512,384]{1,0:T(8,128)(2,1)S(1)}, bf16[512,384]{1,0:T(8,128)(2,1)S(1)}, u32[]{:S(2)}, u32[]{:S(2)}) collective-permute-start(bf16[512,384]{1,0:T(8,128)(2,1)S(1)} %get-tuple-element.20.hidden0), channel_id=1, source_target_pairs={{1,57},{3,59},{5,61},{7,63},{118,127},{116,125},{114,123},{112,121... | collective-permute-start | bytes 1179656 | tf_op jit(solution)/shard_map/ppermute | solution.py:399
  44.4 9.1 %collective-permute-start.2 = (bf16[2,128,384]{2,1,0:T(8,128)(2,1)S(1)}, bf16[2,128,384]{2,1,0:T(8,128)(2,1)S(1)}, u32[]{:S(2)}, u32[]{:S(2)}) collective-permute-start(bf16[2,128,384]{2,1,0:T(8,128)(2,1)S(1)} %get-tuple-element.24), channel_id=1, source_target_pairs={{1,3},{3,5},{5,7},{7,118},{118,116},{116,114},{114,112},{112,1},{1... | collective-permute-start | bytes 589832 | tf_op jit(solution)/shard_map/ppermute | solution.py:408
  45.0 8.5 %collective-permute-start.3 = (bf16[2,128,384]{2,1,0:T(8,128)(2,1)S(1)}, bf16[2,128,384]{2,1,0:T(8,128)(2,1)S(1)}, u32[]{:S(2)}, u32[]{:S(2)}) collective-permute-start(bf16[2,128,384]{2,1,0:T(8,128)(2,1)S(1)} %get-tuple-element.25), channel_id=1, source_target_pairs={{1,112},{3,1},{5,3},{7,5},{118,7},{116,118},{114,116},{112,114},{1... | collective-permute-start | bytes 589832 | tf_op jit(solution)/shard_map/ppermute | solution.py:409
  49.8 3.6 %copy-start.2 = (bf16[3,3,384,384]{3,2,1,0:T(8,128)(2,1)S(1)}, bf16[3,3,384,384]{3,2,1,0:T(8,128)(2,1)}, u32[]{:S(2)}) copy-start(bf16[3,3,384,384]{3,2,1,0:T(8,128)(2,1)} %param.11) | copy-start | bytes 7962628
  53.5 8.1 %copy-start.1 = (bf16[3,3,384,384]{3,2,1,0:T(8,128)(2,1)S(1)}, bf16[3,3,384,384]{3,2,1,0:T(8,128)(2,1)}, u32[]{:S(2)}) copy-start(bf16[3,3,384,384]{3,2,1,0:T(8,128)(2,1)} %kernel.11) | copy-start | bytes 7962628
  58.3 9.1 %collective-permute-start.4 = (bf16[512,384]{1,0:T(8,128)(2,1)S(1)}, bf16[512,384]{1,0:T(8,128)(2,1)S(1)}, u32[]{:S(2)}, u32[]{:S(2)}) collective-permute-start(bf16[512,384]{1,0:T(8,128)(2,1)S(1)} %get-tuple-element.26.hidden1), channel_id=1, source_target_pairs={{1,17},{3,19},{5,21},{7,23},{118,70},{116,68},{114,66},{112,64},{1... | collective-permute-start | bytes 1179656 | tf_op jit(solution)/shard_map/ppermute | solution.py:398
  58.4 9.0 %collective-permute-start.5 = (bf16[512,384]{1,0:T(8,128)(2,1)S(1)}, bf16[512,384]{1,0:T(8,128)(2,1)S(1)}, u32[]{:S(2)}, u32[]{:S(2)}) collective-permute-start(bf16[512,384]{1,0:T(8,128)(2,1)S(1)} %get-tuple-element.27.hidden0), channel_id=1, source_target_pairs={{1,57},{3,59},{5,61},{7,63},{118,127},{116,125},{114,123},{112,121... | collective-permute-start | bytes 1179656 | tf_op jit(solution)/shard_map/ppermute | solution.py:399
  68.3 9.1 %collective-permute-start.6 = (bf16[2,128,384]{2,1,0:T(8,128)(2,1)S(1)}, bf16[2,128,384]{2,1,0:T(8,128)(2,1)S(1)}, u32[]{:S(2)}, u32[]{:S(2)}) collective-permute-start(bf16[2,128,384]{2,1,0:T(8,128)(2,1)S(1)} %get-tuple-element.32), channel_id=1, source_target_pairs={{1,3},{3,5},{5,7},{7,118},{118,116},{116,114},{114,112},{112,1},{1... | collective-permute-start | bytes 589832 | tf_op jit(solution)/shard_map/ppermute | solution.py:408
  68.4 9.0 %collective-permute-start.7 = (bf16[2,128,384]{2,1,0:T(8,128)(2,1)S(1)}, bf16[2,128,384]{2,1,0:T(8,128)(2,1)S(1)}, u32[]{:S(2)}, u32[]{:S(2)}) collective-permute-start(bf16[2,128,384]{2,1,0:T(8,128)(2,1)S(1)} %get-tuple-element.33), channel_id=1, source_target_pairs={{1,112},{3,1},{5,3},{7,5},{118,7},{116,118},{114,116},{112,114},{1... | collective-permute-start | bytes 589832 | tf_op jit(solution)/shard_map/ppermute | solution.py:409
  104.0 2.5 %copy-start.4 = (bf16[384,1536]{1,0:T(8,128)(2,1)S(1)}, bf16[384,1536]{1,0:T(8,128)(2,1)}, u32[]{:S(2)}) copy-start(bf16[384,1536]{1,0:T(8,128)(2,1)} %lift.1) | copy-start | bytes 3538948
  104.0 2.5 %copy-start.6 = (bf16[3,3,96,96]{3,2,1,0:T(8,128)(2,1)S(1)}, bf16[3,3,96,96]{3,2,1,0:T(8,128)(2,1)}, u32[]{:S(2)}) copy-start(bf16[3,3,96,96]{3,2,1,0:T(8,128)(2,1)} %fine.1) | copy-start | bytes 497668
  104.7 1.8 %collective-permute-start.8 = (bf16[6,24,384]{2,1,0:T(8,128)(2,1)S(1)}, bf16[6,24,384]{2,1,0:T(8,128)(2,1)S(1)}, u32[]{:S(2)}, u32[]{:S(2)}) collective-permute-start(bf16[6,24,384]{2,1,0:T(8,128)(2,1)S(1)} %get-tuple-element.35), channel_id=1, source_target_pairs={{0,8},{8,0},{1,9},{9,1},{2,10},{10,2},{3,11},{11,3},{4,12},{12,4},... | collective-permute-start | bytes 331784 | tf_op jit(solution)/shard_map/ppermute | solution.py:445
